TPU v7x, 256 devices: a whole 4x4x8 slice. The times are simulated.
256 devices in a mesh: dp: 4 (over x_lo, core), seq: 64 (over x_hi, z, y).
Axes of the slice: x: 4 (x_hi: 2, x_lo: 2; x = x_hi * 2 + x_lo), y: 4, z: 8, core: 2. Of those that a mesh axis runs over, the one named last changes fastest.
Arguments:
- hidden: bfloat16 [4, 8192, 2048], P('dp', 'seq'), may hold values from -16 to 16
- tokens: int32 [4, 8192], P('dp', 'seq'), may hold values from 0 to 4
- embedding: float32 [5, 2048], replicated, may hold values from -6 to 6
- weight: bfloat16 [2048, 1024], P('dp'), may hold values from -0.125 to 0.125
- kernel: float32 [7, 1024], replicated, may hold values from -2.4 to 2.4
- cotangent: bfloat16 [4, 8192, 1024], P('dp', 'seq'), may hold values from -6 to 6
Outputs:
- block_result: bfloat16 [4, 8192, 1024], P('dp', 'seq')
- grad_hidden: bfloat16 [4, 8192, 2048], P('dp', 'seq')
- grad_weight: float32 [2048, 1024], P('dp')
- grad_kernel: float32 [7, 1024], replicated
- grad_embedding: float32 [5, 2048], replicated
All inputs are finite; a program needn't handle non-finite values.
Results may differ from a plain program's by a relative error of at most 0.0095.
Values may be sent and summed in bfloat16 or wider, within the bound.
No kernel may reach another device: no remote copies, remote signals or barrier semaphores. Data moves between devices by JAX's collectives and lax.ppermute only.
A program may use at most 64 MiB of HBM per device.

v0:
```python
import math

import jax
import jax.numpy as jnp
from jax import lax
from jax.sharding import PartitionSpec as P


def padded_2(cells, sides, width):
    for axis, dim in sides:
        count = lax.axis_size(axis)
        ends = count - 1
        head = lax.slice_in_dim(cells, 0, width, axis=dim)
        tail = lax.slice_in_dim(cells, cells.shape[dim] - width, cells.shape[dim], axis=dim)
        cells = jnp.concatenate(
            [
                lax.ppermute(tail, axis, [(i, (i + 1) % count) for i in range(ends)]),
                cells,
                lax.ppermute(head, axis, [((i + 1) % count, i) for i in range(ends)]),
            ],
            axis=dim,
        )
    return cells


def mirror_rows(conv_block):
    device_list = lax.axis_size("seq")
    row_count = conv_block.shape[0]
    column_names = conv_block.shape[1]
    window_slab_rows = row_count // device_list
    slab_split = conv_block.reshape(device_list, 1, window_slab_rows, column_names)
    spread_out = lax.all_to_all(slab_split, "seq", split_axis=0, concat_axis=1, tiled=True)
    turned = spread_out[0, ::-1].reshape(device_list, 1, window_slab_rows, column_names)
    second = lax.all_to_all(turned, "seq", split_axis=0, concat_axis=1, tiled=True)
    return second.reshape(row_count, column_names)[::-1]


def local(hidden, tokens, embedding, weight, kernel, cotangent):
    window = hidden[0]
    token_codes = tokens[0]
    upstream = cotangent[0]
    row_count = window.shape[0]
    features = window.shape[1]
    tap_count = kernel.shape[0]
    margin = (tap_count - 1) // 2
    positions = hidden.shape[0] * row_count * lax.axis_size("dp") * lax.axis_size("seq")
    factor = 1.0 / math.sqrt(positions)
    one_hot = (
        jnp.arange(embedding.shape[0], dtype=jnp.int32)[:, None] == token_codes[None, :]
    ).astype(jnp.float32)
    looked = lax.dot_general(
        one_hot,
        embedding,
        (((0,), (0,)), ((), ())),
        precision=lax.Precision.HIGHEST,
        preferred_element_type=jnp.float32,
    )
    stream = (window.astype(jnp.float32) + looked).astype(jnp.bfloat16)
    mirrored = mirror_rows(jnp.concatenate([stream, upstream], axis=1))
    stream_rev = mirrored[:, :features][:, ::-1]
    upstream_rev = mirrored[:, features:][:, ::-1]
    kernels = jnp.stack([kernel, kernel])
    stacked = jnp.concatenate([stream, stream_rev], axis=0)
    column_names = stacked
    projected = jnp.dot(
        column_names,
        lax.all_gather(weight, "dp", axis=0, tiled=True),
        preferred_element_type=jnp.float32,
    )
    forward_part = projected[:row_count]
    reverse_part = projected[row_count:]
    values = jnp.stack([forward_part, reverse_part]).astype(jnp.bfloat16)
    padded = padded_2(values, (("seq", 1),), margin)
    widened = padded.astype(jnp.float32)
    mixing = kernels[:, 0][:, None, :] * widened[:, 0:row_count]
    for tap_index in range(1, tap_count):
        mixing = (
            mixing
            + kernels[:, tap_index][:, None, :] * widened[:, tap_index : tap_index + row_count]
        )
    linear = values.astype(jnp.float32)
    logistic = jax.nn.sigmoid(linear)
    gating = linear * logistic
    strands = mixing * gating
    reverse_out = strands[1].astype(jnp.bfloat16)
    returned = mirror_rows(reverse_out)[:, ::-1]
    block_result = (strands[0] + returned.astype(jnp.float32)).astype(jnp.bfloat16)
    upstreams = jnp.stack([upstream, upstream_rev]).astype(jnp.float32)
    grad_mix = upstreams * gating
    accumulated = upstreams * mixing * logistic * (1.0 + linear * (1.0 - logistic))
    grad_padded = padded_2(grad_mix, (("seq", 1),), margin)
    for tap_index in range(tap_count):
        lower = 2 * margin - tap_index
        accumulated = (
            accumulated
            + kernels[:, tap_index][:, None, :] * grad_padded[:, lower : lower + row_count]
        )
    grad_values = accumulated.astype(jnp.bfloat16)
    kernel_terms = jnp.stack(
        [
            jnp.sum(grad_mix * widened[:, tap_index : tap_index + row_count], axis=1)
            for tap_index in range(tap_count)
        ],
        axis=1,
    )
    kernel_part = kernel_terms[0] + kernel_terms[1]
    grad_reverse = grad_values[1]
    grad_stack = jnp.concatenate([grad_values[0], grad_reverse], axis=0)
    column_names = stacked
    owner_rows = lax.psum_scatter(
        lax.dot_general(
            column_names, grad_stack, (((0,), (0,)), ((), ())), preferred_element_type=jnp.float32
        ).astype(jnp.bfloat16),
        "dp",
        scatter_dimension=0,
        tiled=True,
    ).astype(jnp.float32)
    grad_weight = lax.psum(owner_rows, "seq") * factor
    back_stack = lax.dot_general(
        grad_stack,
        lax.all_gather(weight, "dp", axis=0, tiled=True),
        (((1,), (1,)), ((), ())),
        preferred_element_type=jnp.float32,
    )
    reverse_back = back_stack[row_count:].astype(jnp.bfloat16)
    reverse_back = mirror_rows(reverse_back)[:, ::-1]
    grad_stream = back_stack[:row_count] + reverse_back.astype(jnp.float32)
    table_part = jnp.dot(
        one_hot, grad_stream, precision=lax.Precision.HIGHEST, preferred_element_type=jnp.float32
    )
    kernel_sum, table_sum = lax.psum((kernel_part, table_part), ("dp", "seq"))
    return (
        block_result[None],
        grad_stream.astype(jnp.bfloat16)[None],
        grad_weight,
        kernel_sum * factor,
        table_sum * factor,
    )


def solution(mesh):
    in_specs = (P("dp", "seq", None), P("dp", "seq"), P(), P("dp", None), P(), P("dp", "seq", None))
    out_specs = (P("dp", "seq", None), P("dp", "seq", None), P("dp", None), P(), P())
    return jax.shard_map(local, mesh=mesh, in_specs=in_specs, out_specs=out_specs, check_vma=False)
```

profile of v0, /device:TPU:2, one launch (start us, length us, event | category | flops | bytes accessed | tf_op | source)
XLA Modules:
  0.0 851.3 jit_solution(7686276310235606197)
XLA Ops:
  9.0 1.7 fusion
  11.7 38.0 %all_to_all.63 = bf16[64,1,2,3072]{3,2,1,0:T(2,128)(2,1)S(1)} all-to-all(bf16[64,1,2,3072]{3,2,1,0:T(2,128)(2,1)S(1)} %pad_maximum_fusion.3), channel_id=1, replica_groups=mesh['dp'=4,'seq'=64] {'seq'}, dimensions={0} | all-to-all | bytes 1572864 | tf_op jit(solution)/shard_map/all_to_all | solution.py:32
  51.2 6.2 all-to-all-start.1
  57.4 23.5 %all-to-all-done.1 = bf16[64,1,2,3072]{3,2,1,0:T(2,128)(2,1)S(1)} async-done(((bf16[64,1,2,3072]{3,2,1,0:T(2,128)(2,1)}), bf16[64,1,2,3072]{3,2,1,0:T(2,128)(2,1)S(1)}, u32[]{:S(2)}, u32[]{:S(2)}) %all-to-all-start.1) | async-done | bytes 786464 | tf_op jit(solution)/shard_map/all_to_all | solution.py:34
  81.2 5.8 rev.25
  87.0 3.6 convolution_convert_fusion.1
  90.7 2.4 collective-permute-start
  95.3 3.4 collective-permute-done.1
  101.6 4.7 collective-permute-start.3
  106.3 1.5 collective-permute-done.3
  107.9 2.4 fusion.5
  113.4 36.5 %all_to_all.64 = bf16[64,1,2,2048]{3,2,1,0:T(2,128)(2,1)S(1)} all-to-all(bf16[64,1,2,2048]{3,2,1,0:T(2,128)(2,1)S(1)} %bitcast.68), channel_id=1, replica_groups=mesh['dp'=4,'seq'=64] {'seq'}, dimensions={0} | all-to-all | bytes 1048576 | tf_op jit(solution)/shard_map/all_to_all | solution.py:32
  151.0 5.7 all-to-all-start.5
  157.6 14.2 %all-to-all-done.5 = bf16[64,1,2,2048]{3,2,1,0:T(2,128)(2,1)S(1)} async-done(((bf16[64,1,2,2048]{3,2,1,0:T(2,128)(2,1)}), bf16[64,1,2,2048]{3,2,1,0:T(2,128)(2,1)S(1)}, u32[]{:S(2)}, u32[]{:S(2)}) %all-to-all-start.5) | async-done | bytes 524320 | tf_op jit(solution)/shard_map/all_to_all | solution.py:34
  172.1 1.8 rev.30
  173.9 2.4 fusion.25
  176.3 4.3 convolution_convert_fusion
  181.1 18.9 %all_to_all.65 = bf16[64,1,2,1024]{3,2,1,0:T(2,128)(2,1)S(1)} all-to-all(bf16[64,1,2,1024]{3,2,1,0:T(2,128)(2,1)S(1)} %bitcast.70), channel_id=1, replica_groups=mesh['dp'=4,'seq'=64] {'seq'}, dimensions={0} | all-to-all | bytes 524288 | tf_op jit(solution)/shard_map/all_to_all | solution.py:32
  200.2 18.0 %all_to_all.66 = bf16[64,1,2,1024]{3,2,1,0:T(2,128)(2,1)S(1)} all-to-all(bf16[64,1,2,1024]{3,2,1,0:T(2,128)(2,1)S(1)} %reverse_bitcast_fusion.2), channel_id=1, replica_groups=mesh['dp'=4,'seq'=64] {'seq'}, dimensions={0} | all-to-all | bytes 524288 | tf_op jit(solution)/shard_map/all_to_all | solution.py:34
  220.0 2.1 fusion.27
  222.1 194.8 %all-reduce.4.cloned.1.call-done = (f32[7,1024]{1,0:T(8,128)}, f32[5,2048]{1,0:T(8,128)}) async-done(((f32[7,1024]{1,0:T(8,128)}, f32[5,2048]{1,0:T(8,128)}), (f32[7,1024]{1,0:T(8,128)}, f32[5,2048]{1,0:T(8,128)})) %all-reduce.4.cloned.1.call-update) | async-done | bytes 69648 | tf_op jit(solution)/shard_map/psum | solution.py:131
  419.8 42.5 %reduce-scatter.2.cloned.1.call-done = bf16[512,1024]{1,0:T(8,128)(2,1)} async-done(((bf16[2048,1024]{1,0:T(8,128)(2,1)}), bf16[512,1024]{1,0:T(8,128)(2,1)}) %reduce-scatter.2.cloned.1.call-update) | async-done | bytes 1048592 | tf_op jit(solution)/shard_map/reduce_scatter | solution.py:110
  462.3 380.9 %all-reduce.5 = f32[512,1024]{1,0:T(8,128)S(1)} all-reduce(bf16[512,1024]{1,0:T(8,128)(2,1)} %reduce-scatter.2.cloned.1.call-done), channel_id=1, replica_groups=mesh['dp'=4,'seq'=64] {'seq'}, use_global_device_ids=true, to_apply=%region_1.0 | all-reduce | flops 524288 | bytes 3145728 | tf_op jit(solution)/shard_map/psum | solution.py:118
  843.2 1.5 broadcast_multiply_fusion
  (67 shorter events, 20.3 us)
Async XLA Ops:
  7.2 1.8 copy-start
  7.2 79.8 %all-gather.2.cloned.1.call-start = ((), (), s32[]{:S(2)}) async-start(), calls=%async_computation.7 | async-start | bytes 5242880 | tf_op jit(solution)/shard_map/all_gather | solution.py:67
  11.7 45.6 %copy-start.4 = (f32[7,1024]{1,0:T(8,128)S(1)}, f32[7,1024]{1,0:T(8,128)}, u32[]{:S(2)}) copy-start(f32[7,1024]{1,0:T(8,128)} %param.10) | copy-start | bytes 86020
  51.2 29.7 %all-to-all-start.1 = ((bf16[64,1,2,3072]{3,2,1,0:T(2,128)(2,1)}), bf16[64,1,2,3072]{3,2,1,0:T(2,128)(2,1)S(1)}, u32[]{:S(2)}, u32[]{:S(2)}) async-start(bf16[64,1,2,3072]{3,2,1,0:T(2,128)(2,1)} %reverse_bitcast_fusion), calls=%async_computation.1 | async-start | bytes 1572864 | tf_op jit(solution)/shard_map/all_to_all | solution.py:34
  90.6 8.3 copy-start.2
  90.7 4.6 collective-permute-start
  93.1 5.6 collective-permute-start.1
  100.3 6.1 collective-permute-start.2
  101.6 6.3 collective-permute-start.3
  107.9 2.4 copy-start.6
  110.3 1.4 copy-start.3
  111.7 1.3 copy-start.1
  149.9 24.0 %copy-start.5 = (s32[1,128]{1,0:T(1,128)S(1)}, s32[1,128]{1,0:T(1,128)}, u32[]{:S(2)}) copy-start(s32[1,128]{1,0:T(1,128)} %param.7) | copy-start | bytes 1540
  151.0 20.8 %all-to-all-start.5 = ((bf16[64,1,2,2048]{3,2,1,0:T(2,128)(2,1)}), bf16[64,1,2,2048]{3,2,1,0:T(2,128)(2,1)S(1)}, u32[]{:S(2)}, u32[]{:S(2)}) async-start(bf16[64,1,2,2048]{3,2,1,0:T(2,128)(2,1)} %reverse_bitcast_fusion.1), calls=%async_computation.5 | async-start | bytes 1048576 | tf_op jit(solution)/shard_map/all_to_all | solution.py:34
  156.7 260.2 %all-reduce.4.cloned.1.call-start = ((), (), s32[]{:S(2)}) async-start(), calls=%async_computation.9 | async-start | bytes 196608 | tf_op jit(solution)/shard_map/psum | solution.py:131
  176.2 286.0 %reduce-scatter.2.cloned.1.call-start = ((), (), s32[]{:S(2)}) async-start(), calls=%async_computation.8 | async-start | bytes 5242880 | tf_op jit(solution)/shard_map/reduce_scatter | solution.py:110
Sparse Core Ops, SparseCore 0:
  9.8 66.1 all-gather.1
  176.4 240.5 all-reduce.3
  419.5 42.7 reduce-scatter.1
where the time goes:
time: 852 us; the launch traced here: 851 us
  blocking collectives  492 us (58%)
  waiting for transfers between devices  281 us (33%)
  starting transfers between devices  21.7 us (3%)
  local copies, waits for them, and re-layouts  16.3 us (2%)
  between operations  14.2 us (2%)
  matrix products  13.4 us (2%)
  other arithmetic  12.8 us (2%)
    psum x1, blocking collectives, local(): grad_weight = lax.psum(owner_rows, 'seq') * factor  381 us
    psum x1, waiting for transfers between devices, local(): kernel_sum, table_sum = lax.psum((kernel_part, table_part), ('dp', 'seq'))  195 us
    all_to_all x3, blocking collectives, mirror_rows(): lax.all_to_all(slab_split, 'seq', split_axis=0, concat_axis=1, tiled=True)  93.4 us
    reduce_scatter x1, waiting for transfers between devices, local(): lax.psum_scatter(lax.dot_general(column_names, grad_stack, (((0,), (0,)),...  42.5 us
    all_to_all x2, waiting for transfers between devices, mirror_rows(): lax.all_to_all(turned, 'seq', split_axis=0, concat_axis=1, tiled=True)  37.7 us
    all_to_all x1, blocking collectives, mirror_rows(): lax.all_to_all(turned, 'seq', split_axis=0, concat_axis=1, tiled=True)  18 us
  transfers between devices with their start and end apart: 9, of which 6 were waited for; matrix products, arithmetic and copies ran while one was open for 3% of the time, Pallas kernels for 0%

commit v1 on v0

v1 whole, which is shorter than its diff:
```python
import math

import jax
import jax.numpy as jnp
import numpy as np
from jax import lax
from jax.sharding import Mesh, PartitionSpec as P

AXES = ("xl", "c", "xh", "z", "y")
SIZES = (2, 2, 2, 8, 4)
EDGE = 8


def shift(cells, axes, target):
    sizes = [SIZES[AXES.index(axis)] for axis in axes]
    pairs = []
    for place in np.ndindex(*sizes):
        goal = target(*place)
        if goal is not None:
            pairs.append((int(np.ravel_multi_index(place, sizes)), int(np.ravel_multi_index(goal, sizes))))
    return lax.ppermute(cells, axes if len(axes) > 1 else axes[0], pairs)


def swap_core(cells):
    return shift(cells, ("c",), lambda c: (1 - c,))


def side_x(xl, c, xh):
    x = (2 * xh + xl + (1 if c == 0 else 3)) % 4
    return (x % 2, c, x // 2)


def turn_x(xl, xh):
    x = 3 - (2 * xh + xl)
    return (x % 2, x // 2)


def neighbour(step):
    def target(xh, z, y):
        place = (xh * 8 + z) * 4 + y + step
        if not 0 <= place < 64:
            return None
        return (place // 32, place // 4 % 8, place % 4)

    return target


def sum_everywhere(cells):
    cells = cells + swap_core(cells)
    cells = cells + shift(cells, ("xl",), lambda a: (1 - a,))
    cells = cells + shift(cells, ("xl", "xh"), turn_x)
    cells = cells + shift(cells, ("y",), lambda a: (a ^ 1,))
    cells = cells + shift(cells, ("y",), lambda a: (3 - a,))
    cells = cells + shift(cells, ("z",), lambda a: (a ^ 1,))
    cells = cells + shift(cells, ("z",), lambda a: (a ^ 2,))
    return cells + shift(cells, ("z",), lambda a: (7 - a,))


def added(*parts):
    total = parts[0].astype(jnp.float32)
    for part in parts[1:]:
        total = total + part.astype(jnp.float32)
    return total


def reduce_rows(own, mate, side, side_mate):
    side_sum = added(side, swap_core(side_mate)).astype(jnp.bfloat16)
    from_side = shift(side_sum, ("xl", "c", "xh"), side_x)
    block = added(own, swap_core(mate), from_side).astype(jnp.bfloat16)
    y = lax.axis_index("y")
    rows = block.shape[0] // 4
    parts = [lax.dynamic_slice_in_dim(block, y * rows, rows, 0)]
    for step in (1, 2, 3):
        chunk = lax.dynamic_slice_in_dim(block, (y + step) % 4 * rows, rows, 0)
        parts.append(shift(chunk, ("y",), lambda a: ((a + step) % 4,)))
    quarter = added(*parts).astype(jnp.bfloat16)
    pieces = quarter.reshape(16, rows // 16, -1)
    pieces = lax.all_to_all(pieces, ("xh", "z"), split_axis=0, concat_axis=0, tiled=True)
    piece = jnp.sum(pieces.astype(jnp.float32), axis=0).astype(jnp.bfloat16)
    pieces = lax.all_to_all(
        jnp.broadcast_to(piece[None], pieces.shape), ("xh", "z"), split_axis=0, concat_axis=0, tiled=True
    )
    quarter = pieces.reshape(rows, -1)
    quarters = [quarter] + [shift(quarter, ("y",), lambda a: ((a + step) % 4,)) for step in (1, 2, 3)]
    stacked = jnp.stack(quarters)
    return jnp.concatenate([stacked[(y - row) % 4] for row in range(4)], axis=0)


def local(hidden, tokens, embedding, weight, kernel, cotangent):
    window = hidden[0]
    token_codes = tokens[0]
    upstream = cotangent[0]
    rows, features = window.shape
    units = weight.shape[1]
    taps = kernel.shape[0]
    reach = (taps - 1) // 2
    factor = 1.0 / math.sqrt(rows * 256)
    width = features // 4
    me = 2 * lax.axis_index("xl") + lax.axis_index("c")
    blocks = [me ^ r for r in range(4)]
    weights = [weight, swap_core(weight), shift(weight, ("xl", "c", "xh"), side_x)]
    weights.append(swap_core(weights[2]))

    looked = jnp.zeros((rows, features), jnp.float32)
    for symbol in range(embedding.shape[0]):
        looked = looked + jnp.where((token_codes == symbol)[:, None], embedding[symbol][None, :], 0.0)
    stream = (window.astype(jnp.float32) + looked).astype(jnp.bfloat16)
    both = jnp.concatenate([stream, upstream], axis=1)
    before = shift(both[rows - EDGE :], ("xh", "z", "y"), neighbour(1))
    after = shift(both[:EDGE], ("xh", "z", "y"), neighbour(-1))
    wide = jnp.concatenate([before, both, after], axis=0)
    total = rows + 2 * EDGE

    def exchange(size):
        return (
            lax.broadcasted_iota(jnp.int32, (size, size), 0) + lax.broadcasted_iota(jnp.int32, (size, size), 1)
            == size - 1
        ).astype(jnp.bfloat16)

    def flipped(cells):
        size = 256
        count = cells.shape[1] // size
        turn = exchange(size)
        return jnp.concatenate(
            [
                jnp.dot(
                    cells[:, (count - 1 - at) * size : (count - at) * size],
                    turn,
                    preferred_element_type=jnp.float32,
                ).astype(jnp.bfloat16)
                for at in range(count)
            ],
            axis=1,
        )

    forward = [lax.dynamic_slice_in_dim(wide, at * width, width, 1) for at in blocks]
    reverse = [flipped(forward[r ^ 3]) for r in range(4)]
    stacks = [jnp.concatenate([forward[r], reverse[r]], axis=0) for r in range(4)]
    projected = sum(jnp.dot(stacks[r], weights[r], preferred_element_type=jnp.float32) for r in range(4))
    values = projected.astype(jnp.bfloat16).astype(jnp.float32)
    values = [values[:total], values[total:]]
    ups = wide[:, features:]
    ups = [ups.astype(jnp.float32), flipped(ups).astype(jnp.float32)]
    outs = []
    grads = []
    kernel_part = jnp.zeros((taps, units), jnp.float32)
    for way in range(2):
        offsets = [EDGE + (tap - reach if way == 0 else reach - tap) for tap in range(taps)]
        linear = values[way]
        logistic = jax.nn.sigmoid(linear)
        gating = linear * logistic
        grad_mix = ups[way] * gating
        mixing = kernel[0][None] * linear[offsets[0] : offsets[0] + rows]
        for tap in range(1, taps):
            mixing = mixing + kernel[tap][None] * linear[offsets[tap] : offsets[tap] + rows]
        mid = slice(EDGE, EDGE + rows)
        outs.append(mixing * gating[mid])
        accumulated = ups[way][mid] * mixing * logistic[mid] * (1.0 + linear[mid] * (1.0 - logistic[mid]))
        for tap in range(taps):
            lower = 2 * EDGE - offsets[tap]
            accumulated = accumulated + kernel[tap][None] * grad_mix[lower : lower + rows]
        grads.append(accumulated.astype(jnp.bfloat16))
        kernel_part = kernel_part + jnp.stack(
            [jnp.sum(grad_mix[mid] * linear[at : at + rows], axis=0) for at in offsets]
        )
    block_result = (outs[0] + flipped(outs[1].astype(jnp.bfloat16)).astype(jnp.float32)).astype(jnp.bfloat16)
    grad_stack = jnp.concatenate(grads, axis=0)
    mids = [jnp.concatenate([forward[r][EDGE : EDGE + rows], reverse[r][EDGE : EDGE + rows]], axis=0) for r in range(4)]
    products = [
        lax.dot_general(
            mids[r], grad_stack, (((0,), (0,)), ((), ())), preferred_element_type=jnp.float32
        ).astype(jnp.bfloat16)
        for r in range(4)
    ]
    grad_weight = reduce_rows(*products).astype(jnp.float32) * factor
    backs = [
        lax.dot_general(grad_stack, weights[r], (((1,), (1,)), ((), ())), preferred_element_type=jnp.float32)
        for r in range(4)
    ]
    streams = jnp.stack(
        [backs[r][:rows] + flipped(backs[r ^ 3][rows:].astype(jnp.bfloat16)).astype(jnp.float32) for r in range(4)]
    )
    grad_stream = jnp.concatenate([streams[at ^ me] for at in range(4)], axis=1)
    one_hot = (jnp.arange(embedding.shape[0], dtype=jnp.int32)[:, None] == token_codes[None, :]).astype(jnp.float32)
    table_part = jnp.dot(one_hot, grad_stream, precision=lax.Precision.HIGHEST, preferred_element_type=jnp.float32)
    small = jnp.concatenate([kernel_part, table_part.reshape(-1, units)], axis=0)
    small = sum_everywhere(small) * factor
    return (
        block_result[None],
        grad_stream.astype(jnp.bfloat16)[None],
        grad_weight,
        small[:taps],
        small[taps:].reshape(embedding.shape),
    )


def solution(mesh):
    fine = Mesh(mesh.devices.reshape(SIZES), AXES)
    batch = ("xl", "c")
    place = ("xh", "z", "y")
    in_specs = (P(batch, place, None), P(batch, place), P(), P(batch, None), P(), P(batch, place, None))
    out_specs = (P(batch, place, None), P(batch, place, None), P(batch, None), P(), P())
    return jax.shard_map(local, mesh=fine, in_specs=in_specs, out_specs=out_specs, check_vma=False)
```

time: 852 us -> 140 us (0.16)
  blocking collectives: 492 us -> 0 us
  waiting for transfers between devices: 281 us -> 43.8 us
  starting transfers between devices: 21.7 us -> 54.8 us
  between operations: 14.2 us -> 1.45 us
  local copies, waits for them, and re-layouts: 16.3 us -> 7.37 us
    psum x1 -> x0, blocking collectives: 381 us -> none  [local(): grad_weight = lax.psum(owner_rows, 'seq') * factor]
    psum x1 -> x0, waiting for transfers between devices: 195 us -> none  [local(): kernel_sum, table_sum = lax.psum((kernel_part, table_part), ('dp', 'seq'))]
    all_to_all x4 -> x0, blocking collectives: 111 us -> none  [the longest x3 93.4 us: mirror_rows(): lax.all_to_all(slab_split, 'seq', split_axis=0, concat_axis=1, tiled=True)]
    reduce_scatter x1 -> x0, waiting for transfers between devices: 42.5 us -> none  [local(): lax.psum_scatter(lax.dot_general(column_names, grad_stack, (((0,), (0,)),...]
    ppermute x4 -> x22, waiting for transfers between devices: 4.92 us -> 43.8 us  [shift(): return lax.ppermute(cells, axes if len(axes) > 1 else axes[0], pairs)]
    all_to_all x2, waiting for transfers between devices: 37.7 us -> 0.01 us  [the longest x1 0.01 us: reduce_rows(): lax.all_to_all(pieces, ('xh', 'z'), split_axis=0, concat_axis=0, tiled=True)]
    ppermute x4 -> x22, starting transfers between devices: 9.68 us -> 35 us  [shift(): return lax.ppermute(cells, axes if len(axes) > 1 else axes[0], pairs)]
    rev x4 -> x0, local copies, waits for them, and re-layouts: 9.39 us -> none  [the longest x1 5.81 us: local(): stream_rev = mirrored[:, :features][:, ::-1]]
  transfers between devices with their start and end apart: 9 -> 24, of which waited for: 6 -> 13; matrix products, arithmetic and copies ran while one was open for 3% -> 18% of each run, Pallas kernels for 0% -> 0%
where the time goes in v1:
time: 140 us; the launch traced here: 138 us
  starting transfers between devices  54.8 us (39%)
  waiting for transfers between devices  43.8 us (31%)
  other arithmetic  16.4 us (12%)
  matrix products  14.1 us (10%)
  local copies, waits for them, and re-layouts  7.37 us (5%)
  between operations  1.45 us (1%)
    ppermute x22, waiting for transfers between devices, shift(): return lax.ppermute(cells, axes if len(axes) > 1 else axes[0], pairs)  43.8 us
    ppermute x22, starting transfers between devices, shift(): return lax.ppermute(cells, axes if len(axes) > 1 else axes[0], pairs)  35 us
    all_to_all x1, starting transfers between devices, reduce_rows(): lax.all_to_all(pieces, ('xh', 'z'), split_axis=0, concat_axis=0, tiled=True)  10 us
    all_to_all x1, starting transfers between devices, reduce_rows(): lax.all_to_all(jnp.broadcast_to(piece[None], pieces.shape), ('xh', 'z'),...  9.72 us
    dot_general x4, matrix products, local(): lax.dot_general(mids[r], grad_stack, (((0,), (0,)), ((), ())), preferred_...  4.84 us
    dot_general x24, matrix products, flipped(): jnp.dot(cells[:, (count - 1 - at) * size:(count - at) * size], turn, pref...  4.14 us
    convert_element_type x2, other arithmetic, local(): grads.append(accumulated.astype(jnp.bfloat16))  3.53 us
  transfers between devices with their start and end apart: 24, of which 13 were waited for; matrix products, arithmetic and copies ran while one was open for 18% of the time, Pallas kernels for 0%

profile of v1, /device:TPU:2, one launch (start us, length us, event | category | flops | bytes accessed | tf_op | source)
XLA Modules:
  0.0 137.9 jit_solution(6412335678225443970)
XLA Ops:
  6.4 3.5 %collective-permute-start = (bf16[8,3072]{1,0:T(8,128)(2,1)S(1)}, bf16[8,3072]{1,0:T(8,128)(2,1)S(1)}, u32[]{:S(2)}, u32[]{:S(2)}) collective-permute-start(bf16[8,3072]{1,0:T(8,128)(2,1)S(1)} %get-tuple-element.59), channel_id=1, source_target_pairs={{0,1},{1,2},{2,3},{3,4},{4,5},{5,6},{6,7},{7,8},{8,9},{9,10},{10,1... | collective-permute-start | bytes 147464 | tf_op jit(solution)/shard_map/ppermute | solution.py:21
  11.6 4.3 %collective-permute-done.1 = bf16[8,3072]{1,0:T(8,128)(2,1)S(1)} collective-permute-done((bf16[8,3072]{1,0:T(8,128)(2,1)S(1)}, bf16[8,3072]{1,0:T(8,128)(2,1)S(1)}, u32[]{:S(2)}, u32[]{:S(2)}) %collective-permute-start.1) | collective-permute-done | bytes 49184 | tf_op jit(solution)/shard_map/ppermute | solution.py:21
  23.4 1.8 %fusion.20 = (bf16[128,1024]{1,0:T(8,128)(2,1)S(1)}, f32[128,1024]{1,0:T(8,128)}) fusion(f32[144,1024]{1,0:T(8,128)S(1)} %get-tuple-element.33, f32[144,1024]{1,0:T(8,128)S(1)} %maximum_convert_fusion, f32[144,1024]{1,0:T(8,128)S(1)} %get-tuple-element.32, f32[288,1024]{1,0:T(8,128)S(1)} %fusion.1, f32[1024]{0:T(1024)S(1)} %bitcast.96, ...), kind=kLoop, calls=%fused_computation.64 | loop fusion | flops 4456448 | bytes 9203712 | tf_op jit(solution)/shard_map/convert_element_type | solution.py:162
  25.1 1.8 %fusion.30 = (bf16[128,1024]{1,0:T(8,128)(2,1)S(1)}, f32[128,1024]{1,0:T(8,128)}) fusion(f32[144,1024]{1,0:T(8,128)S(1)} %get-tuple-element.34, f32[144,1024]{1,0:T(8,128)S(1)} %slice_convert_fusion, f32[144,1024]{1,0:T(8,128)S(1)} %get-tuple-element.31, f32[288,1024]{1,0:T(8,128)S(1)} %fusion.1, f32[1024]{0:T(1024)S(1)} %bitcast.97, f32[1024]{0:T(1024)S(1)} %bitcast.99, ...), kind=kLoop, calls=%fused_computation.81 | loop fusion | flops 4456448 | bytes 9203712 | tf_op jit(solution)/shard_map/convert_element_type | solution.py:162
  33.7 2.5 %collective-permute-done.6 = bf16[512,1024]{1,0:T(8,128)(2,1)S(1)} collective-permute-done((bf16[512,1024]{1,0:T(8,128)(2,1)S(1)}, bf16[512,1024]{1,0:T(8,128)(2,1)S(1)}, u32[]{:S(2)}, u32[]{:S(2)}) %collective-permute-start.6) | collective-permute-done | bytes 1048608 | tf_op jit(solution)/shard_map/ppermute | solution.py:21
  37.7 6.0 %collective-permute-start.7 = (bf16[512,1024]{1,0:T(8,128)(2,1)}, bf16[512,1024]{1,0:T(8,128)(2,1)}, u32[]{:S(2)}, u32[]{:S(2)}) collective-permute-start(bf16[512,1024]{1,0:T(8,128)(2,1)} %add_convert_fusion.1), channel_id=1, source_target_pairs={{0,128},{32,160},{64,224},{96,192},{128,32},{160,0},{192,64},{224,... | collective-permute-start | bytes 3145736 | tf_op jit(solution)/shard_map/ppermute | solution.py:21
  50.4 5.9 %collective-permute-done.7 = bf16[512,1024]{1,0:T(8,128)(2,1)} collective-permute-done((bf16[512,1024]{1,0:T(8,128)(2,1)}, bf16[512,1024]{1,0:T(8,128)(2,1)}, u32[]{:S(2)}, u32[]{:S(2)}) %collective-permute-start.7) | collective-permute-done | bytes 1048608 | tf_op jit(solution)/shard_map/ppermute | solution.py:21
  56.3 2.2 %add_convert_fusion = bf16[512,1024]{1,0:T(8,128)(2,1)S(1)} fusion(bf16[512,1024]{1,0:T(8,128)(2,1)} %collective-permute-done.7, bf16[512,1024]{1,0:T(8,128)(2,1)} %collective-permute-done.5, bf16[512,1024]{1,0:T(8,128)(2,1)S(1)} %convolution_convert_fusion.3), kind=kLoop, calls=%fused_computation.1 | loop fusion | flops 3145728 | bytes 4194304 | tf_op jit(solution)/shard_map/convert_element_type | solution.py:69
  58.6 1.7 %collective-permute-start.10 = (bf16[128,1024]{1,0:T(8,128)(2,1)S(1)}, bf16[128,1024]{1,0:T(8,128)(2,1)S(1)}, u32[]{:S(2)}, u32[]{:S(2)}) collective-permute-start(bf16[128,1024]{1,0:T(8,128)(2,1)S(1)} %get-tuple-element.45), channel_id=1, source_target_pairs={{0,3},{1,0},{2,1},{3,2},{4,7},{5,4},{6,5},{7,6},{8,11},{9,8},{10,9... | collective-permute-start | bytes 786440 | tf_op jit(solution)/shard_map/ppermute | solution.py:21
  61.9 2.2 %collective-permute-start.15 = (f32[17,1024]{1,0:T(8,128)S(1)}, f32[17,1024]{1,0:T(8,128)S(1)}, u32[]{:S(2)}, u32[]{:S(2)}) collective-permute-start(f32[17,1024]{1,0:T(8,128)S(1)} %fusion.200), channel_id=1, source_target_pairs={{0,128},{128,0},{1,129},{129,1},{2,130},{130,2},{3,131},{131,3},{4... | collective-permute-start | bytes 208904 | tf_op jit(solution)/shard_map/ppermute | solution.py:21
  64.1 3.7 %collective-permute-done.10 = bf16[128,1024]{1,0:T(8,128)(2,1)S(1)} collective-permute-done((bf16[128,1024]{1,0:T(8,128)(2,1)S(1)}, bf16[128,1024]{1,0:T(8,128)(2,1)S(1)}, u32[]{:S(2)}, u32[]{:S(2)}) %collective-permute-start.10) | collective-permute-done | bytes 262176 | tf_op jit(solution)/shard_map/ppermute | solution.py:21
  67.9 6.4 %collective-permute-done.8 = bf16[128,1024]{1,0:T(8,128)(2,1)S(1)} collective-permute-done((bf16[128,1024]{1,0:T(8,128)(2,1)S(1)}, bf16[128,1024]{1,0:T(8,128)(2,1)S(1)}, u32[]{:S(2)}, u32[]{:S(2)}) %collective-permute-start.8) | collective-permute-done | bytes 262176 | tf_op jit(solution)/shard_map/ppermute | solution.py:21
  75.2 10.0 %all-to-all-start = ((bf16[16,8,1024]{2,1,0:T(8,128)(2,1)}), bf16[16,8,1024]{2,1,0:T(8,128)(2,1)S(1)}, u32[]{:S(2)}, u32[]{:S(2)}) async-start(bf16[16,8,1024]{2,1,0:T(8,128)(2,1)} %fusion.63), calls=%async_computation | async-start | bytes 524288 | tf_op jit(solution)/shard_map/all_to_all | solution.py:78
  85.4 2.7 %collective-permute-start.16 = (f32[17,1024]{1,0:T(8,128)S(1)}, f32[17,1024]{1,0:T(8,128)S(1)}, u32[]{:S(2)}, u32[]{:S(2)}) collective-permute-start(f32[17,1024]{1,0:T(8,128)S(1)} %add.396), channel_id=1, source_target_pairs={{0,160},{32,128},{128,32},{160,0},{1,161},{33,129},{129,33},{161,1... | collective-permute-start | bytes 208904 | tf_op jit(solution)/shard_map/ppermute | solution.py:21
  88.3 3.1 %collective-permute-done.16 = f32[17,1024]{1,0:T(8,128)S(1)} collective-permute-done((f32[17,1024]{1,0:T(8,128)S(1)}, f32[17,1024]{1,0:T(8,128)S(1)}, u32[]{:S(2)}, u32[]{:S(2)}) %collective-permute-start.16) | collective-permute-done | bytes 69664 | tf_op jit(solution)/shard_map/ppermute | solution.py:21
  91.7 4.4 %collective-permute-done.17 = f32[17,1024]{1,0:T(8,128)S(1)} collective-permute-done((f32[17,1024]{1,0:T(8,128)S(1)}, f32[17,1024]{1,0:T(8,128)S(1)}, u32[]{:S(2)}, u32[]{:S(2)}) %collective-permute-start.17) | collective-permute-done | bytes 69664 | tf_op jit(solution)/shard_map/ppermute | solution.py:21
  97.3 9.7 %all-to-all-start.1 = ((bf16[16,8,1024]{2,1,0:T(8,128)(2,1)}), bf16[16,8,1024]{2,1,0:T(8,128)(2,1)S(1)}, u32[]{:S(2)}, u32[]{:S(2)}) async-start(bf16[16,8,1024]{2,1,0:T(8,128)(2,1)} %broadcast_in_dim.107), calls=%async_computation.1 | async-start | bytes 524288 | tf_op jit(solution)/shard_map/all_to_all | solution.py:80
  107.2 2.0 %collective-permute-start.19 = (f32[17,1024]{1,0:T(8,128)S(1)}, f32[17,1024]{1,0:T(8,128)S(1)}, u32[]{:S(2)}, u32[]{:S(2)}) collective-permute-start(f32[17,1024]{1,0:T(8,128)S(1)} %add.399), channel_id=1, source_target_pairs={{0,4},{4,0},{8,12},{12,8},{16,20},{20,16},{24,28},{28,24},{1,5},{5... | collective-permute-start | bytes 208904 | tf_op jit(solution)/shard_map/ppermute | solution.py:21
  110.0 4.4 %collective-permute-done.19 = f32[17,1024]{1,0:T(8,128)S(1)} collective-permute-done((f32[17,1024]{1,0:T(8,128)S(1)}, f32[17,1024]{1,0:T(8,128)S(1)}, u32[]{:S(2)}, u32[]{:S(2)}) %collective-permute-start.19) | collective-permute-done | bytes 69664 | tf_op jit(solution)/shard_map/ppermute | solution.py:21
  114.4 3.7 %collective-permute-start.20 = (f32[17,1024]{1,0:T(8,128)S(1)}, f32[17,1024]{1,0:T(8,128)S(1)}, u32[]{:S(2)}, u32[]{:S(2)}) collective-permute-start(f32[17,1024]{1,0:T(8,128)S(1)} %add.400), channel_id=1, source_target_pairs={{0,8},{4,12},{8,0},{12,4},{16,24},{20,28},{24,16},{28,20},{1,9},{5... | collective-permute-start | bytes 208904 | tf_op jit(solution)/shard_map/ppermute | solution.py:21
  118.1 3.4 %collective-permute-done.20 = f32[17,1024]{1,0:T(8,128)S(1)} collective-permute-done((f32[17,1024]{1,0:T(8,128)S(1)}, f32[17,1024]{1,0:T(8,128)S(1)}, u32[]{:S(2)}, u32[]{:S(2)}) %collective-permute-start.20) | collective-permute-done | bytes 69664 | tf_op jit(solution)/shard_map/ppermute | solution.py:21
  121.5 3.1 %collective-permute-start.21 = (f32[17,1024]{1,0:T(8,128)S(1)}, f32[17,1024]{1,0:T(8,128)S(1)}, u32[]{:S(2)}, u32[]{:S(2)}) collective-permute-start(f32[17,1024]{1,0:T(8,128)S(1)} %add.401), channel_id=1, source_target_pairs={{0,28},{4,24},{8,20},{12,16},{16,12},{20,8},{24,4},{28,0},{1,29},{... | collective-permute-start | bytes 208904 | tf_op jit(solution)/shard_map/ppermute | solution.py:21
  124.9 4.0 %collective-permute-start.12 = (bf16[128,1024]{1,0:T(8,128)(2,1)S(1)}, bf16[128,1024]{1,0:T(8,128)(2,1)S(1)}, u32[]{:S(2)}, u32[]{:S(2)}) collective-permute-start(bf16[128,1024]{1,0:T(8,128)(2,1)S(1)} %bitcast.80), channel_id=1, source_target_pairs={{0,2},{1,3},{2,0},{3,1},{4,6},{5,7},{6,4},{7,5},{8,10},{9,11},{10,... | collective-permute-start | bytes 786440 | tf_op jit(solution)/shard_map/ppermute | solution.py:21
  132.6 3.5 %collective-permute-done.12 = bf16[128,1024]{1,0:T(8,128)(2,1)S(1)} collective-permute-done((bf16[128,1024]{1,0:T(8,128)(2,1)S(1)}, bf16[128,1024]{1,0:T(8,128)(2,1)S(1)}, u32[]{:S(2)}, u32[]{:S(2)}) %collective-permute-start.12) | collective-permute-done | bytes 262176 | tf_op jit(solution)/shard_map/ppermute | solution.py:21
  (137 shorter events, 40.6 us)
Async XLA Ops:
  0.7 19.1 %collective-permute-start.2 = (bf16[512,1024]{1,0:T(8,128)(2,1)}, bf16[512,1024]{1,0:T(8,128)(2,1)S(1)}, u32[]{:S(2)}, u32[]{:S(2)}) collective-permute-start(bf16[512,1024]{1,0:T(8,128)(2,1)} %param.9), channel_id=1, source_target_pairs={{0,64},{64,0},{1,65},{65,1},{2,66},{66,2},{3,67},{67,3},{4,68},{68... | collective-permute-start | bytes 3145736 | tf_op jit(solution)/shard_map/ppermute | solution.py:21
  0.8 18.1 %collective-permute-start.3 = (bf16[512,1024]{1,0:T(8,128)(2,1)}, bf16[512,1024]{1,0:T(8,128)(2,1)S(1)}, u32[]{:S(2)}, u32[]{:S(2)}) collective-permute-start(bf16[512,1024]{1,0:T(8,128)(2,1)} %param.9), channel_id=1, source_target_pairs={{0,128},{32,160},{64,224},{96,192},{128,32},{160,0},{192,64},{224,... | collective-permute-start | bytes 3145736 | tf_op jit(solution)/shard_map/ppermute | solution.py:21
  6.4 5.2 %collective-permute-start = (bf16[8,3072]{1,0:T(8,128)(2,1)S(1)}, bf16[8,3072]{1,0:T(8,128)(2,1)S(1)}, u32[]{:S(2)}, u32[]{:S(2)}) collective-permute-start(bf16[8,3072]{1,0:T(8,128)(2,1)S(1)} %get-tuple-element.59), channel_id=1, source_target_pairs={{0,1},{1,2},{2,3},{3,4},{4,5},{5,6},{6,7},{7,8},{8,9},{9,10},{10,1... | collective-permute-start | bytes 147464 | tf_op jit(solution)/shard_map/ppermute | solution.py:21
  9.9 6.0 %collective-permute-start.1 = (bf16[8,3072]{1,0:T(8,128)(2,1)S(1)}, bf16[8,3072]{1,0:T(8,128)(2,1)S(1)}, u32[]{:S(2)}, u32[]{:S(2)}) collective-permute-start(bf16[8,3072]{1,0:T(8,128)(2,1)S(1)} %get-tuple-element.60), channel_id=1, source_target_pairs={{1,0},{2,1},{3,2},{4,3},{5,4},{6,5},{7,6},{8,7},{9,8},{10,9},{11,1... | collective-permute-start | bytes 147464 | tf_op jit(solution)/shard_map/ppermute | solution.py:21
  18.9 2.7 %collective-permute-start.4 = (bf16[512,1024]{1,0:T(8,128)(2,1)S(1)}, bf16[512,1024]{1,0:T(8,128)(2,1)S(1)}, u32[]{:S(2)}, u32[]{:S(2)}) collective-permute-start(bf16[512,1024]{1,0:T(8,128)(2,1)S(1)} %collective-permute-done.3), channel_id=1, source_target_pairs={{0,64},{64,0},{1,65},{65,1},{2,66},{66,2},{3,67},{67,3},{4,68},{68... | collective-permute-start | bytes 3145736 | tf_op jit(solution)/shard_map/ppermute | solution.py:21
  31.8 18.6 %collective-permute-start.5 = (bf16[512,1024]{1,0:T(8,128)(2,1)}, bf16[512,1024]{1,0:T(8,128)(2,1)}, u32[]{:S(2)}, u32[]{:S(2)}) collective-permute-start(bf16[512,1024]{1,0:T(8,128)(2,1)} %convolution_convert_fusion.2), channel_id=1, source_target_pairs={{0,64},{64,0},{1,65},{65,1},{2,66},{66,2},{3,67},{67,3},{4,68},{68... | collective-permute-start | bytes 3145736 | tf_op jit(solution)/shard_map/ppermute | solution.py:21
  32.4 3.8 %collective-permute-start.6 = (bf16[512,1024]{1,0:T(8,128)(2,1)S(1)}, bf16[512,1024]{1,0:T(8,128)(2,1)S(1)}, u32[]{:S(2)}, u32[]{:S(2)}) collective-permute-start(bf16[512,1024]{1,0:T(8,128)(2,1)S(1)} %convolution_convert_fusion), channel_id=1, source_target_pairs={{0,64},{64,0},{1,65},{65,1},{2,66},{66,2},{3,67},{67,3},{4,68},{68... | collective-permute-start | bytes 3145736 | tf_op jit(solution)/shard_map/ppermute | solution.py:21
  37.7 18.6 %collective-permute-start.7 = (bf16[512,1024]{1,0:T(8,128)(2,1)}, bf16[512,1024]{1,0:T(8,128)(2,1)}, u32[]{:S(2)}, u32[]{:S(2)}) collective-permute-start(bf16[512,1024]{1,0:T(8,128)(2,1)} %add_convert_fusion.1), channel_id=1, source_target_pairs={{0,128},{32,160},{64,224},{96,192},{128,32},{160,0},{192,64},{224,... | collective-permute-start | bytes 3145736 | tf_op jit(solution)/shard_map/ppermute | solution.py:21
  48.9 13.0 %collective-permute-start.14 = (f32[17,1024]{1,0:T(8,128)S(1)}, f32[17,1024]{1,0:T(8,128)S(1)}, u32[]{:S(2)}, u32[]{:S(2)}) collective-permute-start(f32[17,1024]{1,0:T(8,128)S(1)} %pad_maximum_fusion.5), channel_id=1, source_target_pairs={{0,64},{64,0},{1,65},{65,1},{2,66},{66,2},{3,67},{67,3},{4,68},{68... | collective-permute-start | bytes 208904 | tf_op jit(solution)/shard_map/ppermute | solution.py:21
  58.6 9.3 %collective-permute-start.10 = (bf16[128,1024]{1,0:T(8,128)(2,1)S(1)}, bf16[128,1024]{1,0:T(8,128)(2,1)S(1)}, u32[]{:S(2)}, u32[]{:S(2)}) collective-permute-start(bf16[128,1024]{1,0:T(8,128)(2,1)S(1)} %get-tuple-element.45), channel_id=1, source_target_pairs={{0,3},{1,0},{2,1},{3,2},{4,7},{5,4},{6,5},{7,6},{8,11},{9,8},{10,9... | collective-permute-start | bytes 786440 | tf_op jit(solution)/shard_map/ppermute | solution.py:21
  60.3 14.0 %collective-permute-start.8 = (bf16[128,1024]{1,0:T(8,128)(2,1)S(1)}, bf16[128,1024]{1,0:T(8,128)(2,1)S(1)}, u32[]{:S(2)}, u32[]{:S(2)}) collective-permute-start(bf16[128,1024]{1,0:T(8,128)(2,1)S(1)} %get-tuple-element.44), channel_id=1, source_target_pairs={{0,1},{1,2},{2,3},{3,0},{4,5},{5,6},{6,7},{7,4},{8,9},{9,10},{10,1... | collective-permute-start | bytes 786440 | tf_op jit(solution)/shard_map/ppermute | solution.py:21
  60.7 13.6 %collective-permute-start.9 = (bf16[128,1024]{1,0:T(8,128)(2,1)S(1)}, bf16[128,1024]{1,0:T(8,128)(2,1)S(1)}, u32[]{:S(2)}, u32[]{:S(2)}) collective-permute-start(bf16[128,1024]{1,0:T(8,128)(2,1)S(1)} %get-tuple-element.46), channel_id=1, source_target_pairs={{0,2},{1,3},{2,0},{3,1},{4,6},{5,7},{6,4},{7,5},{8,10},{9,11},{10,... | collective-permute-start | bytes 786440 | tf_op jit(solution)/shard_map/ppermute | solution.py:21
  61.9 23.5 %collective-permute-start.15 = (f32[17,1024]{1,0:T(8,128)S(1)}, f32[17,1024]{1,0:T(8,128)S(1)}, u32[]{:S(2)}, u32[]{:S(2)}) collective-permute-start(f32[17,1024]{1,0:T(8,128)S(1)} %fusion.200), channel_id=1, source_target_pairs={{0,128},{128,0},{1,129},{129,1},{2,130},{130,2},{3,131},{131,3},{4... | collective-permute-start | bytes 208904 | tf_op jit(solution)/shard_map/ppermute | solution.py:21
  75.2 21.3 %all-to-all-start = ((bf16[16,8,1024]{2,1,0:T(8,128)(2,1)}), bf16[16,8,1024]{2,1,0:T(8,128)(2,1)S(1)}, u32[]{:S(2)}, u32[]{:S(2)}) async-start(bf16[16,8,1024]{2,1,0:T(8,128)(2,1)} %fusion.63), calls=%async_computation | async-start | bytes 524288 | tf_op jit(solution)/shard_map/all_to_all | solution.py:78
  85.4 6.0 %collective-permute-start.16 = (f32[17,1024]{1,0:T(8,128)S(1)}, f32[17,1024]{1,0:T(8,128)S(1)}, u32[]{:S(2)}, u32[]{:S(2)}) collective-permute-start(f32[17,1024]{1,0:T(8,128)S(1)} %add.396), channel_id=1, source_target_pairs={{0,160},{32,128},{128,32},{160,0},{1,161},{33,129},{129,33},{161,1... | collective-permute-start | bytes 208904 | tf_op jit(solution)/shard_map/ppermute | solution.py:21
  91.4 4.7 %collective-permute-start.17 = (f32[17,1024]{1,0:T(8,128)S(1)}, f32[17,1024]{1,0:T(8,128)S(1)}, u32[]{:S(2)}, u32[]{:S(2)}) collective-permute-start(f32[17,1024]{1,0:T(8,128)S(1)} %add.397), channel_id=1, source_target_pairs={{0,1},{1,0},{2,3},{3,2},{4,5},{5,4},{6,7},{7,6},{8,9},{9,8},{10,11... | collective-permute-start | bytes 208904 | tf_op jit(solution)/shard_map/ppermute | solution.py:21
  96.2 11.1 %collective-permute-start.18 = (f32[17,1024]{1,0:T(8,128)S(1)}, f32[17,1024]{1,0:T(8,128)S(1)}, u32[]{:S(2)}, u32[]{:S(2)}) collective-permute-start(f32[17,1024]{1,0:T(8,128)S(1)} %add.398), channel_id=1, source_target_pairs={{0,3},{1,2},{2,1},{3,0},{4,7},{5,6},{6,5},{7,4},{8,11},{9,10},{10,... | collective-permute-start | bytes 208904 | tf_op jit(solution)/shard_map/ppermute | solution.py:21
  97.3 27.4 %all-to-all-start.1 = ((bf16[16,8,1024]{2,1,0:T(8,128)(2,1)}), bf16[16,8,1024]{2,1,0:T(8,128)(2,1)S(1)}, u32[]{:S(2)}, u32[]{:S(2)}) async-start(bf16[16,8,1024]{2,1,0:T(8,128)(2,1)} %broadcast_in_dim.107), calls=%async_computation.1 | async-start | bytes 524288 | tf_op jit(solution)/shard_map/all_to_all | solution.py:80
  107.2 7.2 %collective-permute-start.19 = (f32[17,1024]{1,0:T(8,128)S(1)}, f32[17,1024]{1,0:T(8,128)S(1)}, u32[]{:S(2)}, u32[]{:S(2)}) collective-permute-start(f32[17,1024]{1,0:T(8,128)S(1)} %add.399), channel_id=1, source_target_pairs={{0,4},{4,0},{8,12},{12,8},{16,20},{20,16},{24,28},{28,24},{1,5},{5... | collective-permute-start | bytes 208904 | tf_op jit(solution)/shard_map/ppermute | solution.py:21
  114.4 7.1 %collective-permute-start.20 = (f32[17,1024]{1,0:T(8,128)S(1)}, f32[17,1024]{1,0:T(8,128)S(1)}, u32[]{:S(2)}, u32[]{:S(2)}) collective-permute-start(f32[17,1024]{1,0:T(8,128)S(1)} %add.400), channel_id=1, source_target_pairs={{0,8},{4,12},{8,0},{12,4},{16,24},{20,28},{24,16},{28,20},{1,9},{5... | collective-permute-start | bytes 208904 | tf_op jit(solution)/shard_map/ppermute | solution.py:21
  121.5 8.2 %collective-permute-start.21 = (f32[17,1024]{1,0:T(8,128)S(1)}, f32[17,1024]{1,0:T(8,128)S(1)}, u32[]{:S(2)}, u32[]{:S(2)}) collective-permute-start(f32[17,1024]{1,0:T(8,128)S(1)} %add.401), channel_id=1, source_target_pairs={{0,28},{4,24},{8,20},{12,16},{16,12},{20,8},{24,4},{28,0},{1,29},{... | collective-permute-start | bytes 208904 | tf_op jit(solution)/shard_map/ppermute | solution.py:21
  124.7 7.9 %collective-permute-start.11 = (bf16[128,1024]{1,0:T(8,128)(2,1)S(1)}, bf16[128,1024]{1,0:T(8,128)(2,1)S(1)}, u32[]{:S(2)}, u32[]{:S(2)}) collective-permute-start(bf16[128,1024]{1,0:T(8,128)(2,1)S(1)} %bitcast.79), channel_id=1, source_target_pairs={{0,1},{1,2},{2,3},{3,0},{4,5},{5,6},{6,7},{7,4},{8,9},{9,10},{10,1... | collective-permute-start | bytes 786440 | tf_op jit(solution)/shard_map/ppermute | solution.py:21
  124.9 11.1 %collective-permute-start.12 = (bf16[128,1024]{1,0:T(8,128)(2,1)S(1)}, bf16[128,1024]{1,0:T(8,128)(2,1)S(1)}, u32[]{:S(2)}, u32[]{:S(2)}) collective-permute-start(bf16[128,1024]{1,0:T(8,128)(2,1)S(1)} %bitcast.80), channel_id=1, source_target_pairs={{0,2},{1,3},{2,0},{3,1},{4,6},{5,7},{6,4},{7,5},{8,10},{9,11},{10,... | collective-permute-start | bytes 786440 | tf_op jit(solution)/shard_map/ppermute | solution.py:21
  128.9 7.2 %collective-permute-start.13 = (bf16[128,1024]{1,0:T(8,128)(2,1)S(1)}, bf16[128,1024]{1,0:T(8,128)(2,1)S(1)}, u32[]{:S(2)}, u32[]{:S(2)}) collective-permute-start(bf16[128,1024]{1,0:T(8,128)(2,1)S(1)} %bitcast.81), channel_id=1, source_target_pairs={{0,3},{1,0},{2,1},{3,2},{4,7},{5,4},{6,5},{7,6},{8,11},{9,8},{10,9... | collective-permute-start | bytes 786440 | tf_op jit(solution)/shard_map/ppermute | solution.py:21
  (15 other events, 116.9 us)

commit v2 on v1

v2 whole, which is shorter than its diff:
```python
import functools
import math

import jax
import jax.numpy as jnp
import numpy as np
from jax import lax
from jax.experimental import pallas as pl
from jax.experimental.pallas import tpu as pltpu
from jax.sharding import Mesh, PartitionSpec as P

AXES = ("xl", "c", "xh", "z", "y")
SIZES = (2, 2, 2, 8, 4)
EDGE = 8
REACH = 3
TAPS = 7
LANES = 128
PACK = 32


def shift(cells, axes, target):
    sizes = [SIZES[AXES.index(axis)] for axis in axes]
    pairs = []
    for place in np.ndindex(*sizes):
        goal = target(*place)
        if goal is not None:
            pairs.append((int(np.ravel_multi_index(place, sizes)), int(np.ravel_multi_index(goal, sizes))))
    return lax.ppermute(cells, axes if len(axes) > 1 else axes[0], pairs)


def swap_core(cells):
    return shift(cells, ("c",), lambda c: (1 - c,))


def side_x(xl, c, xh):
    x = (2 * xh + xl + (1 if c == 0 else 3)) % 4
    return (x % 2, c, x // 2)


def turn_x(xl, xh):
    x = 3 - (2 * xh + xl)
    return (x % 2, x // 2)


def neighbour(step):
    def target(xh, z, y):
        place = (xh * 8 + z) * 4 + y + step
        if not 0 <= place < 64:
            return None
        return (place // 32, place // 4 % 8, place % 4)

    return target


def added(*parts):
    total = parts[0].astype(jnp.float32)
    for part in parts[1:]:
        total = total + part.astype(jnp.float32)
    return total


def low_lanes(shape):
    return lax.broadcasted_iota(jnp.int32, shape, len(shape) - 1) < LANES // 2


def paired(cells):
    whole = cells + pltpu.roll(cells, LANES // 2, 1)
    head = whole.astype(jnp.bfloat16).astype(jnp.float32)
    return jnp.where(low_lanes(cells.shape), head, whole - head)


def thirds(cells):
    head = cells.astype(jnp.bfloat16)
    rest = cells - head.astype(jnp.float32)
    middle = rest.astype(jnp.bfloat16)
    return jnp.concatenate([head, middle, (rest - middle.astype(jnp.float32)).astype(jnp.bfloat16)], axis=0)


def turning(size):
    place = lax.broadcasted_iota(jnp.int32, (size, size), 0) + lax.broadcasted_iota(jnp.int32, (size, size), 1)
    return (place == size - 1).astype(jnp.bfloat16)


def strand_kernel(stacks, w0, w1, w2, w3, ups, taps, hot, out, grads, extra, values, mixes, sums):
    total = stacks.shape[1] // 2
    rows = total - 2 * EDGE
    units = w0.shape[1]
    count = units // LANES

    def project(at, _):
        cols = pl.ds(pl.multiple_of(at * 256, 256), 256)
        acc = jnp.zeros((2 * total, 256), jnp.float32)
        for r, w in enumerate((w0, w1, w2, w3)):
            acc = acc + jnp.dot(stacks[r], w[:, cols], preferred_element_type=jnp.float32)
        values[:, cols] = acc.astype(jnp.bfloat16).astype(jnp.float32)
        return 0

    lax.fori_loop(0, units // 256, project, 0)
    sums[...] = jnp.zeros(sums.shape, jnp.float32)
    turn = turning(LANES)

    def work(at, _):
        outs = []
        for way in range(2):
            block = at if way == 0 else count - 1 - at
            cols = pl.ds(pl.multiple_of(block * LANES, LANES), LANES)
            base = way * total
            places = [base + EDGE + (tap - REACH if way == 0 else REACH - tap) for tap in range(TAPS)]
            linear = values[base : base + total, cols]
            logistic = jax.nn.sigmoid(linear)
            gating = linear * logistic
            up = ups[base : base + total, cols].astype(jnp.float32)
            grad_mix = up * gating
            mixes[way] = grad_mix
            mid = slice(EDGE, EDGE + rows)
            linear, logistic, gating, up, grad_mix = [
                cells[mid] for cells in (linear, logistic, gating, up, grad_mix)
            ]
            mixing = jnp.zeros((rows, LANES), jnp.float32)
            for tap in range(TAPS):
                moved = values[places[tap] : places[tap] + rows, cols]
                mixing = mixing + taps[tap : tap + 1, cols] * moved
                sums[tap : tap + 1, cols] += jnp.sum(grad_mix * moved, axis=0, keepdims=True)
            outs.append(mixing * gating)
            acc = up * mixing * logistic * (1.0 + linear * (1.0 - logistic))
            for tap in range(TAPS):
                lower = 2 * EDGE - places[tap] + base
                acc = acc + taps[tap : tap + 1, cols] * mixes[way, lower : lower + rows]
            grads[way * rows : (way + 1) * rows, cols] = acc.astype(jnp.bfloat16)
        turned = jnp.dot(outs[1].astype(jnp.bfloat16), turn, preferred_element_type=jnp.float32)
        out[:, pl.ds(pl.multiple_of(at * LANES, LANES), LANES)] = (outs[0] + turned).astype(jnp.bfloat16)
        return 0

    lax.fori_loop(0, count, work, 0)
    by_token = [
        jnp.dot(hot[...], grads[way * rows : (way + 1) * rows], preferred_element_type=jnp.float32)
        for way in range(2)
    ]
    for at in range(count):
        cols = slice(at * LANES, (at + 1) * LANES)
        pack = jnp.concatenate(
            [sums[:, cols], by_token[0][:8, cols], by_token[1][:8, cols], jnp.zeros((8, LANES), jnp.float32)], axis=0
        )
        head = pack.astype(jnp.bfloat16).astype(jnp.float32)
        rest = pack - head
        low = low_lanes(pack.shape)
        first = jnp.where(low, head, pltpu.roll(rest, LANES // 2, 1))
        second = jnp.where(low, pltpu.roll(head, LANES // 2, 1), rest)
        extra[at * PACK : (at + 1) * PACK] = first.astype(jnp.bfloat16)
        extra[(count + at) * PACK : (count + at + 1) * PACK] = second.astype(jnp.bfloat16)


def product_kernel(rows, grads, extra, out):
    units = grads.shape[1]

    def step(at, _):
        cols = pl.ds(pl.multiple_of(at * 256, 256), 256)
        out[:, cols] = jnp.dot(rows[...], grads[:, cols], preferred_element_type=jnp.float32).astype(jnp.bfloat16)
        return 0

    lax.fori_loop(0, units // 256, step, 0)
    out[:, units:] = extra[...]


def merge_kernel(*refs):
    parts, out = refs[:-1], refs[-1]
    units = out.shape[1] - LANES
    size = 32

    def step(at, _):
        place = pl.ds(pl.multiple_of(at * size, size), size)
        wide = [part for part in parts if part.shape[1] > units]
        plain = [part for part in parts if part.shape[1] == units]
        packed = added(*[part[place, units:] for part in wide])
        out[place, units:] = paired(packed).astype(jnp.bfloat16)
        if len(plain) == 2:
            wide = wide[1:]
        out[place, :units] = added(*[part[place, :units] for part in wide + plain]).astype(jnp.bfloat16)
        return 0

    lax.fori_loop(0, out.shape[0] // size, step, 0)


def piece_kernel(parts, out):
    units = out.shape[1] - LANES
    total = parts[0].astype(jnp.float32)
    for at in range(1, parts.shape[0]):
        total = total + parts[at].astype(jnp.float32)
    out[:, :units] = total[:, :units].astype(jnp.bfloat16)
    out[:, units:] = paired(total[:, units:]).astype(jnp.bfloat16)


def place_kernel(place, q0, q1, q2, q3, out, *, factor):
    rows = q0.shape[0]
    for step, part in enumerate((q0, q1, q2, q3)):
        start = pl.multiple_of((place[0] + 4 - step) % 4 * rows, rows)
        out[pl.ds(start, rows)] = part[...].astype(jnp.float32) * factor


def small_kernel(place, q0, q1, q2, q3, w0, w1, w2, w3, taps_out, table_out, packed, sums, *, factor):
    rows = q0.shape[0]
    for step, part in enumerate((q0, q1, q2, q3)):
        start = pl.multiple_of((place[0] + 4 - step) % 4 * rows, rows)
        packed[pl.ds(start, rows)] = part[...].astype(jnp.float32)
    cells = packed[...]
    whole = cells + pltpu.roll(cells, LANES // 2, 1)
    half = whole.shape[0] // 2
    whole = jnp.where(low_lanes((half, LANES)), whole[:half], whole[half:]) * factor
    count = half // PACK
    for at in range(count):
        cols = slice(at * LANES, (at + 1) * LANES)
        taps_out[:, cols] = whole[at * PACK : at * PACK + TAPS]
        sums[:, cols] = whole[at * PACK + 8 : at * PACK + 24]
    split = thirds(sums[...])
    dims = (((1,), (1,)), ((), ()))
    width = w0.shape[0]
    turn = turning(width)
    backs = []
    for w in (w0, w1, w2, w3):
        back = lax.dot_general(split, w[...], dims, preferred_element_type=jnp.float32)
        backs.append(back[:16] + back[16:32] + back[32:])
    for r in range(4):
        turned = jnp.dot(thirds(backs[r ^ 3][8:]), turn, preferred_element_type=jnp.float32)
        turned = turned[:8] + turned[8:16] + turned[16:]
        start = pl.multiple_of((place[1] ^ r) * width, width)
        table_out[:, pl.ds(start, width)] = (backs[r][:8] + turned)[: table_out.shape[0]]


def call(kernel, outs, *args, scratch=(), scalar=False):
    inside = pl.BlockSpec(memory_space=pltpu.VMEM)
    specs = [inside] * len(args)
    if scalar:
        specs[0] = pl.BlockSpec(memory_space=pltpu.SMEM)
    return pl.pallas_call(
        kernel,
        out_shape=outs,
        in_specs=specs,
        out_specs=jax.tree.map(lambda _: inside, outs),
        scratch_shapes=list(scratch),
        compiler_params=pltpu.CompilerParams(vmem_limit_bytes=48 * 2**20),
    )(*args)


def array(shape, dtype=jnp.bfloat16):
    return jax.ShapeDtypeStruct(shape, dtype)


def merged(*parts):
    rows = parts[0].shape[0]
    return call(merge_kernel, array((rows, max(part.shape[1] for part in parts))), *parts)


def reduce_rows(own, mate, side, side_mate):
    side_sum = merged(side, swap_core(side_mate))
    from_side = shift(side_sum, ("xl", "c", "xh"), side_x)
    block = merged(side_sum, from_side, own, swap_core(mate))
    y = lax.axis_index("y")
    rows = block.shape[0] // 4
    units = own.shape[1]
    parts = [lax.dynamic_slice_in_dim(block, y * rows, rows, 0)]
    for step in (1, 2, 3):
        chunk = lax.dynamic_slice_in_dim(block, (y + step) % 4 * rows, rows, 0)
        parts.append(shift(chunk, ("y",), lambda a: ((a + step) % 4,)))
    quarter = merged(*parts)
    pieces = quarter.reshape(16, rows // 16, -1)
    pieces = lax.all_to_all(pieces, ("xh", "z"), split_axis=0, concat_axis=0, tiled=True)
    piece = call(piece_kernel, array(pieces.shape[1:]), pieces)
    pieces = lax.all_to_all(
        jnp.broadcast_to(piece[None], pieces.shape), ("xh", "z"), split_axis=0, concat_axis=0, tiled=True
    )
    quarter = pieces.reshape(rows, -1)
    large = quarter[:, :units]
    small = quarter[:, units:]
    large = [large] + [shift(large, ("y",), lambda a: ((a + step) % 4,)) for step in (1, 2, 3)]
    small = [small] + [shift(small, ("y",), lambda a: ((a + step) % 4,)) for step in (1, 2, 3)]
    return large, small


def local(hidden, tokens, embedding, weight, kernel, cotangent):
    window = hidden[0]
    token_codes = tokens[0]
    upstream = cotangent[0]
    rows, features = window.shape
    units = weight.shape[1]
    factor = 1.0 / math.sqrt(rows * 256)
    width = features // 4
    me = 2 * lax.axis_index("xl") + lax.axis_index("c")
    blocks = [me ^ r for r in range(4)]
    weights = [weight, swap_core(weight), shift(weight, ("xl", "c", "xh"), side_x)]
    weights.append(swap_core(weights[2]))

    looked = jnp.zeros((rows, features), jnp.float32)
    for symbol in range(embedding.shape[0]):
        looked = looked + jnp.where((token_codes == symbol)[:, None], embedding[symbol][None, :], 0.0)
    stream = (window.astype(jnp.float32) + looked).astype(jnp.bfloat16)
    both = jnp.concatenate([stream, upstream], axis=1)
    before = shift(both[rows - EDGE :], ("xh", "z", "y"), neighbour(1))
    after = shift(both[:EDGE], ("xh", "z", "y"), neighbour(-1))
    wide = jnp.concatenate([before, both, after], axis=0)
    total = rows + 2 * EDGE

    def exchange(size):
        return (
            lax.broadcasted_iota(jnp.int32, (size, size), 0) + lax.broadcasted_iota(jnp.int32, (size, size), 1)
            == size - 1
        ).astype(jnp.bfloat16)

    def flipped(cells):
        size = 256
        count = cells.shape[1] // size
        turn = exchange(size)
        return jnp.concatenate(
            [
                jnp.dot(
                    cells[:, (count - 1 - at) * size : (count - at) * size],
                    turn,
                    preferred_element_type=jnp.float32,
                ).astype(jnp.bfloat16)
                for at in range(count)
            ],
            axis=1,
        )

    forward = [lax.dynamic_slice_in_dim(wide, at * width, width, 1) for at in blocks]
    reverse = [flipped(forward[r ^ 3]) for r in range(4)]
    stacks = [jnp.concatenate([forward[r], reverse[r]], axis=0) for r in range(4)]
    ups = wide[:, features:]
    ups = jnp.concatenate([ups, flipped(ups)], axis=0)
    hot = (jnp.arange(16, dtype=jnp.int32)[:, None] == token_codes[None, :]).astype(jnp.bfloat16)
    mid = slice(EDGE, EDGE + rows)
    columns = [jnp.concatenate([forward[r][mid], reverse[r][mid]], axis=0).T for r in range(4)]
    block_result, grad_stack, extra = call(
        strand_kernel,
        (array((rows, units)), array((2 * rows, units)), array((512, LANES))),
        jnp.stack(stacks),
        *weights,
        ups,
        kernel,
        hot,
        scratch=(
            pltpu.VMEM((2 * total, units), jnp.float32),
            pltpu.VMEM((2, total, LANES), jnp.float32),
            pltpu.VMEM((8, units), jnp.float32),
        ),
    )
    products = [
        jnp.dot(columns[r], grad_stack, preferred_element_type=jnp.float32).astype(jnp.bfloat16) for r in range(2)
    ]
    for r in (2, 3):
        products.append(call(product_kernel, array((width, units + LANES)), columns[r], grad_stack, extra))
    large, small = reduce_rows(*products)
    place = jnp.stack([lax.axis_index("y"), me]).astype(jnp.int32)
    grad_weight = call(
        functools.partial(place_kernel, factor=factor), array((width, units), jnp.float32), place, *large, scalar=True
    )
    grad_kernel, grad_embedding = call(
        functools.partial(small_kernel, factor=factor),
        (array(kernel.shape, jnp.float32), array(embedding.shape, jnp.float32)),
        place,
        *small,
        *weights,
        scalar=True,
        scratch=(pltpu.VMEM((512, LANES), jnp.float32), pltpu.VMEM((16, units), jnp.float32)),
    )
    backs = [
        lax.dot_general(grad_stack, weights[r], (((1,), (1,)), ((), ())), preferred_element_type=jnp.float32)
        for r in range(4)
    ]
    streams = jnp.stack(
        [backs[r][:rows] + flipped(backs[r ^ 3][rows:].astype(jnp.bfloat16)).astype(jnp.float32) for r in range(4)]
    )
    grad_stream = jnp.concatenate([streams[at ^ me] for at in range(4)], axis=1)
    return (
        block_result[None],
        grad_stream.astype(jnp.bfloat16)[None],
        grad_weight,
        grad_kernel,
        grad_embedding,
    )


def solution(mesh):
    fine = Mesh(mesh.devices.reshape(SIZES), AXES)
    batch = ("xl", "c")
    place = ("xh", "z", "y")
    in_specs = (P(batch, place, None), P(batch, place), P(), P(batch, None), P(), P(batch, place, None))
    out_specs = (P(batch, place, None), P(batch, place, None), P(batch, None), P(), P())
    return jax.shard_map(local, mesh=fine, in_specs=in_specs, out_specs=out_specs, check_vma=False)
```

time: 140 us -> 176 us (1.26)
  Pallas kernels: 0 us -> 20.2 us
  local copies, waits for them, and re-layouts: 7.37 us -> 23.4 us
  matrix products: 14.1 us -> 21.4 us
  starting transfers between devices: 54.8 us -> 49.9 us
  waiting for transfers between devices: 43.8 us -> 40 us
  other arithmetic: 16.4 us -> 18.4 us
    pallas_call x0 -> x9, Pallas kernels: none -> 20.2 us  [call(): pl.pallas_call(kernel, out_shape=outs, in_specs=specs, out_specs=jax.tree...]
    ppermute x22 -> x17, waiting for transfers between devices: 43.8 us -> 25.6 us  [shift(): return lax.ppermute(cells, axes if len(axes) > 1 else axes[0], pairs)]
    dot_general x24 -> x20, matrix products: 4.14 us -> 14.2 us  [flipped(): jnp.dot(cells[:, (count - 1 - at) * size:(count - at) * size], turn, pref...]
    all_to_all x1, waiting for transfers between devices: 0.01 us -> 7.7 us  [reduce_rows(): lax.all_to_all(jnp.broadcast_to(piece[None], pieces.shape), ('xh', 'z'),...]
    dot_general x9 -> x2, matrix products: 7.88 us -> 0.95 us  [local(): jnp.dot(columns[r], grad_stack, preferred_element_type=jnp.float32)]
    all_to_all x1, waiting for transfers between devices: 0.01 us -> 6.75 us  [reduce_rows(): lax.all_to_all(pieces, ('xh', 'z'), split_axis=0, concat_axis=0, tiled=True)]
    another operation x3 -> x5, other arithmetic: 0.23 us -> 6.84 us  [local(): jnp.stack([backs[r][:rows] + flipped(backs[r ^ 3][rows:].astype(jnp.bfloa...]
    convert_element_type x6 -> x1, other arithmetic: 5.87 us -> 0.01 us  [local(): (jnp.arange(16, dtype=jnp.int32)[:, None] == token_codes[None, :]).astype...]
  transfers between devices with their start and end apart: 24 -> 19, of which waited for: 13 -> 8; matrix products, arithmetic and copies ran while one was open for 18% -> 35% of each run, Pallas kernels for 0% -> 3%
where the time goes in v2:
time: 176 us; the launch traced here: 175 us
  starting transfers between devices  49.9 us (28%)
  waiting for transfers between devices  40 us (23%)
  local copies, waits for them, and re-layouts  23.4 us (13%)
  matrix products  21.4 us (12%)
  Pallas kernels  20.2 us (11%)
  other arithmetic  18.4 us (10%)
    ppermute x17, starting transfers between devices, shift(): return lax.ppermute(cells, axes if len(axes) > 1 else axes[0], pairs)  39.7 us
    ppermute x17, waiting for transfers between devices, shift(): return lax.ppermute(cells, axes if len(axes) > 1 else axes[0], pairs)  25.6 us
    pallas_call x9, Pallas kernels, call(): pl.pallas_call(kernel, out_shape=outs, in_specs=specs, out_specs=jax.tree...  20.2 us
    dot_general x20, matrix products, flipped(): jnp.dot(cells[:, (count - 1 - at) * size:(count - at) * size], turn, pref...  14.2 us
    all_to_all x1, waiting for transfers between devices, reduce_rows(): lax.all_to_all(jnp.broadcast_to(piece[None], pieces.shape), ('xh', 'z'),...  7.7 us
    another operation x5, other arithmetic, local(): jnp.stack([backs[r][:rows] + flipped(backs[r ^ 3][rows:].astype(jnp.bfloa...  6.84 us
    all_to_all x1, waiting for transfers between devices, reduce_rows(): lax.all_to_all(pieces, ('xh', 'z'), split_axis=0, concat_axis=0, tiled=True)  6.75 us
    dot_general x4, matrix products, local(): lax.dot_general(grad_stack, weights[r], (((1,), (1,)), ((), ())), preferr...  6.24 us
  transfers between devices with their start and end apart: 19, of which 8 were waited for; matrix products, arithmetic and copies ran while one was open for 35% of the time, Pallas kernels for 3%

profile of v2, /device:TPU:2, one launch (start us, length us, event | category | flops | bytes accessed | tf_op | source)
XLA Modules:
  0.0 174.5 jit_solution(5708205195131057714)
XLA Ops:
  5.5 1.8 %fusion = bf16[128,2048]{0,1:T(8,128)(2,1)S(1)} fusion(bf16[1,128,2048]{1,2,0:T(8,128)(2,1)S(1)} %copy.47, f32[2048]{0:T(1024)S(1)} %bitcast.58, f32[2048]{0:T(1024)S(1)} %bitcast.59, f32[2048]{0:T(1024)S(1)} %bitcast.56, f32[2048]{0:T(1024)S(1)} %bitcast.57, f32[2048]{0:T(1024)S(1)} %bitcast.55, pred[128]{0:T(512)(128)(4,1)S(1)} %get-tuple-element.42, ...), kind=kLoop, calls=%fused_computation.26 | loop fusion | flops 3145728 | bytes 1090176 | tf_op jit(solution)/shard_map/convert_element_type | solution.py:295
  7.3 2.2 %slice_maximum_fusion = (bf16[8,3072]{0,1:T(8,128)(2,1)S(1)}, bf16[8,3072]{0,1:T(8,128)(2,1)}) fusion(bf16[128,1024]{0,1:T(8,128)(2,1)} %bitcast.51, bf16[128,2048]{0,1:T(8,128)(2,1)S(1)} %fusion), kind=kLoop, calls=%fused_computation.28 | loop fusion | flops 196608 | bytes 884736 | tf_op jit(solution)/shard_map/concatenate | solution.py:296
  13.0 5.2 %collective-permute-start = (bf16[8,3072]{1,0:T(8,128)(2,1)}, bf16[8,3072]{1,0:T(8,128)(2,1)}, u32[]{:S(2)}, u32[]{:S(2)}) collective-permute-start(bf16[8,3072]{1,0:T(8,128)(2,1)} %copy.49), channel_id=1, source_target_pairs={{0,1},{1,2},{2,3},{3,4},{4,5},{5,6},{6,7},{7,8},{8,9},{9,10},{10,1... | collective-permute-start | bytes 147464 | tf_op jit(solution)/shard_map/ppermute | solution.py:28
  19.7 2.0 %copy.51 = bf16[8,3072]{0,1:T(8,128)(2,1)} copy(bf16[8,3072]{1,0:T(8,128)(2,1)} %collective-permute-done) | data formatting | bytes 98304 | tf_op jit(solution)/shard_map/ppermute | solution.py:28
  21.6 2.2 %pad_maximum_fusion = bf16[144,3072]{0,1:T(8,128)(2,1)S(1)} fusion(bf16[8,3072]{0,1:T(8,128)(2,1)S(1)} %copy.52, bf16[128,1024]{0,1:T(8,128)(2,1)} %bitcast.52, bf16[128,2048]{0,1:T(8,128)(2,1)S(1)} %fusion, bf16[8,3072]{0,1:T(8,128)(2,1)} %copy.51), kind=kLoop, calls=%fused_computation | loop fusion | flops 3538944 | bytes 1769472 | tf_op jit(solution)/shard_map/concatenate | solution.py:299
  38.8 2.5 %copy.65.stacks = bf16[4,288,512]{2,1,0:T(8,128)(2,1)} copy(bf16[4,288,512]{1,2,0:T(8,128)(2,1)} %pad_maximum_fusion.1) | data formatting | bytes 2359296 | tf_op jit(solution)/shard_map/stack | solution.py:335
  45.2 2.3 %copy.66.ups = bf16[288,1024]{1,0:T(8,128)(2,1)} copy(bf16[288,1024]{0,1:T(8,128)(2,1)} %maximum_maximum_fusion) | data formatting | bytes 1179648 | tf_op jit(solution)/shard_map/concatenate | solution.py:328
  50.3 8.9 %shard_map.101 = (bf16[128,1024]{1,0:T(8,128)(2,1)}, bf16[256,1024]{1,0:T(8,128)(2,1)S(1)}, bf16[512,128]{1,0:T(8,128)(2,1)S(1)}) custom-call(bf16[4,288,512]{2,1,0:T(8,128)(2,1)} %copy.65.stacks, bf16[512,1024]{1,0:T(8,128)(2,1)S(1)} %copy-done, bf16[512,1024]{1,0:T(8,128)(2,1)S(1)} %collective-permute-done.2.w1, ...), custom_call_target="tpu_custom_call" | custom-call | tf_op jit(solution)/shard_map/pallas_call | solution.py:234
  67.1 16.3 %collective-permute-start.6 = (bf16[512,1152]{1,0:T(8,128)(2,1)S(1)}, bf16[512,1152]{1,0:T(8,128)(2,1)S(1)}, u32[]{:S(2)}, u32[]{:S(2)}) collective-permute-start(bf16[512,1152]{1,0:T(8,128)(2,1)S(1)} %shard_map.104.refs_0_), channel_id=1, source_target_pairs={{0,128},{32,160},{64,224},{96,192},{128,32},{160,0},{192,64},{224,... | collective-permute-start | bytes 3538952 | tf_op jit(solution)/shard_map/ppermute | solution.py:28
  86.8 2.4 %fusion.115 = (bf16[256,512]{1,0:T(8,128)(2,1)}, f32[256,512]{1,0:T(8,128)S(1)}) fusion(bf16[256,1024]{1,0:T(8,128)(2,1)S(1)} %get-tuple-element.11.grads, bf16[512,1024]{1,0:T(8,128)(2,1)} %collective-permute-done.4.w3), kind=kOutput, calls=%fused_computation.170 | convolution fusion | flops 268566528 | bytes 2359296 | tf_op jit(solution)/shard_map/dot_general | solution.py:366
  89.2 8.0 %collective-permute-done.6.refs_1_ = bf16[512,1152]{1,0:T(8,128)(2,1)S(1)} collective-permute-done((bf16[512,1152]{1,0:T(8,128)(2,1)S(1)}, bf16[512,1152]{1,0:T(8,128)(2,1)S(1)}, u32[]{:S(2)}, u32[]{:S(2)}) %collective-permute-start.6) | collective-permute-done | bytes 1179680 | tf_op jit(solution)/shard_map/ppermute | solution.py:28
  99.1 3.1 %collective-permute-start.10 = (bf16[128,1152]{1,0:T(8,128)(2,1)S(1)}, bf16[128,1152]{1,0:T(8,128)(2,1)S(1)}, u32[]{:S(2)}, u32[]{:S(2)}) collective-permute-start(bf16[128,1152]{1,0:T(8,128)(2,1)S(1)} %get-tuple-element.23), channel_id=1, source_target_pairs={{0,3},{1,0},{2,1},{3,2},{4,7},{5,4},{6,5},{7,6},{8,11},{9,8},{10,9... | collective-permute-start | bytes 884744 | tf_op jit(solution)/shard_map/ppermute | solution.py:28
  103.7 11.7 %collective-permute-done.8.refs_1_ = bf16[128,1152]{1,0:T(8,128)(2,1)S(1)} collective-permute-done((bf16[128,1152]{1,0:T(8,128)(2,1)S(1)}, bf16[128,1152]{1,0:T(8,128)(2,1)S(1)}, u32[]{:S(2)}, u32[]{:S(2)}) %collective-permute-start.8) | collective-permute-done | bytes 294944 | tf_op jit(solution)/shard_map/ppermute | solution.py:28
  117.2 5.5 %all-to-all-start = ((bf16[16,8,1152]{2,1,0:T(8,128)(2,1)}), bf16[16,8,1152]{2,1,0:T(8,128)(2,1)S(1)}, u32[]{:S(2)}, u32[]{:S(2)}) async-start(bf16[16,8,1152]{2,1,0:T(8,128)(2,1)} %bitcast.50), calls=%async_computation | async-start | bytes 589824 | tf_op jit(solution)/shard_map/all_to_all | solution.py:266
  127.6 6.7 %all-to-all-done.parts = bf16[16,8,1152]{2,1,0:T(8,128)(2,1)S(1)} async-done(((bf16[16,8,1152]{2,1,0:T(8,128)(2,1)}), bf16[16,8,1152]{2,1,0:T(8,128)(2,1)S(1)}, u32[]{:S(2)}, u32[]{:S(2)}) %all-to-all-start) | async-done | bytes 294944 | tf_op jit(solution)/shard_map/all_to_all | solution.py:266
  135.2 4.7 %all-to-all-start.1 = ((bf16[16,8,1152]{2,1,0:T(8,128)(2,1)}), bf16[16,8,1152]{2,1,0:T(8,128)(2,1)S(1)}, u32[]{:S(2)}, u32[]{:S(2)}) async-start(bf16[16,8,1152]{2,1,0:T(8,128)(2,1)} %broadcast_in_dim.107), calls=%async_computation.1 | async-start | bytes 589824 | tf_op jit(solution)/shard_map/all_to_all | solution.py:268
  141.9 1.9 %pad_maximum_fusion.2 = bf16[4,128,512]{2,1,0:T(8,128)(2,1)} fusion(bf16[1,128,512]{2,1,0:T(8,128)(2,1)} %fusion.29, bf16[1,128,512]{2,1,0:T(8,128)(2,1)} %fusion.30, bf16[1,128,512]{2,1,0:T(8,128)(2,1)} %fusion.31, bf16[1,128,512]{2,1,0:T(8,128)(2,1)S(1)} %fusion.32), kind=kLoop, calls=%fused_computation.24 | loop fusion | flops 786432 | bytes 1048576 | tf_op jit(solution)/shard_map/stack | solution.py:369
  143.8 7.7 %all-to-all-done.1 = bf16[16,8,1152]{2,1,0:T(8,128)(2,1)S(1)} async-done(((bf16[16,8,1152]{2,1,0:T(8,128)(2,1)}), bf16[16,8,1152]{2,1,0:T(8,128)(2,1)S(1)}, u32[]{:S(2)}, u32[]{:S(2)}) %all-to-all-start.1) | async-done | bytes 294944 | tf_op jit(solution)/shard_map/all_to_all | solution.py:268
  152.9 3.2 %collective-permute-start.12 = (bf16[128,1024]{1,0:T(8,128)(2,1)S(1)}, bf16[128,1024]{1,0:T(8,128)(2,1)S(1)}, u32[]{:S(2)}, u32[]{:S(2)}) collective-permute-start(bf16[128,1024]{1,0:T(8,128)(2,1)S(1)} %slice.207.q0), channel_id=1, source_target_pairs={{0,2},{1,3},{2,0},{3,1},{4,6},{5,7},{6,4},{7,5},{8,10},{9,11},{10,... | collective-permute-start | bytes 786440 | tf_op jit(solution)/shard_map/ppermute | solution.py:28
  156.1 2.0 %collective-permute-start.14 = (bf16[128,128]{1,0:T(8,128)(2,1)S(1)}, bf16[128,128]{1,0:T(8,128)(2,1)S(1)}, u32[]{:S(2)}, u32[]{:S(2)}) collective-permute-start(bf16[128,128]{1,0:T(8,128)(2,1)S(1)} %slice.208.q0), channel_id=1, source_target_pairs={{0,1},{1,2},{2,3},{3,0},{4,5},{5,6},{6,7},{7,4},{8,9},{9,10},{10,1... | collective-permute-start | bytes 98312 | tf_op jit(solution)/shard_map/ppermute | solution.py:28
  159.7 3.6 %collective-permute-done.14.q1 = bf16[128,128]{1,0:T(8,128)(2,1)S(1)} collective-permute-done((bf16[128,128]{1,0:T(8,128)(2,1)S(1)}, bf16[128,128]{1,0:T(8,128)(2,1)S(1)}, u32[]{:S(2)}, u32[]{:S(2)}) %collective-permute-start.14) | collective-permute-done | bytes 32800 | tf_op jit(solution)/shard_map/ppermute | solution.py:28
  163.2 4.1 %collective-permute-start.16 = (bf16[128,128]{1,0:T(8,128)(2,1)S(1)}, bf16[128,128]{1,0:T(8,128)(2,1)S(1)}, u32[]{:S(2)}, u32[]{:S(2)}) collective-permute-start(bf16[128,128]{1,0:T(8,128)(2,1)S(1)} %slice.208.q0), channel_id=1, source_target_pairs={{0,3},{1,0},{2,1},{3,2},{4,7},{5,4},{6,5},{7,6},{8,11},{9,8},{10,9... | collective-permute-start | bytes 98312 | tf_op jit(solution)/shard_map/ppermute | solution.py:28
  168.9 3.6 %shard_map.109 = (f32[7,1024]{1,0:T(8,128)}, f32[5,2048]{1,0:T(8,128)}) custom-call(s32[2]{0:T(128)S(1)} %pad_add_fusion.place, bf16[128,128]{1,0:T(8,128)(2,1)S(1)} %slice.208.q0, bf16[128,128]{1,0:T(8,128)(2,1)S(1)} %collective-permute-done.14.q1, bf16[128,128]{1,0:T(8,128)(2,1)S(1)} %collective-permute-done.15.q2, ...), custom_call_target="tpu_custom_call" | custom-call | tf_op jit(solution)/shard_map/pallas_call | solution.py:234
  172.5 2.0 %shard_map.108 = f32[512,1024]{1,0:T(8,128)} custom-call(s32[2]{0:T(128)S(1)} %pad_add_fusion.place, bf16[128,1024]{1,0:T(8,128)(2,1)S(1)} %slice.207.q0, bf16[128,1024]{1,0:T(8,128)(2,1)S(1)} %collective-permute-done.11.q1, bf16[128,1024]{1,0:T(8,128)(2,1)S(1)} %collective-permute-done.12.q2, bf16[128,1024]{1,0:T(8,128)(2,1)S(1)} %collective-permute-done.13.q3), custom_call_target="tpu_custom_call" | custom-call | tf_op jit(solution)/shard_map/pallas_call | solution.py:234
  (137 shorter events, 60.0 us)
Async XLA Ops:
  0.7 49.6 %collective-permute-start.2 = (bf16[512,1024]{1,0:T(8,128)(2,1)}, bf16[512,1024]{1,0:T(8,128)(2,1)S(1)}, u32[]{:S(2)}, u32[]{:S(2)}) collective-permute-start(bf16[512,1024]{1,0:T(8,128)(2,1)} %w0.3), channel_id=1, source_target_pairs={{0,64},{64,0},{1,65},{65,1},{2,66},{66,2},{3,67},{67,3},{4,68},{68... | collective-permute-start | bytes 3145736 | tf_op jit(solution)/shard_map/ppermute | solution.py:28
  0.8 36.4 %collective-permute-start.3 = (bf16[512,1024]{1,0:T(8,128)(2,1)}, bf16[512,1024]{1,0:T(8,128)(2,1)S(1)}, u32[]{:S(2)}, u32[]{:S(2)}) collective-permute-start(bf16[512,1024]{1,0:T(8,128)(2,1)} %w0.3), channel_id=1, source_target_pairs={{0,128},{32,160},{64,224},{96,192},{128,32},{160,0},{192,64},{224,... | collective-permute-start | bytes 3145736 | tf_op jit(solution)/shard_map/ppermute | solution.py:28
  10.9 7.4 %collective-permute-start.1 = (bf16[8,3072]{1,0:T(8,128)(2,1)S(1)}, bf16[8,3072]{1,0:T(8,128)(2,1)S(1)}, u32[]{:S(2)}, u32[]{:S(2)}) collective-permute-start(bf16[8,3072]{1,0:T(8,128)(2,1)S(1)} %copy.50), channel_id=1, source_target_pairs={{1,0},{2,1},{3,2},{4,3},{5,4},{6,5},{7,6},{8,7},{9,8},{10,9},{11,1... | collective-permute-start | bytes 147464 | tf_op jit(solution)/shard_map/ppermute | solution.py:28
  13.0 6.6 %collective-permute-start = (bf16[8,3072]{1,0:T(8,128)(2,1)}, bf16[8,3072]{1,0:T(8,128)(2,1)}, u32[]{:S(2)}, u32[]{:S(2)}) collective-permute-start(bf16[8,3072]{1,0:T(8,128)(2,1)} %copy.49), channel_id=1, source_target_pairs={{0,1},{1,2},{2,3},{3,4},{4,5},{5,6},{6,7},{7,8},{8,9},{9,10},{10,1... | collective-permute-start | bytes 147464 | tf_op jit(solution)/shard_map/ppermute | solution.py:28
  26.2 9.0 %copy-start.6 = (bf16[144,256]{0,1:T(8,128)(2,1)}, bf16[144,256]{0,1:T(8,128)(2,1)S(1)}, u32[]{:S(2)}) copy-start(bf16[144,256]{0,1:T(8,128)(2,1)S(1)} %copy.57) | copy-start | bytes 221188
  27.6 7.7 %copy-start.7 = (bf16[144,256]{0,1:T(8,128)(2,1)}, bf16[144,256]{0,1:T(8,128)(2,1)S(1)}, u32[]{:S(2)}) copy-start(bf16[144,256]{0,1:T(8,128)(2,1)S(1)} %copy.59) | copy-start | bytes 221188
  37.1 13.1 %collective-permute-start.4 = (bf16[512,1024]{1,0:T(8,128)(2,1)S(1)}, bf16[512,1024]{1,0:T(8,128)(2,1)}, u32[]{:S(2)}, u32[]{:S(2)}) collective-permute-start(bf16[512,1024]{1,0:T(8,128)(2,1)S(1)} %collective-permute-done.3.w2), channel_id=1, source_target_pairs={{0,64},{64,0},{1,65},{65,1},{2,66},{66,2},{3,67},{67,3},{4,68},{68... | collective-permute-start | bytes 3145736 | tf_op jit(solution)/shard_map/ppermute | solution.py:28
  61.2 4.4 %collective-permute-start.5 = (bf16[512,1152]{1,0:T(8,128)(2,1)S(1)}, bf16[512,1152]{1,0:T(8,128)(2,1)S(1)}, u32[]{:S(2)}, u32[]{:S(2)}) collective-permute-start(bf16[512,1152]{1,0:T(8,128)(2,1)S(1)} %shard_map.103), channel_id=1, source_target_pairs={{0,64},{64,0},{1,65},{65,1},{2,66},{66,2},{3,67},{67,3},{4,68},{68... | collective-permute-start | bytes 3538952 | tf_op jit(solution)/shard_map/ppermute | solution.py:28
  62.2 27.0 %collective-permute-start.7 = (bf16[512,1024]{1,0:T(8,128)(2,1)S(1)}, bf16[512,1024]{1,0:T(8,128)(2,1)S(1)}, u32[]{:S(2)}, u32[]{:S(2)}) collective-permute-start(bf16[512,1024]{1,0:T(8,128)(2,1)S(1)} %convolution_convert_fusion), channel_id=1, source_target_pairs={{0,64},{64,0},{1,65},{65,1},{2,66},{66,2},{3,67},{67,3},{4,68},{68... | collective-permute-start | bytes 3145736 | tf_op jit(solution)/shard_map/ppermute | solution.py:28
  67.1 19.2 %copy-start.10 = (bf16[144,256]{0,1:T(8,128)(2,1)S(1)}, bf16[144,256]{0,1:T(8,128)(2,1)}, u32[]{:S(2)}) copy-start(bf16[144,256]{0,1:T(8,128)(2,1)} %copy.54) | copy-start | bytes 221188
  67.1 19.2 %copy-start.12 = (bf16[144,256]{0,1:T(8,128)(2,1)S(1)}, bf16[144,256]{0,1:T(8,128)(2,1)}, u32[]{:S(2)}) copy-start(bf16[144,256]{0,1:T(8,128)(2,1)} %copy.53) | copy-start | bytes 221188
  67.1 30.0 %collective-permute-start.6 = (bf16[512,1152]{1,0:T(8,128)(2,1)S(1)}, bf16[512,1152]{1,0:T(8,128)(2,1)S(1)}, u32[]{:S(2)}, u32[]{:S(2)}) collective-permute-start(bf16[512,1152]{1,0:T(8,128)(2,1)S(1)} %shard_map.104.refs_0_), channel_id=1, source_target_pairs={{0,128},{32,160},{64,224},{96,192},{128,32},{160,0},{192,64},{224,... | collective-permute-start | bytes 3538952 | tf_op jit(solution)/shard_map/ppermute | solution.py:28
  98.9 16.5 %collective-permute-start.8 = (bf16[128,1152]{1,0:T(8,128)(2,1)S(1)}, bf16[128,1152]{1,0:T(8,128)(2,1)S(1)}, u32[]{:S(2)}, u32[]{:S(2)}) collective-permute-start(bf16[128,1152]{1,0:T(8,128)(2,1)S(1)} %get-tuple-element.25), channel_id=1, source_target_pairs={{0,1},{1,2},{2,3},{3,0},{4,5},{5,6},{6,7},{7,4},{8,9},{9,10},{10,1... | collective-permute-start | bytes 884744 | tf_op jit(solution)/shard_map/ppermute | solution.py:28
  99.0 16.4 %collective-permute-start.9 = (bf16[128,1152]{1,0:T(8,128)(2,1)S(1)}, bf16[128,1152]{1,0:T(8,128)(2,1)S(1)}, u32[]{:S(2)}, u32[]{:S(2)}) collective-permute-start(bf16[128,1152]{1,0:T(8,128)(2,1)S(1)} %get-tuple-element.24), channel_id=1, source_target_pairs={{0,2},{1,3},{2,0},{3,1},{4,6},{5,7},{6,4},{7,5},{8,10},{9,11},{10,... | collective-permute-start | bytes 884744 | tf_op jit(solution)/shard_map/ppermute | solution.py:28
  99.1 16.9 %collective-permute-start.10 = (bf16[128,1152]{1,0:T(8,128)(2,1)S(1)}, bf16[128,1152]{1,0:T(8,128)(2,1)S(1)}, u32[]{:S(2)}, u32[]{:S(2)}) collective-permute-start(bf16[128,1152]{1,0:T(8,128)(2,1)S(1)} %get-tuple-element.23), channel_id=1, source_target_pairs={{0,3},{1,0},{2,1},{3,2},{4,7},{5,4},{6,5},{7,6},{8,11},{9,8},{10,9... | collective-permute-start | bytes 884744 | tf_op jit(solution)/shard_map/ppermute | solution.py:28
  117.2 17.2 %all-to-all-start = ((bf16[16,8,1152]{2,1,0:T(8,128)(2,1)}), bf16[16,8,1152]{2,1,0:T(8,128)(2,1)S(1)}, u32[]{:S(2)}, u32[]{:S(2)}) async-start(bf16[16,8,1152]{2,1,0:T(8,128)(2,1)} %bitcast.50), calls=%async_computation | async-start | bytes 589824 | tf_op jit(solution)/shard_map/all_to_all | solution.py:266
  126.0 15.0 %copy-start.17 = (bf16[128,256]{1,0:T(8,128)(2,1)S(1)}, bf16[128,256]{1,0:T(8,128)(2,1)}, u32[]{:S(2)}) copy-start(bf16[128,256]{1,0:T(8,128)(2,1)} %convolution_convert_fusion.20) | copy-start | bytes 196612
  135.2 16.3 %all-to-all-start.1 = ((bf16[16,8,1152]{2,1,0:T(8,128)(2,1)}), bf16[16,8,1152]{2,1,0:T(8,128)(2,1)S(1)}, u32[]{:S(2)}, u32[]{:S(2)}) async-start(bf16[16,8,1152]{2,1,0:T(8,128)(2,1)} %broadcast_in_dim.107), calls=%async_computation.1 | async-start | bytes 589824 | tf_op jit(solution)/shard_map/all_to_all | solution.py:268
  151.6 20.9 %collective-permute-start.11 = (bf16[128,1024]{1,0:T(8,128)(2,1)S(1)}, bf16[128,1024]{1,0:T(8,128)(2,1)S(1)}, u32[]{:S(2)}, u32[]{:S(2)}) collective-permute-start(bf16[128,1024]{1,0:T(8,128)(2,1)S(1)} %slice.207.q0), channel_id=1, source_target_pairs={{0,1},{1,2},{2,3},{3,0},{4,5},{5,6},{6,7},{7,4},{8,9},{9,10},{10,1... | collective-permute-start | bytes 786440 | tf_op jit(solution)/shard_map/ppermute | solution.py:28
  152.9 19.6 %collective-permute-start.12 = (bf16[128,1024]{1,0:T(8,128)(2,1)S(1)}, bf16[128,1024]{1,0:T(8,128)(2,1)S(1)}, u32[]{:S(2)}, u32[]{:S(2)}) collective-permute-start(bf16[128,1024]{1,0:T(8,128)(2,1)S(1)} %slice.207.q0), channel_id=1, source_target_pairs={{0,2},{1,3},{2,0},{3,1},{4,6},{5,7},{6,4},{7,5},{8,10},{9,11},{10,... | collective-permute-start | bytes 786440 | tf_op jit(solution)/shard_map/ppermute | solution.py:28
  156.1 16.4 %collective-permute-start.13 = (bf16[128,1024]{1,0:T(8,128)(2,1)S(1)}, bf16[128,1024]{1,0:T(8,128)(2,1)S(1)}, u32[]{:S(2)}, u32[]{:S(2)}) collective-permute-start(bf16[128,1024]{1,0:T(8,128)(2,1)S(1)} %slice.207.q0), channel_id=1, source_target_pairs={{0,3},{1,0},{2,1},{3,2},{4,7},{5,4},{6,5},{7,6},{8,11},{9,8},{10,9... | collective-permute-start | bytes 786440 | tf_op jit(solution)/shard_map/ppermute | solution.py:28
  156.1 7.1 %collective-permute-start.14 = (bf16[128,128]{1,0:T(8,128)(2,1)S(1)}, bf16[128,128]{1,0:T(8,128)(2,1)S(1)}, u32[]{:S(2)}, u32[]{:S(2)}) collective-permute-start(bf16[128,128]{1,0:T(8,128)(2,1)S(1)} %slice.208.q0), channel_id=1, source_target_pairs={{0,1},{1,2},{2,3},{3,0},{4,5},{5,6},{6,7},{7,4},{8,9},{9,10},{10,1... | collective-permute-start | bytes 98312 | tf_op jit(solution)/shard_map/ppermute | solution.py:28
  159.2 8.9 %collective-permute-start.15 = (bf16[128,128]{1,0:T(8,128)(2,1)S(1)}, bf16[128,128]{1,0:T(8,128)(2,1)S(1)}, u32[]{:S(2)}, u32[]{:S(2)}) collective-permute-start(bf16[128,128]{1,0:T(8,128)(2,1)S(1)} %slice.208.q0), channel_id=1, source_target_pairs={{0,2},{1,3},{2,0},{3,1},{4,6},{5,7},{6,4},{7,5},{8,10},{9,11},{10,... | collective-permute-start | bytes 98312 | tf_op jit(solution)/shard_map/ppermute | solution.py:28
  163.2 5.7 %collective-permute-start.16 = (bf16[128,128]{1,0:T(8,128)(2,1)S(1)}, bf16[128,128]{1,0:T(8,128)(2,1)S(1)}, u32[]{:S(2)}, u32[]{:S(2)}) collective-permute-start(bf16[128,128]{1,0:T(8,128)(2,1)S(1)} %slice.208.q0), channel_id=1, source_target_pairs={{0,3},{1,0},{2,1},{3,2},{4,7},{5,4},{6,5},{7,6},{8,11},{9,8},{10,9... | collective-permute-start | bytes 98312 | tf_op jit(solution)/shard_map/ppermute | solution.py:28
  (16 other events, 43.6 us)

commit v3 on v2

v3 whole, which is shorter than its diff:
```python
import functools
import math

import jax
import jax.numpy as jnp
import numpy as np
from jax import lax
from jax.experimental import pallas as pl
from jax.experimental.pallas import tpu as pltpu
from jax.sharding import Mesh, PartitionSpec as P


AXES = ("xl", "c", "xh", "z", "y")
SIZES = (2, 2, 2, 8, 4)
EDGE = 8
REACH = 3
TAPS = 7
LANES = 128
PACK = 32


def shift(cells, axes, target):
    sizes = [SIZES[AXES.index(axis)] for axis in axes]
    pairs = []
    for place in np.ndindex(*sizes):
        goal = target(*place)
        if goal is not None:
            pairs.append((int(np.ravel_multi_index(place, sizes)), int(np.ravel_multi_index(goal, sizes))))
    return lax.ppermute(cells, axes if len(axes) > 1 else axes[0], pairs)


def swap_core(cells):
    return shift(cells, ("c",), lambda c: (1 - c,))


def side(cells):
    def target(xl, c, xh):
        x = (2 * xh + xl + (1 if c == 0 else 3)) % 4
        return (x % 2, c, x // 2)

    return shift(cells, ("xl", "c", "xh"), target)


def along_y(cells, step):
    return shift(cells, ("y",), lambda y: ((y + step) % 4,))


def neighbour(step):
    def target(xh, z, y):
        place = (xh * 8 + z) * 4 + y + step
        if not 0 <= place < 64:
            return None
        return (place // 32, place // 4 % 8, place % 4)

    return target


def added(*parts):
    total = parts[0].astype(jnp.float32)
    for part in parts[1:]:
        total = total + part.astype(jnp.float32)
    return total


def low_lanes(shape):
    return lax.broadcasted_iota(jnp.int32, shape, len(shape) - 1) < LANES // 2


def paired(cells):
    whole = cells + pltpu.roll(cells, LANES // 2, 1)
    head = whole.astype(jnp.bfloat16).astype(jnp.float32)
    return jnp.where(low_lanes(cells.shape), head, whole - head)


def thirds(cells):
    head = cells.astype(jnp.bfloat16)
    rest = cells - head.astype(jnp.float32)
    middle = rest.astype(jnp.bfloat16)
    return head, middle, (rest - middle.astype(jnp.float32)).astype(jnp.bfloat16)


def turning(size):
    place = lax.broadcasted_iota(jnp.int32, (size, size), 0) + lax.broadcasted_iota(jnp.int32, (size, size), 1)
    return (place == size - 1).astype(jnp.bfloat16)


def dot(a, b):
    return jnp.dot(a, b, preferred_element_type=jnp.float32)


def turned(cells, turn):
    size = turn.shape[0]
    count = cells.shape[1] // size
    return jnp.concatenate([dot(cells[:, at * size : (at + 1) * size], turn) for at in range(count)[::-1]], axis=1)


def ready_kernel(place, window, codes, table, before, after, upstream, stacks, columns, ups):
    rows, features = window.shape
    width = features // 4
    total = rows + 2 * EDGE
    turn = turning(256)
    for r in range(4):
        cols = pl.ds(pl.multiple_of((place[0] ^ r) * width, width), width)
        looked = jnp.zeros((rows, width), jnp.float32)
        for symbol in range(table.shape[0]):
            looked = looked + jnp.where(codes[...] == symbol, table[symbol : symbol + 1, cols], 0.0)
        middle = (window[:, cols].astype(jnp.float32) + looked).astype(jnp.bfloat16)
        whole = jnp.concatenate(
            [
                before[:, cols].astype(jnp.float32),
                middle.astype(jnp.float32),
                after[:, cols].astype(jnp.float32),
            ],
            axis=0,
        ).astype(jnp.bfloat16)
        back = turned(whole, turn)
        stacks[r, :total] = whole
        stacks[3 - r, total:] = back.astype(jnp.bfloat16)
        columns[r, :, :rows] = middle.astype(jnp.float32).T.astype(jnp.bfloat16)
        columns[3 - r, :, rows:] = back[EDGE : EDGE + rows].T.astype(jnp.bfloat16)
    whole = jnp.concatenate(
        [
            before[:, features:].astype(jnp.float32),
            upstream[...].astype(jnp.float32),
            after[:, features:].astype(jnp.float32),
        ],
        axis=0,
    ).astype(jnp.bfloat16)
    ups[:total] = whole
    ups[total:] = turned(whole, turn).astype(jnp.bfloat16)


def strand_kernel(stacks, w0, w1, w2, w3, ups, taps, out, grads, sums, values, mixes):
    total = stacks.shape[1] // 2
    rows = total - 2 * EDGE
    units = w0.shape[1]
    count = units // LANES

    def project(at, _):
        cols = pl.ds(pl.multiple_of(at * 256, 256), 256)
        acc = jnp.zeros((2 * total, 256), jnp.float32)
        for r, w in enumerate((w0, w1, w2, w3)):
            acc = acc + dot(stacks[r], w[:, cols])
        values[:, cols] = acc.astype(jnp.bfloat16).astype(jnp.float32)
        return 0

    lax.fori_loop(0, units // 256, project, 0)
    sums[...] = jnp.zeros(sums.shape, jnp.float32)
    turn = turning(LANES)

    def work(at, _):
        outs = []
        for way in range(2):
            block = at if way == 0 else count - 1 - at
            cols = pl.ds(pl.multiple_of(block * LANES, LANES), LANES)
            base = way * total
            places = [base + EDGE + (tap - REACH if way == 0 else REACH - tap) for tap in range(TAPS)]
            linear = values[base : base + total, cols]
            logistic = jax.nn.sigmoid(linear)
            gating = linear * logistic
            up = ups[base : base + total, cols].astype(jnp.float32)
            grad_mix = up * gating
            mixes[way] = grad_mix
            mid = slice(EDGE, EDGE + rows)
            linear, logistic, gating, up, grad_mix = [
                cells[mid] for cells in (linear, logistic, gating, up, grad_mix)
            ]
            mixing = jnp.zeros((rows, LANES), jnp.float32)
            for tap in range(TAPS):
                moved = values[places[tap] : places[tap] + rows, cols]
                mixing = mixing + taps[tap : tap + 1, cols] * moved
                sums[tap : tap + 1, cols] += jnp.sum(grad_mix * moved, axis=0, keepdims=True)
            outs.append(mixing * gating)
            acc = up * mixing * logistic * (1.0 + linear * (1.0 - logistic))
            for tap in range(TAPS):
                lower = 2 * EDGE - places[tap] + base
                acc = acc + taps[tap : tap + 1, cols] * mixes[way, lower : lower + rows]
            grads[way * rows : (way + 1) * rows, cols] = acc.astype(jnp.bfloat16)
        out[:, pl.ds(pl.multiple_of(at * LANES, LANES), LANES)] = (
            outs[0] + dot(outs[1].astype(jnp.bfloat16), turn)
        ).astype(jnp.bfloat16)
        return 0

    lax.fori_loop(0, count, work, 0)


def product_kernel(columns, grads, out, *, block, start):
    out[...] = dot(columns[block, start : start + out.shape[0]], grads[...]).astype(jnp.bfloat16)


def later_product_kernel(columns, grads, earlier, out, *, block, start):
    product_kernel(columns, grads, out, block=block, start=start)


def side_kernel(columns, grads, came, out, *, block, start):
    own = dot(columns[block, start : start + out.shape[0]], grads[...])
    out[...] = (own + came[...].astype(jnp.float32)).astype(jnp.bfloat16)


def back_kernel(place, grads, hot, sums, w0, w1, w2, w3, later, out, packed, table):
    rows = out.shape[0]
    width = w0.shape[0]
    turn = turning(256)
    dims = (((1,), (1,)), ((), ()))
    weights = (w0, w1, w2, w3)
    for r in range(4):
        here = lax.dot_general(grads[:rows], weights[r][...], dims, preferred_element_type=jnp.float32)
        there = lax.dot_general(grads[rows:], weights[3 - r][...], dims, preferred_element_type=jnp.float32)
        whole = here + turned(there.astype(jnp.bfloat16), turn)
        cols = pl.ds(pl.multiple_of((place[0] ^ r) * width, width), width)
        out[:, cols] = whole.astype(jnp.bfloat16)
        table[:, cols] = added(*[dot(hot[...], part) for part in thirds(whole)])
    count = sums.shape[1] // LANES
    half = table.shape[1] // 2
    for at in range(count):
        cols = slice(at * LANES, (at + 1) * LANES)
        packed[at * PACK : at * PACK + 8] = sums[:, cols]
        packed[at * PACK + 8 : at * PACK + 16] = table[:8, cols]
        packed[at * PACK + 16 : at * PACK + 24] = table[:8, half + at * LANES : half + (at + 1) * LANES]
        packed[at * PACK + 24 : at * PACK + 32] = jnp.zeros((8, LANES), jnp.float32)


def block_kernel(place, columns, grads, mate, came, *refs, start):
    if len(refs) > 4:
        packed, packed_came, outs, first, second = refs[0], refs[1], refs[2:6], refs[6], refs[7]
        whole = packed[...] + packed_came[...]
        head = whole.astype(jnp.bfloat16).astype(jnp.float32)
        rest = whole - head
        low = low_lanes(whole.shape)
        first[...] = jnp.where(low, head, pltpu.roll(rest, LANES // 2, 1))
        second[...] = jnp.where(low, pltpu.roll(head, LANES // 2, 1), rest)
    else:
        outs = refs
    rows = outs[0].shape[0]
    units = grads.shape[1]
    for step, out in enumerate(outs):
        at = pl.multiple_of((place[1] + step) % 4 * rows, rows)
        own = dot(columns[0, pl.ds(start + at, rows)], grads[...])
        here = pl.ds(at, rows)
        out[:, :units] = (
            own + mate[pl.ds(start + at, rows)].astype(jnp.float32) + came[here].astype(jnp.float32)
        ).astype(jnp.bfloat16)
        if len(refs) > 4:
            out[:, units : units + LANES] = first[here].astype(jnp.bfloat16)
            out[:, units + LANES :] = second[here].astype(jnp.bfloat16)


def quarter_kernel(*refs):
    head, tail, out = refs[:4], refs[4:8], refs[8]
    rows, units = head[0].shape
    size = 16

    def step(at, _):
        here = pl.ds(pl.multiple_of(at * size, size), size)
        there = pl.ds(pl.multiple_of(rows + at * size, size), size)
        out[here, :units] = added(*[part[here] for part in head]).astype(jnp.bfloat16)
        out[there, :units] = added(*[part[here, :units] for part in tail]).astype(jnp.bfloat16)
        for goal, start in ((here, units), (there, units + LANES)):
            cells = added(*[part[here, start : start + LANES] for part in tail])
            out[goal, units:] = paired(cells).astype(jnp.bfloat16)
        return 0

    lax.fori_loop(0, rows // size, step, 0)


def piece_kernel(parts, out):
    units = out.shape[2] - LANES
    total = parts[0].astype(jnp.float32)
    for at in range(1, parts.shape[0]):
        total = total + parts[at].astype(jnp.float32)
    plain = total[:, :units].astype(jnp.bfloat16)
    packed = paired(total[:, units:]).astype(jnp.bfloat16)
    for at in range(parts.shape[0]):
        out[at, :, :units] = plain
        out[at, :, units:] = packed


def final_kernel(place, q0, q1, q2, q3, weight_out, taps_out, table_out, packed, *, factor):
    rows = q0.shape[0] // 2
    units = weight_out.shape[1]
    for step, part in enumerate((q0, q1, q2, q3)):
        at = pl.multiple_of((place[1] + 4 - step) % 4 * rows, rows)
        for half in range(2):
            here = slice(half * rows, (half + 1) * rows)
            there = pl.ds(half * 4 * rows + at, rows)
            weight_out[there] = part[here, :units].astype(jnp.float32) * factor
            packed[there] = part[here, units:].astype(jnp.float32)
    cells = packed[...]
    whole = cells + pltpu.roll(cells, LANES // 2, 1)
    half = whole.shape[0] // 2
    whole = jnp.where(low_lanes((half, LANES)), whole[:half], whole[half:]) * factor
    count = half // PACK
    symbols = table_out.shape[0]
    for at in range(count):
        cols = slice(at * LANES, (at + 1) * LANES)
        taps_out[:, cols] = whole[at * PACK : at * PACK + TAPS]
        table_out[:, cols] = whole[at * PACK + 8 : at * PACK + 8 + symbols]
        cols = slice(units + at * LANES, units + (at + 1) * LANES)
        table_out[:, cols] = whole[at * PACK + 16 : at * PACK + 16 + symbols]


def call(kernel, outs, *args, scratch=(), scalar=False, unread=None, **fixed):
    inside = pl.BlockSpec(memory_space=pltpu.VMEM)
    specs = [inside] * len(args)
    if scalar:
        specs[0] = pl.BlockSpec(memory_space=pltpu.SMEM)
    if unread is not None:
        specs[unread] = pl.BlockSpec(memory_space=pl.ANY)
    return pl.pallas_call(
        functools.partial(kernel, **fixed),
        out_shape=outs,
        in_specs=specs,
        out_specs=jax.tree.map(lambda _: inside, outs),
        scratch_shapes=list(scratch),
        compiler_params=pltpu.CompilerParams(vmem_limit_bytes=20 * 2**20),
    )(*args)


def array(shape, dtype=jnp.bfloat16):
    return jax.ShapeDtypeStruct(shape, dtype)


def step(hidden, tokens, embedding, weight, kernel, cotangent):
    window = hidden[0]
    upstream = cotangent[0]
    rows, features = window.shape
    units = weight.shape[1]
    symbols = embedding.shape[0]
    factor = 1.0 / math.sqrt(rows * 256)
    width = features // 4
    total = rows + 2 * EDGE
    me = 2 * lax.axis_index("xl") + lax.axis_index("c")
    place = jnp.stack([me, lax.axis_index("y")]).astype(jnp.int32)
    weights = [weight, swap_core(weight), side(weight)]
    weights.append(swap_core(weights[2]))
    codes = tokens[0][:, None]

    def edge(part):
        looked = jnp.zeros((EDGE, features), jnp.float32)
        for symbol in range(symbols):
            looked = looked + jnp.where(codes[part] == symbol, embedding[symbol][None, :], 0.0)
        stream = (window[part].astype(jnp.float32) + looked).astype(jnp.bfloat16)
        return jnp.concatenate([stream, upstream[part]], axis=1)

    before = shift(edge(slice(rows - EDGE, rows)), ("xh", "z", "y"), neighbour(1))
    after = shift(edge(slice(0, EDGE)), ("xh", "z", "y"), neighbour(-1))
    stacks, columns, ups = call(
        ready_kernel,
        (array((4, 2 * total, width)), array((4, width, 2 * rows)), array((2 * total, units))),
        place,
        window,
        codes,
        embedding,
        before,
        after,
        upstream,
        scalar=True,
    )
    block_result, grads, sums = call(
        strand_kernel,
        (array((rows, units)), array((2 * rows, units)), array((8, units), jnp.float32)),
        stacks,
        *weights,
        ups,
        kernel,
        scratch=(pltpu.VMEM((2 * total, units), jnp.float32), pltpu.VMEM((2, total, LANES), jnp.float32)),
    )

    half = width // 2
    chunk = array((half, units))
    goes = call(product_kernel, chunk, columns, grads, block=3, start=0)
    goes = [goes, call(later_product_kernel, chunk, columns, grads, goes, unread=2, block=3, start=half)]
    mate = call(later_product_kernel, array((width, units)), columns, grads, goes[1], unread=2, block=1, start=0)
    came = [swap_core(goes[at]) for at in range(2)]
    mate = swap_core(mate)
    sides = [call(side_kernel, chunk, columns, grads, came[at], block=2, start=at * half) for at in range(2)]
    came = [side(sides[at]) for at in range(2)]
    hot = (jnp.arange(16, dtype=jnp.int32)[:, None] == tokens).astype(jnp.bfloat16)
    grad_hidden, packed = call(
        back_kernel,
        (array((rows, features)), array((units // LANES * PACK, LANES), jnp.float32)),
        place,
        grads,
        hot,
        sums,
        *weights,
        sides[1],
        scalar=True,
        unread=8,
        scratch=(pltpu.VMEM((16, features), jnp.float32),),
    )
    packed = packed + swap_core(packed)
    part = half // 4
    head = call(block_kernel, (array((part, units)),) * 4, place, columns, grads, mate, came[0], scalar=True, start=0)
    head = [head[0]] + [along_y(head[step], step) for step in (1, 2, 3)]
    tail = call(
        block_kernel,
        (array((part, units + 2 * LANES)),) * 4,
        place,
        columns,
        grads,
        mate,
        came[1],
        packed,
        side(packed),
        scalar=True,
        scratch=(pltpu.VMEM(packed.shape, jnp.float32),) * 2,
        start=half,
    )
    tail = [tail[0]] + [along_y(tail[step], step) for step in (1, 2, 3)]
    quarter = call(quarter_kernel, array((2 * part, units + LANES)), *head, *tail)
    pieces = quarter.reshape(16, part // 8, -1)
    pieces = lax.all_to_all(pieces, ("xh", "z"), split_axis=0, concat_axis=0, tiled=True)
    pieces = call(piece_kernel, array(pieces.shape), pieces)
    pieces = lax.all_to_all(pieces, ("xh", "z"), split_axis=0, concat_axis=0, tiled=True)
    quarter = pieces.reshape(quarter.shape)
    quarters = [quarter] + [along_y(quarter, step) for step in (1, 2, 3)]
    grad_weight, grad_kernel, grad_embedding = call(
        final_kernel,
        (array((width, units), jnp.float32), array(kernel.shape, jnp.float32), array(embedding.shape, jnp.float32)),
        place,
        *quarters,
        scalar=True,
        scratch=(pltpu.VMEM((width, LANES), jnp.float32),),
        factor=factor,
    )
    return block_result[None], grad_hidden[None], grad_weight, grad_kernel, grad_embedding


def solution(mesh):
    fine = Mesh(mesh.devices.reshape(SIZES), AXES)
    batch = ("xl", "c")
    spot = ("xh", "z", "y")
    in_specs = (P(batch, spot, None), P(batch, spot), P(), P(batch, None), P(), P(batch, spot, None))
    out_specs = (P(batch, spot, None), P(batch, spot, None), P(batch, None), P(), P())
    return jax.shard_map(step, mesh=fine, in_specs=in_specs, out_specs=out_specs, check_vma=False)
```

time: 176 us -> 140 us (0.80)
  blocking collectives: 0 us -> 36.3 us
  matrix products: 21.4 us -> 0 us
  starting transfers between devices: 49.9 us -> 28.5 us
  local copies, waits for them, and re-layouts: 23.4 us -> 6.16 us
  other arithmetic: 18.4 us -> 1.81 us
  waiting for transfers between devices: 40 us -> 43.5 us
  Pallas kernels: 20.2 us -> 22.5 us
    all_to_all x0 -> x2, blocking collectives: none -> 36.3 us  [step(): lax.all_to_all(pieces, ('xh', 'z'), split_axis=0, concat_axis=0, tiled=True)]
    dot_general x26 -> x0, matrix products: 21.4 us -> none  [the longest x20 14.2 us: flipped(): jnp.dot(cells[:, (count - 1 - at) * size:(count - at) * size], turn, pref...]
    ppermute x17 -> x21, waiting for transfers between devices: 25.6 us -> 43.5 us  [shift(): return lax.ppermute(cells, axes if len(axes) > 1 else axes[0], pairs)]
    all_to_all x2 -> x0, waiting for transfers between devices: 14.4 us -> none  [the longest x1 7.7 us: reduce_rows(): lax.all_to_all(jnp.broadcast_to(piece[None], pieces.shape), ('xh', 'z'),...]
    ppermute x17 -> x21, starting transfers between devices: 39.7 us -> 28.5 us  [shift(): return lax.ppermute(cells, axes if len(axes) > 1 else axes[0], pairs)]
    all_to_all x2 -> x0, starting transfers between devices: 10.2 us -> none  [the longest x1 5.49 us: reduce_rows(): lax.all_to_all(pieces, ('xh', 'z'), split_axis=0, concat_axis=0, tiled=True)]
    another operation x9 -> x1, other arithmetic: 9.1 us -> 0.08 us  [step(): place = jnp.stack([me, lax.axis_index('y')]).astype(jnp.int32)]
    concatenate x4 -> x2, other arithmetic: 6.4 us -> 0.01 us  [edge(): return jnp.concatenate([stream, upstream[part]], axis=1)]
  transfers between devices with their start and end apart: 19 -> 21, of which waited for: 8 -> 10; matrix products, arithmetic and copies ran while one was open for 35% -> 3% of each run, Pallas kernels for 3% -> 8%
where the time goes in v3:
time: 140 us
  waiting for transfers between devices  43.5 us (31%)
  blocking collectives  36.3 us (26%)
  starting transfers between devices  28.5 us (20%)
  Pallas kernels  22.5 us (16%)
  local copies, waits for them, and re-layouts  6.16 us (4%)
  other arithmetic  1.81 us (1%)
    ppermute x21, waiting for transfers between devices, shift(): return lax.ppermute(cells, axes if len(axes) > 1 else axes[0], pairs)  43.5 us
    all_to_all x2, blocking collectives, step(): lax.all_to_all(pieces, ('xh', 'z'), split_axis=0, concat_axis=0, tiled=True)  36.3 us
    ppermute x21, starting transfers between devices, shift(): return lax.ppermute(cells, axes if len(axes) > 1 else axes[0], pairs)  28.5 us
    pallas_call x13, Pallas kernels, call(): pl.pallas_call(functools.partial(kernel, **fixed), out_shape=outs, in_spe...  22.5 us
    unnamed x12, local copies, waits for them, and re-layouts  3.59 us
  transfers between devices with their start and end apart: 21, of which 10 were waited for; matrix products, arithmetic and copies ran while one was open for 3% of the time, Pallas kernels for 8%

profile of v3, /device:TPU:2, one launch (start us, length us, event | category | flops | bytes accessed | tf_op | source)
XLA Modules:
  0.0 139.5 jit_solution(3899255179146803437)
XLA Ops:
  0.6 1.6 %collective-permute-start.3 = (bf16[512,1024]{1,0:T(8,128)(2,1)}, bf16[512,1024]{1,0:T(8,128)(2,1)S(1)}, u32[]{:S(2)}, u32[]{:S(2)}) collective-permute-start(bf16[512,1024]{1,0:T(8,128)(2,1)} %w0.3), channel_id=1, source_target_pairs={{0,128},{32,160},{64,224},{96,192},{128,32},{160,0},{192,64},{224,... | collective-permute-start | bytes 3145736 | tf_op jit(solution)/shard_map/ppermute | solution.py:29
  4.1 11.9 %collective-permute-done.3.w2 = bf16[512,1024]{1,0:T(8,128)(2,1)S(1)} collective-permute-done((bf16[512,1024]{1,0:T(8,128)(2,1)}, bf16[512,1024]{1,0:T(8,128)(2,1)S(1)}, u32[]{:S(2)}, u32[]{:S(2)}) %collective-permute-start.3) | collective-permute-done | bytes 1048608 | tf_op jit(solution)/shard_map/ppermute | solution.py:29
  17.6 3.3 %collective-permute-start = (bf16[8,3072]{1,0:T(8,128)(2,1)S(1)}, bf16[8,3072]{1,0:T(8,128)(2,1)S(1)}, u32[]{:S(2)}, u32[]{:S(2)}) collective-permute-start(bf16[8,3072]{1,0:T(8,128)(2,1)S(1)} %pad_maximum_fusion), channel_id=1, source_target_pairs={{0,1},{1,2},{2,3},{3,4},{4,5},{5,6},{6,7},{7,8},{8,9},{9,10},{10,1... | collective-permute-start | bytes 147464 | tf_op jit(solution)/shard_map/ppermute | solution.py:29
  20.9 1.3 collective-permute-start.1
  23.0 3.8 %collective-permute-done.1.after = bf16[8,3072]{1,0:T(8,128)(2,1)S(1)} collective-permute-done((bf16[8,3072]{1,0:T(8,128)(2,1)S(1)}, bf16[8,3072]{1,0:T(8,128)(2,1)S(1)}, u32[]{:S(2)}, u32[]{:S(2)}) %collective-permute-start.1) | collective-permute-done | bytes 49184 | tf_op jit(solution)/shard_map/ppermute | solution.py:29
  29.7 1.5 %shard_map.101 = (bf16[4,288,512]{2,1,0:T(8,128)(2,1)S(1)}, bf16[4,512,256]{2,1,0:T(8,128)(2,1)S(1)}, bf16[288,1024]{1,0:T(8,128)(2,1)S(1)}) custom-call(s32[2]{0:T(128)S(1)} %pad_add_fusion.place, bf16[128,2048]{1,0:T(8,128)(2,1)S(1)} %bitcast.50, s32[128,1]{1,0:T(8,128)S(1)} %copy.11.codes, f32[5,2048]{1,0:T(8,128)S(1)} %copy-done.3, ...), custom_call_target="tpu_custom_call" | custom-call | tf_op jit(solution)/shard_map/pallas_call | solution.py:309
  32.0 8.5 %shard_map.102 = (bf16[128,1024]{1,0:T(8,128)(2,1)}, bf16[256,1024]{1,0:T(8,128)(2,1)S(1)}, f32[8,1024]{1,0:T(8,128)S(1)}) custom-call(bf16[4,288,512]{2,1,0:T(8,128)(2,1)S(1)} %get-tuple-element.24.stacks, bf16[512,1024]{1,0:T(8,128)(2,1)S(1)} %copy-done, bf16[512,1024]{1,0:T(8,128)(2,1)S(1)} %collective-permute-done.2.w1, ...), custom_call_target="tpu_custom_call" | custom-call | tf_op jit(solution)/shard_map/pallas_call | solution.py:309
  43.5 7.1 %collective-permute-start.8 = (bf16[256,1024]{1,0:T(8,128)(2,1)S(1)}, bf16[256,1024]{1,0:T(8,128)(2,1)S(1)}, u32[]{:S(2)}, u32[]{:S(2)}) collective-permute-start(bf16[256,1024]{1,0:T(8,128)(2,1)S(1)} %shard_map.108), channel_id=1, source_target_pairs={{0,128},{32,160},{64,224},{96,192},{128,32},{160,0},{192,64},{224,... | collective-permute-start | bytes 1572872 | tf_op jit(solution)/shard_map/ppermute | solution.py:29
  50.9 1.9 %collective-permute-start.12 = (bf16[256,1024]{1,0:T(8,128)(2,1)S(1)}, bf16[256,1024]{1,0:T(8,128)(2,1)S(1)}, u32[]{:S(2)}, u32[]{:S(2)}) collective-permute-start(bf16[256,1024]{1,0:T(8,128)(2,1)S(1)} %shard_map.105.later), channel_id=1, source_target_pairs={{0,128},{32,160},{64,224},{96,192},{128,32},{160,0},{192,64},{224,... | collective-permute-start | bytes 1572872 | tf_op jit(solution)/shard_map/ppermute | solution.py:29
  52.9 5.9 %shard_map.106 = (bf16[128,2048]{1,0:T(8,128)(2,1)}, f32[256,128]{1,0:T(8,128)S(1)}) custom-call(s32[2]{0:T(128)S(1)} %pad_add_fusion.place, bf16[256,1024]{1,0:T(8,128)(2,1)S(1)} %get-tuple-element.27.grads, bf16[16,128]{1,0:T(8,128)(2,1)S(1)} %fusion.2.hot, f32[8,1024]{1,0:T(8,128)S(1)} %get-tuple-element.28.sums, bf16[512,1024]{1,0:T(8,128)(2,1)S(1)} %copy-done, ...), custom_call_target="tpu_custom_call" | custom-call | tf_op jit(solution)/shard_map/pallas_call | solution.py:309
  58.8 1.3 collective-permute-done.13
  60.2 1.1 collective-permute-start.14
  62.5 2.9 %collective-permute-done.14.refs_1_ = f32[256,128]{1,0:T(8,128)S(1)} collective-permute-done((f32[256,128]{1,0:T(8,128)S(1)}, f32[256,128]{1,0:T(8,128)S(1)}, u32[]{:S(2)}, u32[]{:S(2)}) %collective-permute-start.14) | collective-permute-done | bytes 131104 | tf_op jit(solution)/shard_map/ppermute | solution.py:29
  66.6 1.7 %collective-permute-start.16 = (bf16[64,1280]{1,0:T(8,128)(2,1)S(1)}, bf16[64,1280]{1,0:T(8,128)(2,1)S(1)}, u32[]{:S(2)}, u32[]{:S(2)}) collective-permute-start(bf16[64,1280]{1,0:T(8,128)(2,1)S(1)} %get-tuple-element.38), channel_id=1, source_target_pairs={{0,2},{1,3},{2,0},{3,1},{4,6},{5,7},{6,4},{7,5},{8,10},{9,11},{10,... | collective-permute-start | bytes 491528 | tf_op jit(solution)/shard_map/ppermute | solution.py:29
  68.3 1.5 %collective-permute-start.17 = (bf16[64,1280]{1,0:T(8,128)(2,1)S(1)}, bf16[64,1280]{1,0:T(8,128)(2,1)S(1)}, u32[]{:S(2)}, u32[]{:S(2)}) collective-permute-start(bf16[64,1280]{1,0:T(8,128)(2,1)S(1)} %get-tuple-element.39), channel_id=1, source_target_pairs={{0,3},{1,0},{2,1},{3,2},{4,7},{5,4},{6,5},{7,6},{8,11},{9,8},{10,9... | collective-permute-start | bytes 491528 | tf_op jit(solution)/shard_map/ppermute | solution.py:29
  69.8 2.9 %collective-permute-start.10 = (bf16[64,1024]{1,0:T(8,128)(2,1)S(1)}, bf16[64,1024]{1,0:T(8,128)(2,1)S(1)}, u32[]{:S(2)}, u32[]{:S(2)}) collective-permute-start(bf16[64,1024]{1,0:T(8,128)(2,1)S(1)} %get-tuple-element.33), channel_id=1, source_target_pairs={{0,2},{1,3},{2,0},{3,1},{4,6},{5,7},{6,4},{7,5},{8,10},{9,11},{10,... | collective-permute-start | bytes 393224 | tf_op jit(solution)/shard_map/ppermute | solution.py:29
  73.3 5.5 %collective-permute-done.10.refs_2_ = bf16[64,1024]{1,0:T(8,128)(2,1)S(1)} collective-permute-done((bf16[64,1024]{1,0:T(8,128)(2,1)S(1)}, bf16[64,1024]{1,0:T(8,128)(2,1)S(1)}, u32[]{:S(2)}, u32[]{:S(2)}) %collective-permute-start.10) | collective-permute-done | bytes 131104 | tf_op jit(solution)/shard_map/ppermute | solution.py:29
  78.9 4.0 %collective-permute-done.11.refs_3_ = bf16[64,1024]{1,0:T(8,128)(2,1)S(1)} collective-permute-done((bf16[64,1024]{1,0:T(8,128)(2,1)S(1)}, bf16[64,1024]{1,0:T(8,128)(2,1)S(1)}, u32[]{:S(2)}, u32[]{:S(2)}) %collective-permute-start.11) | collective-permute-done | bytes 131104 | tf_op jit(solution)/shard_map/ppermute | solution.py:29
  83.4 20.2 %all_to_all.10.parts = bf16[16,8,1152]{2,1,0:T(8,128)(2,1)S(1)} all-to-all(bf16[16,8,1152]{2,1,0:T(8,128)(2,1)S(1)} %bitcast.49), channel_id=1, replica_groups=mesh['xl'=2,'c'=2,'xh'=2,'z'=8,'y'=4] {'xh','z'}, dimensions={0} | all-to-all | bytes 589824 | tf_op jit(solution)/shard_map/all_to_all | solution.py:413
  103.7 16.1 %all_to_all.11 = bf16[16,8,1152]{2,1,0:T(8,128)(2,1)S(1)} all-to-all(bf16[16,8,1152]{2,1,0:T(8,128)(2,1)S(1)} %shard_map.112), channel_id=1, replica_groups=mesh['xl'=2,'c'=2,'xh'=2,'z'=8,'y'=4] {'xh','z'}, dimensions={0} | all-to-all | bytes 589824 | tf_op jit(solution)/shard_map/all_to_all | solution.py:415
  119.8 3.6 %collective-permute-start.20 = (bf16[128,1152]{1,0:T(8,128)(2,1)S(1)}, bf16[128,1152]{1,0:T(8,128)(2,1)S(1)}, u32[]{:S(2)}, u32[]{:S(2)}) collective-permute-start(bf16[128,1152]{1,0:T(8,128)(2,1)S(1)} %bitcast.45), channel_id=1, source_target_pairs={{0,3},{1,0},{2,1},{3,2},{4,7},{5,4},{6,5},{7,6},{8,11},{9,8},{10,9... | collective-permute-start | bytes 884744 | tf_op jit(solution)/shard_map/ppermute | solution.py:29
  124.3 9.7 %collective-permute-done.20.q3 = bf16[128,1152]{1,0:T(8,128)(2,1)S(1)} collective-permute-done((bf16[128,1152]{1,0:T(8,128)(2,1)S(1)}, bf16[128,1152]{1,0:T(8,128)(2,1)S(1)}, u32[]{:S(2)}, u32[]{:S(2)}) %collective-permute-start.20) | collective-permute-done | bytes 294944 | tf_op jit(solution)/shard_map/ppermute | solution.py:29
  134.6 2.8 %collective-permute-done.18.q1 = bf16[128,1152]{1,0:T(8,128)(2,1)S(1)} collective-permute-done((bf16[128,1152]{1,0:T(8,128)(2,1)S(1)}, bf16[128,1152]{1,0:T(8,128)(2,1)S(1)}, u32[]{:S(2)}, u32[]{:S(2)}) %collective-permute-start.18) | collective-permute-done | bytes 294944 | tf_op jit(solution)/shard_map/ppermute | solution.py:29
  137.4 2.1 %shard_map.113 = (f32[512,1024]{1,0:T(8,128)}, f32[7,1024]{1,0:T(8,128)}, f32[5,2048]{1,0:T(8,128)}) custom-call(s32[2]{0:T(128)S(1)} %pad_add_fusion.place, bf16[128,1152]{1,0:T(8,128)(2,1)S(1)} %bitcast.48, bf16[128,1152]{1,0:T(8,128)(2,1)S(1)} %collective-permute-done.18.q1, bf16[128,1152]{1,0:T(8,128)(2,1)S(1)} %collective-permute-done.19.q2, ...), custom_call_target="tpu_custom_call" | custom-call | tf_op jit(solution)/shard_map/pallas_call | solution.py:309
  (55 shorter events, 16.1 us)
Async XLA Ops:
  0.6 30.6 %copy-start = (bf16[512,1024]{1,0:T(8,128)(2,1)S(1)}, bf16[512,1024]{1,0:T(8,128)(2,1)}, u32[]{:S(2)}) copy-start(bf16[512,1024]{1,0:T(8,128)(2,1)} %w0.3) | copy-start | bytes 3145732
  0.6 15.3 %collective-permute-start.3 = (bf16[512,1024]{1,0:T(8,128)(2,1)}, bf16[512,1024]{1,0:T(8,128)(2,1)S(1)}, u32[]{:S(2)}, u32[]{:S(2)}) collective-permute-start(bf16[512,1024]{1,0:T(8,128)(2,1)} %w0.3), channel_id=1, source_target_pairs={{0,128},{32,160},{64,224},{96,192},{128,32},{160,0},{192,64},{224,... | collective-permute-start | bytes 3145736 | tf_op jit(solution)/shard_map/ppermute | solution.py:29
  2.2 29.0 %collective-permute-start.2 = (bf16[512,1024]{1,0:T(8,128)(2,1)}, bf16[512,1024]{1,0:T(8,128)(2,1)S(1)}, u32[]{:S(2)}, u32[]{:S(2)}) collective-permute-start(bf16[512,1024]{1,0:T(8,128)(2,1)} %w0.3), channel_id=1, source_target_pairs={{0,64},{64,0},{1,65},{65,1},{2,66},{66,2},{3,67},{67,3},{4,68},{68... | collective-permute-start | bytes 3145736 | tf_op jit(solution)/shard_map/ppermute | solution.py:29
  15.9 15.3 %collective-permute-start.4 = (bf16[512,1024]{1,0:T(8,128)(2,1)S(1)}, bf16[512,1024]{1,0:T(8,128)(2,1)}, u32[]{:S(2)}, u32[]{:S(2)}) collective-permute-start(bf16[512,1024]{1,0:T(8,128)(2,1)S(1)} %collective-permute-done.3.w2), channel_id=1, source_target_pairs={{0,64},{64,0},{1,65},{65,1},{2,66},{66,2},{3,67},{67,3},{4,68},{68... | collective-permute-start | bytes 3145736 | tf_op jit(solution)/shard_map/ppermute | solution.py:29
  17.6 5.4 %collective-permute-start = (bf16[8,3072]{1,0:T(8,128)(2,1)S(1)}, bf16[8,3072]{1,0:T(8,128)(2,1)S(1)}, u32[]{:S(2)}, u32[]{:S(2)}) collective-permute-start(bf16[8,3072]{1,0:T(8,128)(2,1)S(1)} %pad_maximum_fusion), channel_id=1, source_target_pairs={{0,1},{1,2},{2,3},{3,4},{4,5},{5,6},{6,7},{7,8},{8,9},{9,10},{10,1... | collective-permute-start | bytes 147464 | tf_op jit(solution)/shard_map/ppermute | solution.py:29
  20.9 6.0 %collective-permute-start.1 = (bf16[8,3072]{1,0:T(8,128)(2,1)S(1)}, bf16[8,3072]{1,0:T(8,128)(2,1)S(1)}, u32[]{:S(2)}, u32[]{:S(2)}) collective-permute-start(bf16[8,3072]{1,0:T(8,128)(2,1)S(1)} %pad_maximum_fusion.1), channel_id=1, source_target_pairs={{1,0},{2,1},{3,2},{4,3},{5,4},{6,5},{7,6},{8,7},{9,8},{10,9},{11,1... | collective-permute-start | bytes 147464 | tf_op jit(solution)/shard_map/ppermute | solution.py:29
  26.9 1.0 copy-start.1
  41.2 2.0 %collective-permute-start.7 = (bf16[256,1024]{1,0:T(8,128)(2,1)S(1)}, bf16[256,1024]{1,0:T(8,128)(2,1)S(1)}, u32[]{:S(2)}, u32[]{:S(2)}) collective-permute-start(bf16[256,1024]{1,0:T(8,128)(2,1)S(1)} %shard_map.103.earlier), channel_id=1, source_target_pairs={{0,64},{64,0},{1,65},{65,1},{2,66},{66,2},{3,67},{67,3},{4,68},{68... | collective-permute-start | bytes 1572872 | tf_op jit(solution)/shard_map/ppermute | solution.py:29
  41.7 11.2 %copy-start.5 = (s32[1,128]{1,0:T(1,128)S(1)}, s32[1,128]{1,0:T(1,128)}, u32[]{:S(2)}) copy-start(s32[1,128]{1,0:T(1,128)} %param.7) | copy-start | bytes 1540
  41.7 19.6 %collective-permute-start.6 = (bf16[512,1024]{1,0:T(8,128)(2,1)S(1)}, bf16[512,1024]{1,0:T(8,128)(2,1)S(1)}, u32[]{:S(2)}, u32[]{:S(2)}) collective-permute-start(bf16[512,1024]{1,0:T(8,128)(2,1)S(1)} %shard_map.107), channel_id=1, source_target_pairs={{0,64},{64,0},{1,65},{65,1},{2,66},{66,2},{3,67},{67,3},{4,68},{68... | collective-permute-start | bytes 3145736 | tf_op jit(solution)/shard_map/ppermute | solution.py:29
  42.3 8.3 %collective-permute-start.5 = (bf16[256,1024]{1,0:T(8,128)(2,1)S(1)}, bf16[256,1024]{1,0:T(8,128)(2,1)S(1)}, u32[]{:S(2)}, u32[]{:S(2)}) collective-permute-start(bf16[256,1024]{1,0:T(8,128)(2,1)S(1)} %shard_map.104.earlier), channel_id=1, source_target_pairs={{0,64},{64,0},{1,65},{65,1},{2,66},{66,2},{3,67},{67,3},{4,68},{68... | collective-permute-start | bytes 1572872 | tf_op jit(solution)/shard_map/ppermute | solution.py:29
  43.5 17.9 %collective-permute-start.8 = (bf16[256,1024]{1,0:T(8,128)(2,1)S(1)}, bf16[256,1024]{1,0:T(8,128)(2,1)S(1)}, u32[]{:S(2)}, u32[]{:S(2)}) collective-permute-start(bf16[256,1024]{1,0:T(8,128)(2,1)S(1)} %shard_map.108), channel_id=1, source_target_pairs={{0,128},{32,160},{64,224},{96,192},{128,32},{160,0},{192,64},{224,... | collective-permute-start | bytes 1572872 | tf_op jit(solution)/shard_map/ppermute | solution.py:29
  50.9 14.5 %collective-permute-start.12 = (bf16[256,1024]{1,0:T(8,128)(2,1)S(1)}, bf16[256,1024]{1,0:T(8,128)(2,1)S(1)}, u32[]{:S(2)}, u32[]{:S(2)}) collective-permute-start(bf16[256,1024]{1,0:T(8,128)(2,1)S(1)} %shard_map.105.later), channel_id=1, source_target_pairs={{0,128},{32,160},{64,224},{96,192},{128,32},{160,0},{192,64},{224,... | collective-permute-start | bytes 1572872 | tf_op jit(solution)/shard_map/ppermute | solution.py:29
  58.8 1.3 collective-permute-start.13
  60.2 5.2 %collective-permute-start.14 = (f32[256,128]{1,0:T(8,128)S(1)}, f32[256,128]{1,0:T(8,128)S(1)}, u32[]{:S(2)}, u32[]{:S(2)}) collective-permute-start(f32[256,128]{1,0:T(8,128)S(1)} %add.47.refs_0_), channel_id=1, source_target_pairs={{0,128},{32,160},{64,224},{96,192},{128,32},{160,0},{192,64},{224,... | collective-permute-start | bytes 393224 | tf_op jit(solution)/shard_map/ppermute | solution.py:29
  62.4 10.4 %collective-permute-start.9 = (bf16[64,1024]{1,0:T(8,128)(2,1)S(1)}, bf16[64,1024]{1,0:T(8,128)(2,1)S(1)}, u32[]{:S(2)}, u32[]{:S(2)}) collective-permute-start(bf16[64,1024]{1,0:T(8,128)(2,1)S(1)} %get-tuple-element.32), channel_id=1, source_target_pairs={{0,1},{1,2},{2,3},{3,0},{4,5},{5,6},{6,7},{7,4},{8,9},{9,10},{10,1... | collective-permute-start | bytes 393224 | tf_op jit(solution)/shard_map/ppermute | solution.py:29
  66.5 16.4 %collective-permute-start.15 = (bf16[64,1280]{1,0:T(8,128)(2,1)S(1)}, bf16[64,1280]{1,0:T(8,128)(2,1)S(1)}, u32[]{:S(2)}, u32[]{:S(2)}) collective-permute-start(bf16[64,1280]{1,0:T(8,128)(2,1)S(1)} %get-tuple-element.37), channel_id=1, source_target_pairs={{0,1},{1,2},{2,3},{3,0},{4,5},{5,6},{6,7},{7,4},{8,9},{9,10},{10,1... | collective-permute-start | bytes 491528 | tf_op jit(solution)/shard_map/ppermute | solution.py:29
  66.6 16.4 %collective-permute-start.16 = (bf16[64,1280]{1,0:T(8,128)(2,1)S(1)}, bf16[64,1280]{1,0:T(8,128)(2,1)S(1)}, u32[]{:S(2)}, u32[]{:S(2)}) collective-permute-start(bf16[64,1280]{1,0:T(8,128)(2,1)S(1)} %get-tuple-element.38), channel_id=1, source_target_pairs={{0,2},{1,3},{2,0},{3,1},{4,6},{5,7},{6,4},{7,5},{8,10},{9,11},{10,... | collective-permute-start | bytes 491528 | tf_op jit(solution)/shard_map/ppermute | solution.py:29
  68.3 14.6 %collective-permute-start.17 = (bf16[64,1280]{1,0:T(8,128)(2,1)S(1)}, bf16[64,1280]{1,0:T(8,128)(2,1)S(1)}, u32[]{:S(2)}, u32[]{:S(2)}) collective-permute-start(bf16[64,1280]{1,0:T(8,128)(2,1)S(1)} %get-tuple-element.39), channel_id=1, source_target_pairs={{0,3},{1,0},{2,1},{3,2},{4,7},{5,4},{6,5},{7,6},{8,11},{9,8},{10,9... | collective-permute-start | bytes 491528 | tf_op jit(solution)/shard_map/ppermute | solution.py:29
  69.8 9.1 %collective-permute-start.10 = (bf16[64,1024]{1,0:T(8,128)(2,1)S(1)}, bf16[64,1024]{1,0:T(8,128)(2,1)S(1)}, u32[]{:S(2)}, u32[]{:S(2)}) collective-permute-start(bf16[64,1024]{1,0:T(8,128)(2,1)S(1)} %get-tuple-element.33), channel_id=1, source_target_pairs={{0,2},{1,3},{2,0},{3,1},{4,6},{5,7},{6,4},{7,5},{8,10},{9,11},{10,... | collective-permute-start | bytes 393224 | tf_op jit(solution)/shard_map/ppermute | solution.py:29
  72.7 10.2 %collective-permute-start.11 = (bf16[64,1024]{1,0:T(8,128)(2,1)S(1)}, bf16[64,1024]{1,0:T(8,128)(2,1)S(1)}, u32[]{:S(2)}, u32[]{:S(2)}) collective-permute-start(bf16[64,1024]{1,0:T(8,128)(2,1)S(1)} %get-tuple-element.34), channel_id=1, source_target_pairs={{0,3},{1,0},{2,1},{3,2},{4,7},{5,4},{6,5},{7,6},{8,11},{9,8},{10,9... | collective-permute-start | bytes 393224 | tf_op jit(solution)/shard_map/ppermute | solution.py:29
  119.8 14.2 %collective-permute-start.20 = (bf16[128,1152]{1,0:T(8,128)(2,1)S(1)}, bf16[128,1152]{1,0:T(8,128)(2,1)S(1)}, u32[]{:S(2)}, u32[]{:S(2)}) collective-permute-start(bf16[128,1152]{1,0:T(8,128)(2,1)S(1)} %bitcast.45), channel_id=1, source_target_pairs={{0,3},{1,0},{2,1},{3,2},{4,7},{5,4},{6,5},{7,6},{8,11},{9,8},{10,9... | collective-permute-start | bytes 884744 | tf_op jit(solution)/shard_map/ppermute | solution.py:29
  123.4 11.2 %collective-permute-start.19 = (bf16[128,1152]{1,0:T(8,128)(2,1)S(1)}, bf16[128,1152]{1,0:T(8,128)(2,1)S(1)}, u32[]{:S(2)}, u32[]{:S(2)}) collective-permute-start(bf16[128,1152]{1,0:T(8,128)(2,1)S(1)} %bitcast.46), channel_id=1, source_target_pairs={{0,2},{1,3},{2,0},{3,1},{4,6},{5,7},{6,4},{7,5},{8,10},{9,11},{10,... | collective-permute-start | bytes 884744 | tf_op jit(solution)/shard_map/ppermute | solution.py:29
  123.4 14.0 %collective-permute-start.18 = (bf16[128,1152]{1,0:T(8,128)(2,1)S(1)}, bf16[128,1152]{1,0:T(8,128)(2,1)S(1)}, u32[]{:S(2)}, u32[]{:S(2)}) collective-permute-start(bf16[128,1152]{1,0:T(8,128)(2,1)S(1)} %bitcast.47), channel_id=1, source_target_pairs={{0,1},{1,2},{2,3},{3,0},{4,5},{5,6},{6,7},{7,4},{8,9},{9,10},{10,1... | collective-permute-start | bytes 884744 | tf_op jit(solution)/shard_map/ppermute | solution.py:29
  (3 other events, 2.6 us)

commit v4 on v3

--- a/solution.py
+++ b/solution.py
@@ -94,54 +94,108 @@
     return jnp.concatenate([dot(cells[:, at * size : (at + 1) * size], turn) for at in range(count)[::-1]], axis=1)
 
 
-def ready_kernel(place, window, codes, table, before, after, upstream, stacks, columns, ups):
+def edge_kernel(codes, last, first, up_last, up_first, table, before, after, looked):
+    rows = codes.shape[1]
+    features = table.shape[1]
+    for start, cells, up, out in ((rows - EDGE, last, up_last, before), (0, first, up_first, after)):
+        for at in range(EDGE):
+            looked[at : at + 1] = table[pl.ds(codes[0, start + at], 1)]
+        out[:, :features] = (cells[...].astype(jnp.float32) + looked[...]).astype(jnp.bfloat16)
+        out[:, features:] = up[...]
+
+
+def centre_kernel(
+    place, codes, taps, window_far, table_far, up_far, stacks, columns, ups, taps_near, hot, window, table, up, done
+):
+    loads = [
+        pltpu.make_async_copy(far, near, done.at[at])
+        for at, (far, near) in enumerate(((window_far, window), (table_far, table), (up_far, up)))
+    ]
+    for load in loads:
+        load.start()
+    taps_near[...] = taps[...]
     rows, features = window.shape
+    symbol = lax.broadcasted_iota(jnp.int32, (16, rows), 0)
+    one_hot = jnp.where(symbol == codes[...], 1.0, 0.0).astype(jnp.bfloat16)
+    for at in range(3):
+        hot[:, at * rows : (at + 1) * rows] = one_hot
     width = features // 4
+    turn = turning(256)
+    by_row = jnp.broadcast_to(codes[...].astype(jnp.float32), (rows, rows)).T
+    by_row = jnp.concatenate([by_row] * (width // rows), axis=1)
+    for load in loads:
+        load.wait()
+    for r in range(4):
+        cols = pl.ds(pl.multiple_of((place[0] ^ r) * width, width), width)
+        looked = jnp.zeros((rows, width), jnp.float32)
+        for symbol in range(table.shape[0]):
+            looked = looked + jnp.where(by_row == symbol, table[symbol : symbol + 1, cols], 0.0)
+        middle = (window[:, cols].astype(jnp.float32) + looked).astype(jnp.bfloat16)
+        back = turned(middle, turn)
+        stacks[r, :rows] = middle
+        stacks[3 - r, rows:] = back.astype(jnp.bfloat16)
+        columns[r, :, :rows] = middle.astype(jnp.float32).T.astype(jnp.bfloat16)
+        columns[3 - r, :, rows:] = back.T.astype(jnp.bfloat16)
+    ups[:rows] = up[...].astype(jnp.float32)
+    ups[rows:] = turned(up[...], turn)
+
+
+def early_kernel(place, centre, up_centre, before, after, w0, w1, stacks, ups, partial):
+    rows = up_centre.shape[0] // 2
+    features = 4 * centre.shape[2]
+    width = centre.shape[2]
     total = rows + 2 * EDGE
     turn = turning(256)
     for r in range(4):
         cols = pl.ds(pl.multiple_of((place[0] ^ r) * width, width), width)
-        looked = jnp.zeros((rows, width), jnp.float32)
-        for symbol in range(table.shape[0]):
-            looked = looked + jnp.where(codes[...] == symbol, table[symbol : symbol + 1, cols], 0.0)
-        middle = (window[:, cols].astype(jnp.float32) + looked).astype(jnp.bfloat16)
-        whole = jnp.concatenate(
-            [
-                before[:, cols].astype(jnp.float32),
-                middle.astype(jnp.float32),
-                after[:, cols].astype(jnp.float32),
-            ],
-            axis=0,
-        ).astype(jnp.bfloat16)
-        back = turned(whole, turn)
-        stacks[r, :total] = whole
-        stacks[3 - r, total:] = back.astype(jnp.bfloat16)
-        columns[r, :, :rows] = middle.astype(jnp.float32).T.astype(jnp.bfloat16)
-        columns[3 - r, :, rows:] = back[EDGE : EDGE + rows].T.astype(jnp.bfloat16)
-    whole = jnp.concatenate(
-        [
-            before[:, features:].astype(jnp.float32),
-            upstream[...].astype(jnp.float32),
-            after[:, features:].astype(jnp.float32),
-        ],
-        axis=0,
-    ).astype(jnp.bfloat16)
-    ups[:total] = whole
-    ups[total:] = turned(whole, turn).astype(jnp.bfloat16)
-
-
-def strand_kernel(stacks, w0, w1, w2, w3, ups, taps, out, grads, sums, values, mixes):
+        halo = jnp.concatenate([before[:, cols].astype(jnp.float32), after[:, cols].astype(jnp.float32)], axis=0)
+        halo = halo.astype(jnp.bfloat16)
+        stacks[r, : 2 * rows] = centre[r]
+        stacks[r, 2 * rows : 2 * rows + 2 * EDGE] = halo
+        stacks[3 - r, 2 * rows + 2 * EDGE :] = turned(halo, turn).astype(jnp.bfloat16)
+    for way in range(2):
+        base = way * total
+        ups[base + EDGE : base + EDGE + rows] = up_centre[way * rows : (way + 1) * rows]
+        for part, start in ((before, base), (after, base + EDGE + rows)):
+            cells = part[:, features:].astype(jnp.float32)
+            if way == 1:
+                cells = turned(cells.astype(jnp.bfloat16), turn)
+            ups[start : start + EDGE] = cells
+    add_products(partial, None, ((stacks.at[0], w0), (stacks.at[1], w1)))
+
+
+def add_products(out, start, pairs):
+    def step(at, _):
+        cols = pl.ds(pl.multiple_of(at * 256, 256), 256)
+        acc = added(*[dot(cells[...], w[:, cols]) for cells, w in pairs])
+        if start is not None:
+            acc = acc + start[:, cols]
+        out[:, cols] = acc
+        return 0
+
+    lax.fori_loop(0, out.shape[1] // 256, step, 0)
+
+
+def middle_kernel(stacks, partial, w2, out):
+    add_products(out, partial, ((stacks.at[2], w2),))
+
+
+def strand_kernel(stacks, partial, w3, ups, taps, out, grads, sums, values, mixes):
     total = stacks.shape[1] // 2
     rows = total - 2 * EDGE
-    units = w0.shape[1]
+    units = w3.shape[1]
     count = units // LANES
 
     def project(at, _):
         cols = pl.ds(pl.multiple_of(at * 256, 256), 256)
-        acc = jnp.zeros((2 * total, 256), jnp.float32)
-        for r, w in enumerate((w0, w1, w2, w3)):
-            acc = acc + dot(stacks[r], w[:, cols])
-        values[:, cols] = acc.astype(jnp.bfloat16).astype(jnp.float32)
+        acc = partial[:, cols] + dot(stacks[3], w3[:, cols])
+        acc = acc.astype(jnp.bfloat16).astype(jnp.float32)
+        for way in range(2):
+            base = way * total
+            halo = 2 * rows + way * 2 * EDGE
+            values[base : base + EDGE, cols] = acc[halo : halo + EDGE]
+            values[base + EDGE : base + EDGE + rows, cols] = acc[way * rows : (way + 1) * rows]
+            values[base + EDGE + rows : base + total, cols] = acc[halo + EDGE : halo + 2 * EDGE]
         return 0
 
     lax.fori_loop(0, units // 256, project, 0)
@@ -158,7 +212,7 @@
             linear = values[base : base + total, cols]
             logistic = jax.nn.sigmoid(linear)
             gating = linear * logistic
-            up = ups[base : base + total, cols].astype(jnp.float32)
+            up = ups[base : base + total, cols]
             grad_mix = up * gating
             mixes[way] = grad_mix
             mid = slice(EDGE, EDGE + rows)
@@ -197,19 +251,18 @@
     out[...] = (own + came[...].astype(jnp.float32)).astype(jnp.bfloat16)
 
 
-def back_kernel(place, grads, hot, sums, w0, w1, w2, w3, later, out, packed, table):
+def back_kernel(place, grads, hot, sums, w0, w1, w2, w3, later, out, packed, table, backs):
     rows = out.shape[0]
     width = w0.shape[0]
     turn = turning(256)
     dims = (((1,), (1,)), ((), ()))
-    weights = (w0, w1, w2, w3)
+    for r, w in enumerate((w0, w1, w2, w3)):
+        backs[r] = lax.dot_general(grads[...], w[...], dims, preferred_element_type=jnp.float32)
     for r in range(4):
-        here = lax.dot_general(grads[:rows], weights[r][...], dims, preferred_element_type=jnp.float32)
-        there = lax.dot_general(grads[rows:], weights[3 - r][...], dims, preferred_element_type=jnp.float32)
-        whole = here + turned(there.astype(jnp.bfloat16), turn)
+        whole = backs[r, :rows] + turned(backs[3 - r, rows:].astype(jnp.bfloat16), turn)
         cols = pl.ds(pl.multiple_of((place[0] ^ r) * width, width), width)
         out[:, cols] = whole.astype(jnp.bfloat16)
-        table[:, cols] = added(*[dot(hot[...], part) for part in thirds(whole)])
+        table[:, cols] = dot(hot[...], jnp.concatenate(thirds(whole), axis=0))
     count = sums.shape[1] // LANES
     half = table.shape[1] // 2
     for at in range(count):
@@ -221,7 +274,9 @@
 
 
 def block_kernel(place, columns, grads, mate, came, *refs, start):
-    if len(refs) > 4:
+    wide = len(refs) > 5
+    own = refs[-1]
+    if wide:
         packed, packed_came, outs, first, second = refs[0], refs[1], refs[2:6], refs[6], refs[7]
         whole = packed[...] + packed_came[...]
         head = whole.astype(jnp.bfloat16).astype(jnp.float32)
@@ -230,17 +285,15 @@
         first[...] = jnp.where(low, head, pltpu.roll(rest, LANES // 2, 1))
         second[...] = jnp.where(low, pltpu.roll(head, LANES // 2, 1), rest)
     else:
-        outs = refs
+        outs = refs[:4]
     rows = outs[0].shape[0]
     units = grads.shape[1]
+    own[...] = dot(columns[0, start : start + 4 * rows], grads[...])
     for step, out in enumerate(outs):
         at = pl.multiple_of((place[1] + step) % 4 * rows, rows)
-        own = dot(columns[0, pl.ds(start + at, rows)], grads[...])
         here = pl.ds(at, rows)
-        out[:, :units] = (
-            own + mate[pl.ds(start + at, rows)].astype(jnp.float32) + came[here].astype(jnp.float32)
-        ).astype(jnp.bfloat16)
-        if len(refs) > 4:
+        out[:, :units] = added(own[here], mate[pl.ds(start + at, rows)], came[here]).astype(jnp.bfloat16)
+        if wide:
             out[:, units : units + LANES] = first[here].astype(jnp.bfloat16)
             out[:, units + LANES :] = second[here].astype(jnp.bfloat16)
 
@@ -299,13 +352,13 @@
         table_out[:, cols] = whole[at * PACK + 16 : at * PACK + 16 + symbols]
 
 
-def call(kernel, outs, *args, scratch=(), scalar=False, unread=None, **fixed):
+def call(kernel, outs, *args, scratch=(), scalar=False, unread=(), **fixed):
     inside = pl.BlockSpec(memory_space=pltpu.VMEM)
     specs = [inside] * len(args)
     if scalar:
         specs[0] = pl.BlockSpec(memory_space=pltpu.SMEM)
-    if unread is not None:
-        specs[unread] = pl.BlockSpec(memory_space=pl.ANY)
+    for at in unread:
+        specs[at] = pl.BlockSpec(memory_space=pl.ANY)
     return pl.pallas_call(
         functools.partial(kernel, **fixed),
         out_shape=outs,
@@ -333,49 +386,86 @@
     place = jnp.stack([me, lax.axis_index("y")]).astype(jnp.int32)
     weights = [weight, swap_core(weight), side(weight)]
     weights.append(swap_core(weights[2]))
-    codes = tokens[0][:, None]
-
-    def edge(part):
-        looked = jnp.zeros((EDGE, features), jnp.float32)
-        for symbol in range(symbols):
-            looked = looked + jnp.where(codes[part] == symbol, embedding[symbol][None, :], 0.0)
-        stream = (window[part].astype(jnp.float32) + looked).astype(jnp.bfloat16)
-        return jnp.concatenate([stream, upstream[part]], axis=1)
-
-    before = shift(edge(slice(rows - EDGE, rows)), ("xh", "z", "y"), neighbour(1))
-    after = shift(edge(slice(0, EDGE)), ("xh", "z", "y"), neighbour(-1))
-    stacks, columns, ups = call(
-        ready_kernel,
-        (array((4, 2 * total, width)), array((4, width, 2 * rows)), array((2 * total, units))),
+    top = pl.BlockSpec((EDGE, features), lambda at: (0, 0))
+    bottom = pl.BlockSpec((EDGE, features), lambda at: (rows // EDGE - 1, 0))
+    up_top = pl.BlockSpec((EDGE, units), lambda at: (0, 0))
+    up_bottom = pl.BlockSpec((EDGE, units), lambda at: (rows // EDGE - 1, 0))
+    edge = array((EDGE, features + units))
+    before, after = pl.pallas_call(
+        edge_kernel,
+        out_shape=(edge, edge),
+        grid=(1,),
+        in_specs=[
+            pl.BlockSpec(memory_space=pltpu.SMEM),
+            bottom,
+            top,
+            up_bottom,
+            up_top,
+            pl.BlockSpec((symbols, features), lambda at: (0, 0)),
+        ],
+        out_specs=[pl.BlockSpec(edge.shape, lambda at: (0, 0))] * 2,
+        scratch_shapes=[pltpu.VMEM((EDGE, features), jnp.float32)],
+    )(tokens, window, window, upstream, upstream, embedding)
+    before = shift(before, ("xh", "z", "y"), neighbour(1))
+    after = shift(after, ("xh", "z", "y"), neighbour(-1))
+    centre, columns, up_centre, taps, hot = call(
+        centre_kernel,
+        (
+            array((4, 2 * rows, width)),
+            array((4, width, 2 * rows)),
+            array((2 * rows, units), jnp.float32),
+            array(kernel.shape, jnp.float32),
+            array((16, 3 * rows)),
+        ),
         place,
+        tokens,
+        kernel,
         window,
-        codes,
         embedding,
+        upstream,
+        scalar=True,
+        unread=(3, 4, 5),
+        scratch=(
+            pltpu.VMEM((rows, features), jnp.bfloat16),
+            pltpu.VMEM((symbols, features), jnp.float32),
+            pltpu.VMEM((rows, units), jnp.bfloat16),
+            pltpu.SemaphoreType.DMA((3,)),
+        ),
+    )
+    wide = array((2 * total, units), jnp.float32)
+    stacks, ups, partial = call(
+        early_kernel,
+        (array((4, 2 * total, width)), wide, wide),
+        place,
+        centre,
+        up_centre,
         before,
         after,
-        upstream,
+        weights[0],
+        weights[1],
         scalar=True,
     )
+    partial = call(middle_kernel, wide, stacks, partial, weights[2])
     block_result, grads, sums = call(
         strand_kernel,
         (array((rows, units)), array((2 * rows, units)), array((8, units), jnp.float32)),
         stacks,
-        *weights,
+        partial,
+        weights[3],
         ups,
-        kernel,
+        taps,
         scratch=(pltpu.VMEM((2 * total, units), jnp.float32), pltpu.VMEM((2, total, LANES), jnp.float32)),
     )
 
     half = width // 2
     chunk = array((half, units))
     goes = call(product_kernel, chunk, columns, grads, block=3, start=0)
-    goes = [goes, call(later_product_kernel, chunk, columns, grads, goes, unread=2, block=3, start=half)]
-    mate = call(later_product_kernel, array((width, units)), columns, grads, goes[1], unread=2, block=1, start=0)
+    goes = [goes, call(later_product_kernel, chunk, columns, grads, goes, unread=(2,), block=3, start=half)]
+    mate = call(later_product_kernel, array((width, units)), columns, grads, goes[1], unread=(2,), block=1, start=0)
     came = [swap_core(goes[at]) for at in range(2)]
     mate = swap_core(mate)
     sides = [call(side_kernel, chunk, columns, grads, came[at], block=2, start=at * half) for at in range(2)]
     came = [side(sides[at]) for at in range(2)]
-    hot = (jnp.arange(16, dtype=jnp.int32)[:, None] == tokens).astype(jnp.bfloat16)
     grad_hidden, packed = call(
         back_kernel,
         (array((rows, features)), array((units // LANES * PACK, LANES), jnp.float32)),
@@ -386,12 +476,23 @@
         *weights,
         sides[1],
         scalar=True,
-        unread=8,
-        scratch=(pltpu.VMEM((16, features), jnp.float32),),
+        unread=(8,),
+        scratch=(pltpu.VMEM((16, features), jnp.float32), pltpu.VMEM((4, 2 * rows, width), jnp.float32)),
     )
     packed = packed + swap_core(packed)
     part = half // 4
-    head = call(block_kernel, (array((part, units)),) * 4, place, columns, grads, mate, came[0], scalar=True, start=0)
+    head = call(
+        block_kernel,
+        (array((part, units)),) * 4,
+        place,
+        columns,
+        grads,
+        mate,
+        came[0],
+        scalar=True,
+        scratch=(pltpu.VMEM((half, units), jnp.float32),),
+        start=0,
+    )
     head = [head[0]] + [along_y(head[step], step) for step in (1, 2, 3)]
     tail = call(
         block_kernel,
@@ -404,7 +505,7 @@
         packed,
         side(packed),
         scalar=True,
-        scratch=(pltpu.VMEM(packed.shape, jnp.float32),) * 2,
+        scratch=(pltpu.VMEM(packed.shape, jnp.float32),) * 2 + (pltpu.VMEM((half, units), jnp.float32),),
         start=half,
     )
     tail = [tail[0]] + [along_y(tail[step], step) for step in (1, 2, 3)]

time: 140 us -> 133 us (0.950)
  local copies, waits for them, and re-layouts: 6.16 us -> 0.02 us
  Pallas kernels: 22.5 us -> 26.3 us
  other arithmetic: 1.81 us -> 0.1 us
    unnamed x12, local copies, waits for them, and re-layouts: 3.59 us -> 0.02 us
    pallas_call x13 -> x15, Pallas kernels: 22.5 us -> 24.6 us  [call(): pl.pallas_call(functools.partial(kernel, **fixed), out_shape=outs, in_spe...]
    slice x2 -> x0, local copies, waits for them, and re-layouts: 1.81 us -> none  [the longest x1 1.06 us: edge(): embedding[symbol][None, :]]
    pallas_call x0 -> x1, Pallas kernels: none -> 1.69 us  [step(): pl.pallas_call(edge_kernel, out_shape=(edge, edge), grid=(1,), in_specs=[...]
  transfers between devices with their start and end apart: 21 -> 21, of which waited for: 10 -> 8; matrix products, arithmetic and copies ran while one was open for 3% -> 0% of each run, Pallas kernels for 8% -> 12%
where the time goes in v4:
time: 133 us
  waiting for transfers between devices  42.1 us (32%)
  blocking collectives  35.6 us (27%)
  starting transfers between devices  27.8 us (21%)
  Pallas kernels  26.3 us (20%)
    ppermute x21, waiting for transfers between devices, shift(): return lax.ppermute(cells, axes if len(axes) > 1 else axes[0], pairs)  42.1 us
    all_to_all x2, blocking collectives, step(): lax.all_to_all(pieces, ('xh', 'z'), split_axis=0, concat_axis=0, tiled=True)  35.6 us
    ppermute x21, starting transfers between devices, shift(): return lax.ppermute(cells, axes if len(axes) > 1 else axes[0], pairs)  27.8 us
    pallas_call x15, Pallas kernels, call(): pl.pallas_call(functools.partial(kernel, **fixed), out_shape=outs, in_spe...  24.6 us
  transfers between devices with their start and end apart: 21, of which 8 were waited for; matrix products, arithmetic and copies ran while one was open for 0% of the time, Pallas kernels for 12%

profile of v4, /device:TPU:2, one launch (start us, length us, event | category | flops | bytes accessed | tf_op | source)
XLA Modules:
  0.0 132.7 jit_solution(12874890610161048757)
XLA Ops:
  0.7 1.6 %collective-permute-start.3 = (bf16[512,1024]{1,0:T(8,128)(2,1)}, bf16[512,1024]{1,0:T(8,128)(2,1)}, u32[]{:S(2)}, u32[]{:S(2)}) collective-permute-start(bf16[512,1024]{1,0:T(8,128)(2,1)} %w0.3), channel_id=1, source_target_pairs={{0,128},{32,160},{64,224},{96,192},{128,32},{160,0},{192,64},{224,... | collective-permute-start | bytes 3145736 | tf_op jit(solution)/shard_map/ppermute | solution.py:29
  2.3 13.8 %collective-permute-done.3.w2 = bf16[512,1024]{1,0:T(8,128)(2,1)} collective-permute-done((bf16[512,1024]{1,0:T(8,128)(2,1)}, bf16[512,1024]{1,0:T(8,128)(2,1)}, u32[]{:S(2)}, u32[]{:S(2)}) %collective-permute-start.3) | collective-permute-done | bytes 1048608 | tf_op jit(solution)/shard_map/ppermute | solution.py:29
  16.1 1.7 %shard_map.102 = (bf16[8,3072]{1,0:T(8,128)(2,1)}, bf16[8,3072]{1,0:T(8,128)(2,1)}) custom-call(s32[1,128]{1,0:T(1,128)} %codes.3, bf16[128,2048]{1,0:T(8,128)(2,1)} %bitcast.8, bf16[128,2048]{1,0:T(8,128)(2,1)} %bitcast.9, bf16[128,1024]{1,0:T(8,128)(2,1)} %bitcast.11, bf16[128,1024]{1,0:T(8,128)(2,1)} %bitcast.12, f32[5,2048]{1,0:T(8,128)} %table.1), custom_call_target="tpu_custom_call" | custom-call | tf_op jit(solution)/shard_map/pallas_call | solution.py:394
  17.8 3.2 %collective-permute-start = (bf16[8,3072]{1,0:T(8,128)(2,1)}, bf16[8,3072]{1,0:T(8,128)(2,1)S(1)}, u32[]{:S(2)}, u32[]{:S(2)}) collective-permute-start(bf16[8,3072]{1,0:T(8,128)(2,1)} %get-tuple-element.33), channel_id=1, source_target_pairs={{0,1},{1,2},{2,3},{3,4},{4,5},{5,6},{6,7},{7,8},{8,9},{9,10},{10,1... | collective-permute-start | bytes 147464 | tf_op jit(solution)/shard_map/ppermute | solution.py:29
  21.0 1.3 collective-permute-start.1
  22.5 1.7 %shard_map.101 = (bf16[4,256,512]{2,1,0:T(8,128)(2,1)S(1)}, bf16[4,512,256]{2,1,0:T(8,128)(2,1)S(1)}, f32[256,1024]{1,0:T(8,128)S(1)}, f32[7,1024]{1,0:T(8,128)S(1)}, bf16[16,384]{1,0:T(8,128)(2,1)S(1)}) custom-call(s32[2]{0:T(128)S(1)} %pad_add_fusion.place, s32[1,128]{1,0:T(1,128)S(1)} %copy-done.5, f32[7,1024]{1,0:T(8,128)S(1)} %copy-done.4, ...), custom_call_target="tpu_custom_call" | custom-call | tf_op jit(solution)/shard_map/pallas_call | solution.py:362
  24.1 3.1 %collective-permute-done.1.after = bf16[8,3072]{1,0:T(8,128)(2,1)S(1)} collective-permute-done((bf16[8,3072]{1,0:T(8,128)(2,1)}, bf16[8,3072]{1,0:T(8,128)(2,1)S(1)}, u32[]{:S(2)}, u32[]{:S(2)}) %collective-permute-start.1) | collective-permute-done | bytes 49184 | tf_op jit(solution)/shard_map/ppermute | solution.py:29
  27.2 2.3 %shard_map.103 = (bf16[4,288,512]{2,1,0:T(8,128)(2,1)S(1)}, f32[288,1024]{1,0:T(8,128)S(1)}, f32[288,1024]{1,0:T(8,128)S(1)}) custom-call(s32[2]{0:T(128)S(1)} %pad_add_fusion.place, bf16[4,256,512]{2,1,0:T(8,128)(2,1)S(1)} %get-tuple-element.31.centre, f32[256,1024]{1,0:T(8,128)S(1)} %get-tuple-element.32.up_centre, ...), custom_call_target="tpu_custom_call" | custom-call | tf_op jit(solution)/shard_map/pallas_call | solution.py:362
  29.5 2.2 %shard_map.104.partial = f32[288,1024]{1,0:T(8,128)S(1)} custom-call(bf16[4,288,512]{2,1,0:T(8,128)(2,1)S(1)} %get-tuple-element.35.stacks, f32[288,1024]{1,0:T(8,128)S(1)} %get-tuple-element.36.partial, bf16[512,1024]{1,0:T(8,128)(2,1)} %collective-permute-done.3.w2), custom_call_target="tpu_custom_call" | custom-call | tf_op jit(solution)/shard_map/pallas_call | solution.py:362
  31.7 7.5 %shard_map.105 = (bf16[128,1024]{1,0:T(8,128)(2,1)}, bf16[256,1024]{1,0:T(8,128)(2,1)S(1)}, f32[8,1024]{1,0:T(8,128)S(1)}) custom-call(bf16[4,288,512]{2,1,0:T(8,128)(2,1)S(1)} %get-tuple-element.35.stacks, f32[288,1024]{1,0:T(8,128)S(1)} %shard_map.104.partial, bf16[512,1024]{1,0:T(8,128)(2,1)} %collective-permute-done.4.w3, ...), custom_call_target="tpu_custom_call" | custom-call | tf_op jit(solution)/shard_map/pallas_call | solution.py:362
  42.1 7.2 %collective-permute-start.8 = (bf16[256,1024]{1,0:T(8,128)(2,1)S(1)}, bf16[256,1024]{1,0:T(8,128)(2,1)S(1)}, u32[]{:S(2)}, u32[]{:S(2)}) collective-permute-start(bf16[256,1024]{1,0:T(8,128)(2,1)S(1)} %shard_map.111), channel_id=1, source_target_pairs={{0,128},{32,160},{64,224},{96,192},{128,32},{160,0},{192,64},{224,... | collective-permute-start | bytes 1572872 | tf_op jit(solution)/shard_map/ppermute | solution.py:29
  49.7 1.9 %collective-permute-start.12 = (bf16[256,1024]{1,0:T(8,128)(2,1)S(1)}, bf16[256,1024]{1,0:T(8,128)(2,1)S(1)}, u32[]{:S(2)}, u32[]{:S(2)}) collective-permute-start(bf16[256,1024]{1,0:T(8,128)(2,1)S(1)} %shard_map.108.later), channel_id=1, source_target_pairs={{0,128},{32,160},{64,224},{96,192},{128,32},{160,0},{192,64},{224,... | collective-permute-start | bytes 1572872 | tf_op jit(solution)/shard_map/ppermute | solution.py:29
  51.6 4.5 %shard_map.109 = (bf16[128,2048]{1,0:T(8,128)(2,1)}, f32[256,128]{1,0:T(8,128)S(1)}) custom-call(s32[2]{0:T(128)S(1)} %pad_add_fusion.place, bf16[256,1024]{1,0:T(8,128)(2,1)S(1)} %get-tuple-element.40.grads, bf16[16,384]{1,0:T(8,128)(2,1)S(1)} %get-tuple-element.41.hot, f32[8,1024]{1,0:T(8,128)S(1)} %get-tuple-element.42.sums, ...), custom_call_target="tpu_custom_call" | custom-call | tf_op jit(solution)/shard_map/pallas_call | solution.py:362
  56.1 1.3 %collective-permute-done.13 = f32[256,128]{1,0:T(8,128)S(1)} collective-permute-done((f32[256,128]{1,0:T(8,128)S(1)}, f32[256,128]{1,0:T(8,128)S(1)}, u32[]{:S(2)}, u32[]{:S(2)}) %collective-permute-start.13) | collective-permute-done | bytes 131104 | tf_op jit(solution)/shard_map/ppermute | solution.py:29
  59.8 3.3 %collective-permute-done.14.refs_1_ = f32[256,128]{1,0:T(8,128)S(1)} collective-permute-done((f32[256,128]{1,0:T(8,128)S(1)}, f32[256,128]{1,0:T(8,128)S(1)}, u32[]{:S(2)}, u32[]{:S(2)}) %collective-permute-start.14) | collective-permute-done | bytes 131104 | tf_op jit(solution)/shard_map/ppermute | solution.py:29
  64.3 1.9 %collective-permute-start.16 = (bf16[64,1280]{1,0:T(8,128)(2,1)S(1)}, bf16[64,1280]{1,0:T(8,128)(2,1)S(1)}, u32[]{:S(2)}, u32[]{:S(2)}) collective-permute-start(bf16[64,1280]{1,0:T(8,128)(2,1)S(1)} %get-tuple-element.52), channel_id=1, source_target_pairs={{0,2},{1,3},{2,0},{3,1},{4,6},{5,7},{6,4},{7,5},{8,10},{9,11},{10,... | collective-permute-start | bytes 491528 | tf_op jit(solution)/shard_map/ppermute | solution.py:29
  66.2 1.3 collective-permute-start.17
  69.5 8.7 %collective-permute-done.11.refs_3_ = bf16[64,1024]{1,0:T(8,128)(2,1)S(1)} collective-permute-done((bf16[64,1024]{1,0:T(8,128)(2,1)S(1)}, bf16[64,1024]{1,0:T(8,128)(2,1)S(1)}, u32[]{:S(2)}, u32[]{:S(2)}) %collective-permute-start.11) | collective-permute-done | bytes 131104 | tf_op jit(solution)/shard_map/ppermute | solution.py:29
  78.8 19.5 %all_to_all.10.parts = bf16[16,8,1152]{2,1,0:T(8,128)(2,1)S(1)} all-to-all(bf16[16,8,1152]{2,1,0:T(8,128)(2,1)S(1)} %bitcast.18), channel_id=1, replica_groups=mesh['xl'=2,'c'=2,'xh'=2,'z'=8,'y'=4] {'xh','z'}, dimensions={0} | all-to-all | bytes 589824 | tf_op jit(solution)/shard_map/all_to_all | solution.py:514
  98.3 16.1 %all_to_all.11 = bf16[16,8,1152]{2,1,0:T(8,128)(2,1)S(1)} all-to-all(bf16[16,8,1152]{2,1,0:T(8,128)(2,1)S(1)} %shard_map.115), channel_id=1, replica_groups=mesh['xl'=2,'c'=2,'xh'=2,'z'=8,'y'=4] {'xh','z'}, dimensions={0} | all-to-all | bytes 589824 | tf_op jit(solution)/shard_map/all_to_all | solution.py:516
  115.7 3.8 %collective-permute-start.19 = (bf16[128,1152]{1,0:T(8,128)(2,1)S(1)}, bf16[128,1152]{1,0:T(8,128)(2,1)S(1)}, u32[]{:S(2)}, u32[]{:S(2)}) collective-permute-start(bf16[128,1152]{1,0:T(8,128)(2,1)S(1)} %bitcast.15), channel_id=1, source_target_pairs={{0,2},{1,3},{2,0},{3,1},{4,6},{5,7},{6,4},{7,5},{8,10},{9,11},{10,... | collective-permute-start | bytes 884744 | tf_op jit(solution)/shard_map/ppermute | solution.py:29
  119.6 5.5 %collective-permute-done.18.q1 = bf16[128,1152]{1,0:T(8,128)(2,1)S(1)} collective-permute-done((bf16[128,1152]{1,0:T(8,128)(2,1)S(1)}, bf16[128,1152]{1,0:T(8,128)(2,1)S(1)}, u32[]{:S(2)}, u32[]{:S(2)}) %collective-permute-start.18) | collective-permute-done | bytes 294944 | tf_op jit(solution)/shard_map/ppermute | solution.py:29
  125.1 5.5 %collective-permute-done.19.q2 = bf16[128,1152]{1,0:T(8,128)(2,1)S(1)} collective-permute-done((bf16[128,1152]{1,0:T(8,128)(2,1)S(1)}, bf16[128,1152]{1,0:T(8,128)(2,1)S(1)}, u32[]{:S(2)}, u32[]{:S(2)}) %collective-permute-start.19) | collective-permute-done | bytes 294944 | tf_op jit(solution)/shard_map/ppermute | solution.py:29
  130.6 2.1 %shard_map.116 = (f32[512,1024]{1,0:T(8,128)}, f32[7,1024]{1,0:T(8,128)}, f32[5,2048]{1,0:T(8,128)}) custom-call(s32[2]{0:T(128)S(1)} %pad_add_fusion.place, bf16[128,1152]{1,0:T(8,128)(2,1)S(1)} %bitcast.17, bf16[128,1152]{1,0:T(8,128)(2,1)S(1)} %collective-permute-done.18.q1, bf16[128,1152]{1,0:T(8,128)(2,1)S(1)} %collective-permute-done.19.q2, ...), custom_call_target="tpu_custom_call" | custom-call | tf_op jit(solution)/shard_map/pallas_call | solution.py:362
  (50 shorter events, 10.7 us)
Async XLA Ops:
  0.6 21.8 %copy-start = (bf16[1,128,2048]{2,1,0:T(8,128)(2,1)S(1)}, bf16[1,128,2048]{2,1,0:T(8,128)(2,1)}, u32[]{:S(2)}) copy-start(bf16[1,128,2048]{2,1,0:T(8,128)(2,1)} %param.6) | copy-start | bytes 1572868
  0.6 21.8 %copy-start.2 = (bf16[1,128,1024]{2,1,0:T(8,128)(2,1)S(1)}, bf16[1,128,1024]{2,1,0:T(8,128)(2,1)}, u32[]{:S(2)}) copy-start(bf16[1,128,1024]{2,1,0:T(8,128)(2,1)} %param.11) | copy-start | bytes 786436
  0.7 21.8 %copy-start.5 = (s32[1,128]{1,0:T(1,128)S(1)}, s32[1,128]{1,0:T(1,128)}, u32[]{:S(2)}) copy-start(s32[1,128]{1,0:T(1,128)} %codes.3) | copy-start | bytes 1540
  0.7 15.4 %collective-permute-start.3 = (bf16[512,1024]{1,0:T(8,128)(2,1)}, bf16[512,1024]{1,0:T(8,128)(2,1)}, u32[]{:S(2)}, u32[]{:S(2)}) collective-permute-start(bf16[512,1024]{1,0:T(8,128)(2,1)} %w0.3), channel_id=1, source_target_pairs={{0,128},{32,160},{64,224},{96,192},{128,32},{160,0},{192,64},{224,... | collective-permute-start | bytes 3145736 | tf_op jit(solution)/shard_map/ppermute | solution.py:29
  2.3 25.0 %collective-permute-start.2 = (bf16[512,1024]{1,0:T(8,128)(2,1)}, bf16[512,1024]{1,0:T(8,128)(2,1)S(1)}, u32[]{:S(2)}, u32[]{:S(2)}) collective-permute-start(bf16[512,1024]{1,0:T(8,128)(2,1)} %w0.3), channel_id=1, source_target_pairs={{0,64},{64,0},{1,65},{65,1},{2,66},{66,2},{3,67},{67,3},{4,68},{68... | collective-permute-start | bytes 3145736 | tf_op jit(solution)/shard_map/ppermute | solution.py:29
  16.1 15.6 %collective-permute-start.4 = (bf16[512,1024]{1,0:T(8,128)(2,1)}, bf16[512,1024]{1,0:T(8,128)(2,1)}, u32[]{:S(2)}, u32[]{:S(2)}) collective-permute-start(bf16[512,1024]{1,0:T(8,128)(2,1)} %collective-permute-done.3.w2), channel_id=1, source_target_pairs={{0,64},{64,0},{1,65},{65,1},{2,66},{66,2},{3,67},{67,3},{4,68},{68... | collective-permute-start | bytes 3145736 | tf_op jit(solution)/shard_map/ppermute | solution.py:29
  17.8 6.3 %collective-permute-start = (bf16[8,3072]{1,0:T(8,128)(2,1)}, bf16[8,3072]{1,0:T(8,128)(2,1)S(1)}, u32[]{:S(2)}, u32[]{:S(2)}) collective-permute-start(bf16[8,3072]{1,0:T(8,128)(2,1)} %get-tuple-element.33), channel_id=1, source_target_pairs={{0,1},{1,2},{2,3},{3,4},{4,5},{5,6},{6,7},{7,8},{8,9},{9,10},{10,1... | collective-permute-start | bytes 147464 | tf_op jit(solution)/shard_map/ppermute | solution.py:29
  21.0 6.2 %collective-permute-start.1 = (bf16[8,3072]{1,0:T(8,128)(2,1)}, bf16[8,3072]{1,0:T(8,128)(2,1)S(1)}, u32[]{:S(2)}, u32[]{:S(2)}) collective-permute-start(bf16[8,3072]{1,0:T(8,128)(2,1)} %get-tuple-element.34), channel_id=1, source_target_pairs={{1,0},{2,1},{3,2},{4,3},{5,4},{6,5},{7,6},{8,7},{9,8},{10,9},{11,1... | collective-permute-start | bytes 147464 | tf_op jit(solution)/shard_map/ppermute | solution.py:29
  39.8 2.0 %collective-permute-start.7 = (bf16[256,1024]{1,0:T(8,128)(2,1)S(1)}, bf16[256,1024]{1,0:T(8,128)(2,1)S(1)}, u32[]{:S(2)}, u32[]{:S(2)}) collective-permute-start(bf16[256,1024]{1,0:T(8,128)(2,1)S(1)} %shard_map.106.earlier), channel_id=1, source_target_pairs={{0,64},{64,0},{1,65},{65,1},{2,66},{66,2},{3,67},{67,3},{4,68},{68... | collective-permute-start | bytes 1572872 | tf_op jit(solution)/shard_map/ppermute | solution.py:29
  40.4 18.0 %collective-permute-start.6 = (bf16[512,1024]{1,0:T(8,128)(2,1)S(1)}, bf16[512,1024]{1,0:T(8,128)(2,1)S(1)}, u32[]{:S(2)}, u32[]{:S(2)}) collective-permute-start(bf16[512,1024]{1,0:T(8,128)(2,1)S(1)} %shard_map.110), channel_id=1, source_target_pairs={{0,64},{64,0},{1,65},{65,1},{2,66},{66,2},{3,67},{67,3},{4,68},{68... | collective-permute-start | bytes 3145736 | tf_op jit(solution)/shard_map/ppermute | solution.py:29
  41.0 8.4 %collective-permute-start.5 = (bf16[256,1024]{1,0:T(8,128)(2,1)S(1)}, bf16[256,1024]{1,0:T(8,128)(2,1)S(1)}, u32[]{:S(2)}, u32[]{:S(2)}) collective-permute-start(bf16[256,1024]{1,0:T(8,128)(2,1)S(1)} %shard_map.107.earlier), channel_id=1, source_target_pairs={{0,64},{64,0},{1,65},{65,1},{2,66},{66,2},{3,67},{67,3},{4,68},{68... | collective-permute-start | bytes 1572872 | tf_op jit(solution)/shard_map/ppermute | solution.py:29
  42.1 16.3 %collective-permute-start.8 = (bf16[256,1024]{1,0:T(8,128)(2,1)S(1)}, bf16[256,1024]{1,0:T(8,128)(2,1)S(1)}, u32[]{:S(2)}, u32[]{:S(2)}) collective-permute-start(bf16[256,1024]{1,0:T(8,128)(2,1)S(1)} %shard_map.111), channel_id=1, source_target_pairs={{0,128},{32,160},{64,224},{96,192},{128,32},{160,0},{192,64},{224,... | collective-permute-start | bytes 1572872 | tf_op jit(solution)/shard_map/ppermute | solution.py:29
  49.7 13.4 %collective-permute-start.12 = (bf16[256,1024]{1,0:T(8,128)(2,1)S(1)}, bf16[256,1024]{1,0:T(8,128)(2,1)S(1)}, u32[]{:S(2)}, u32[]{:S(2)}) collective-permute-start(bf16[256,1024]{1,0:T(8,128)(2,1)S(1)} %shard_map.108.later), channel_id=1, source_target_pairs={{0,128},{32,160},{64,224},{96,192},{128,32},{160,0},{192,64},{224,... | collective-permute-start | bytes 1572872 | tf_op jit(solution)/shard_map/ppermute | solution.py:29
  56.1 1.3 %collective-permute-start.13 = (f32[256,128]{1,0:T(8,128)S(1)}, f32[256,128]{1,0:T(8,128)S(1)}, u32[]{:S(2)}, u32[]{:S(2)}) collective-permute-start(f32[256,128]{1,0:T(8,128)S(1)} %get-tuple-element.49), channel_id=1, source_target_pairs={{0,64},{64,0},{1,65},{65,1},{2,66},{66,2},{3,67},{67,3},{4,68},{68... | collective-permute-start | bytes 393224 | tf_op jit(solution)/shard_map/ppermute | solution.py:29
  57.5 5.6 %collective-permute-start.14 = (f32[256,128]{1,0:T(8,128)S(1)}, f32[256,128]{1,0:T(8,128)S(1)}, u32[]{:S(2)}, u32[]{:S(2)}) collective-permute-start(f32[256,128]{1,0:T(8,128)S(1)} %add.7.refs_0_), channel_id=1, source_target_pairs={{0,128},{32,160},{64,224},{96,192},{128,32},{160,0},{192,64},{224,... | collective-permute-start | bytes 393224 | tf_op jit(solution)/shard_map/ppermute | solution.py:29
  59.5 9.0 %collective-permute-start.10 = (bf16[64,1024]{1,0:T(8,128)(2,1)S(1)}, bf16[64,1024]{1,0:T(8,128)(2,1)S(1)}, u32[]{:S(2)}, u32[]{:S(2)}) collective-permute-start(bf16[64,1024]{1,0:T(8,128)(2,1)S(1)} %get-tuple-element.47), channel_id=1, source_target_pairs={{0,2},{1,3},{2,0},{3,1},{4,6},{5,7},{6,4},{7,5},{8,10},{9,11},{10,... | collective-permute-start | bytes 393224 | tf_op jit(solution)/shard_map/ppermute | solution.py:29
  64.2 14.1 %collective-permute-start.15 = (bf16[64,1280]{1,0:T(8,128)(2,1)S(1)}, bf16[64,1280]{1,0:T(8,128)(2,1)S(1)}, u32[]{:S(2)}, u32[]{:S(2)}) collective-permute-start(bf16[64,1280]{1,0:T(8,128)(2,1)S(1)} %get-tuple-element.51), channel_id=1, source_target_pairs={{0,1},{1,2},{2,3},{3,0},{4,5},{5,6},{6,7},{7,4},{8,9},{9,10},{10,1... | collective-permute-start | bytes 491528 | tf_op jit(solution)/shard_map/ppermute | solution.py:29
  64.3 14.0 %collective-permute-start.16 = (bf16[64,1280]{1,0:T(8,128)(2,1)S(1)}, bf16[64,1280]{1,0:T(8,128)(2,1)S(1)}, u32[]{:S(2)}, u32[]{:S(2)}) collective-permute-start(bf16[64,1280]{1,0:T(8,128)(2,1)S(1)} %get-tuple-element.52), channel_id=1, source_target_pairs={{0,2},{1,3},{2,0},{3,1},{4,6},{5,7},{6,4},{7,5},{8,10},{9,11},{10,... | collective-permute-start | bytes 491528 | tf_op jit(solution)/shard_map/ppermute | solution.py:29
  66.2 12.1 %collective-permute-start.17 = (bf16[64,1280]{1,0:T(8,128)(2,1)S(1)}, bf16[64,1280]{1,0:T(8,128)(2,1)S(1)}, u32[]{:S(2)}, u32[]{:S(2)}) collective-permute-start(bf16[64,1280]{1,0:T(8,128)(2,1)S(1)} %get-tuple-element.53), channel_id=1, source_target_pairs={{0,3},{1,0},{2,1},{3,2},{4,7},{5,4},{6,5},{7,6},{8,11},{9,8},{10,9... | collective-permute-start | bytes 491528 | tf_op jit(solution)/shard_map/ppermute | solution.py:29
  67.5 10.7 %collective-permute-start.11 = (bf16[64,1024]{1,0:T(8,128)(2,1)S(1)}, bf16[64,1024]{1,0:T(8,128)(2,1)S(1)}, u32[]{:S(2)}, u32[]{:S(2)}) collective-permute-start(bf16[64,1024]{1,0:T(8,128)(2,1)S(1)} %get-tuple-element.48), channel_id=1, source_target_pairs={{0,3},{1,0},{2,1},{3,2},{4,7},{5,4},{6,5},{7,6},{8,11},{9,8},{10,9... | collective-permute-start | bytes 393224 | tf_op jit(solution)/shard_map/ppermute | solution.py:29
  68.5 9.8 %collective-permute-start.9 = (bf16[64,1024]{1,0:T(8,128)(2,1)S(1)}, bf16[64,1024]{1,0:T(8,128)(2,1)S(1)}, u32[]{:S(2)}, u32[]{:S(2)}) collective-permute-start(bf16[64,1024]{1,0:T(8,128)(2,1)S(1)} %get-tuple-element.46), channel_id=1, source_target_pairs={{0,1},{1,2},{2,3},{3,0},{4,5},{5,6},{6,7},{7,4},{8,9},{9,10},{10,1... | collective-permute-start | bytes 393224 | tf_op jit(solution)/shard_map/ppermute | solution.py:29
  114.4 10.6 %collective-permute-start.18 = (bf16[128,1152]{1,0:T(8,128)(2,1)S(1)}, bf16[128,1152]{1,0:T(8,128)(2,1)S(1)}, u32[]{:S(2)}, u32[]{:S(2)}) collective-permute-start(bf16[128,1152]{1,0:T(8,128)(2,1)S(1)} %bitcast.14), channel_id=1, source_target_pairs={{0,1},{1,2},{2,3},{3,0},{4,5},{5,6},{6,7},{7,4},{8,9},{9,10},{10,1... | collective-permute-start | bytes 884744 | tf_op jit(solution)/shard_map/ppermute | solution.py:29
  115.7 14.9 %collective-permute-start.19 = (bf16[128,1152]{1,0:T(8,128)(2,1)S(1)}, bf16[128,1152]{1,0:T(8,128)(2,1)S(1)}, u32[]{:S(2)}, u32[]{:S(2)}) collective-permute-start(bf16[128,1152]{1,0:T(8,128)(2,1)S(1)} %bitcast.15), channel_id=1, source_target_pairs={{0,2},{1,3},{2,0},{3,1},{4,6},{5,7},{6,4},{7,5},{8,10},{9,11},{10,... | collective-permute-start | bytes 884744 | tf_op jit(solution)/shard_map/ppermute | solution.py:29
  119.6 11.0 %collective-permute-start.20 = (bf16[128,1152]{1,0:T(8,128)(2,1)S(1)}, bf16[128,1152]{1,0:T(8,128)(2,1)S(1)}, u32[]{:S(2)}, u32[]{:S(2)}) collective-permute-start(bf16[128,1152]{1,0:T(8,128)(2,1)S(1)} %bitcast.16), channel_id=1, source_target_pairs={{0,3},{1,0},{2,1},{3,2},{4,7},{5,4},{6,5},{7,6},{8,11},{9,8},{10,9... | collective-permute-start | bytes 884744 | tf_op jit(solution)/shard_map/ppermute | solution.py:29
  (3 other events, 54.7 us)

commit v5 on v4

--- a/solution.py
+++ b/solution.py
@@ -176,40 +176,41 @@
     lax.fori_loop(0, out.shape[1] // 256, step, 0)
 
 
-def middle_kernel(stacks, partial, w2, out):
-    add_products(out, partial, ((stacks.at[2], w2),))
-
-
-def strand_kernel(stacks, partial, w3, ups, taps, out, grads, sums, values, mixes):
+def middle_kernel(stacks, partial, w, out, *, start):
+    add_products(out, partial, ((stacks.at[2, :, start : start + w.shape[0]], w),))
+
+
+def strand_kernel(stacks, partial, w3, w3_rest, ups, taps, grads, ahead, behind, sums, values, mixes, *, first):
     total = stacks.shape[1] // 2
     rows = total - 2 * EDGE
-    units = w3.shape[1]
+    units = sums.shape[1]
+    split = w3.shape[0]
     count = units // LANES
+    turn = turning(LANES)
 
     def project(at, _):
-        cols = pl.ds(pl.multiple_of(at * 256, 256), 256)
-        acc = partial[:, cols] + dot(stacks[3], w3[:, cols])
+        near = pl.ds(pl.multiple_of(at * 256, 256), 256)
+        cols = pl.ds(pl.multiple_of(first + at * 256, 256), 256)
+        acc = partial[:, cols] + dot(stacks[3, :, :split], w3[:, cols]) + dot(stacks[3, :, split:], w3_rest[:, cols])
         acc = acc.astype(jnp.bfloat16).astype(jnp.float32)
         for way in range(2):
             base = way * total
             halo = 2 * rows + way * 2 * EDGE
-            values[base : base + EDGE, cols] = acc[halo : halo + EDGE]
-            values[base + EDGE : base + EDGE + rows, cols] = acc[way * rows : (way + 1) * rows]
-            values[base + EDGE + rows : base + total, cols] = acc[halo + EDGE : halo + 2 * EDGE]
+            values[base : base + EDGE, near] = acc[halo : halo + EDGE]
+            values[base + EDGE : base + EDGE + rows, near] = acc[way * rows : (way + 1) * rows]
+            values[base + EDGE + rows : base + total, near] = acc[halo + EDGE : halo + 2 * EDGE]
         return 0
 
     lax.fori_loop(0, units // 256, project, 0)
     sums[...] = jnp.zeros(sums.shape, jnp.float32)
-    turn = turning(LANES)
 
     def work(at, _):
-        outs = []
+        near = pl.ds(pl.multiple_of(at * LANES, LANES), LANES)
+        cols = pl.ds(pl.multiple_of(first + at * LANES, LANES), LANES)
         for way in range(2):
-            block = at if way == 0 else count - 1 - at
-            cols = pl.ds(pl.multiple_of(block * LANES, LANES), LANES)
             base = way * total
             places = [base + EDGE + (tap - REACH if way == 0 else REACH - tap) for tap in range(TAPS)]
-            linear = values[base : base + total, cols]
+            linear = values[base : base + total, near]
             logistic = jax.nn.sigmoid(linear)
             gating = linear * logistic
             up = ups[base : base + total, cols]
@@ -221,43 +222,66 @@
             ]
             mixing = jnp.zeros((rows, LANES), jnp.float32)
             for tap in range(TAPS):
-                moved = values[places[tap] : places[tap] + rows, cols]
+                moved = values[places[tap] : places[tap] + rows, near]
                 mixing = mixing + taps[tap : tap + 1, cols] * moved
-                sums[tap : tap + 1, cols] += jnp.sum(grad_mix * moved, axis=0, keepdims=True)
-            outs.append(mixing * gating)
+                sums[tap : tap + 1, near] += jnp.sum(grad_mix * moved, axis=0, keepdims=True)
+            strand_out = mixing * gating
             acc = up * mixing * logistic * (1.0 + linear * (1.0 - logistic))
             for tap in range(TAPS):
                 lower = 2 * EDGE - places[tap] + base
                 acc = acc + taps[tap : tap + 1, cols] * mixes[way, lower : lower + rows]
-            grads[way * rows : (way + 1) * rows, cols] = acc.astype(jnp.bfloat16)
-        out[:, pl.ds(pl.multiple_of(at * LANES, LANES), LANES)] = (
-            outs[0] + dot(outs[1].astype(jnp.bfloat16), turn)
-        ).astype(jnp.bfloat16)
+            grads[way * rows : (way + 1) * rows, near] = acc.astype(jnp.bfloat16)
+            if way == 0:
+                ahead[:, near] = strand_out
+            else:
+                far = pl.ds(pl.multiple_of((count - 1 - at) * LANES, LANES), LANES)
+                behind[:, far] = dot(strand_out.astype(jnp.bfloat16), turn)
         return 0
 
     lax.fori_loop(0, count, work, 0)
 
 
-def product_kernel(columns, grads, out, *, block, start):
-    out[...] = dot(columns[block, start : start + out.shape[0]], grads[...]).astype(jnp.bfloat16)
-
-
-def later_product_kernel(columns, grads, earlier, out, *, block, start):
-    product_kernel(columns, grads, out, block=block, start=start)
-
-
-def side_kernel(columns, grads, came, out, *, block, start):
-    own = dot(columns[block, start : start + out.shape[0]], grads[...])
-    out[...] = (own + came[...].astype(jnp.float32)).astype(jnp.bfloat16)
-
-
-def back_kernel(place, grads, hot, sums, w0, w1, w2, w3, later, out, packed, table, backs):
+def product_kernel(columns, *refs, block):
+    grads, out = refs[:-1], refs[-1]
+    start = 0
+    for part in grads:
+        stop = start + part.shape[1]
+        out[:, start:stop] = dot(columns[block], part[...]).astype(out.dtype)
+        start = stop
+
+
+def merge_kernel(columns, came, *refs, block):
+    grads, out = refs[:-1], refs[-1]
+    start = 0
+    for part in grads:
+        stop = start + part.shape[1]
+        own = dot(columns[block], part[...])
+        out[:, start:stop] = (own + came[:, start:stop].astype(jnp.float32)).astype(jnp.bfloat16)
+        start = stop
+
+
+def back_kernel(place, hot, w0, w1, w2, w2_rest, w3, w3_rest, later, *refs):
+    parts, (out, block, packed, table, backs, grads, sums) = refs[:12], refs[12:]
     rows = out.shape[0]
     width = w0.shape[0]
     turn = turning(256)
     dims = (((1,), (1,)), ((), ()))
-    for r, w in enumerate((w0, w1, w2, w3)):
-        backs[r] = lax.dot_general(grads[...], w[...], dims, preferred_element_type=jnp.float32)
+    start = 0
+    for at in range(3):
+        part, part_sums = parts[at * 4], parts[at * 4 + 3]
+        stop = start + part.shape[1]
+        grads[:, start:stop] = part[...]
+        sums[:, start:stop] = part_sums[...]
+        start = stop
+    forward = jnp.concatenate([parts[at * 4 + 1][...] for at in range(3)], axis=1)
+    backward = jnp.concatenate([parts[at * 4 + 2][...] for at in (2, 1, 0)], axis=1)
+    block[...] = (forward + backward).astype(jnp.bfloat16)
+    for r, group in enumerate(((w0,), (w1,), (w2, w2_rest), (w3, w3_rest))):
+        size = width // len(group)
+        for at, w in enumerate(group):
+            backs[r, :, at * size : (at + 1) * size] = lax.dot_general(
+                grads[...], w[...], dims, preferred_element_type=jnp.float32
+            )
     for r in range(4):
         whole = backs[r, :rows] + turned(backs[3 - r, rows:].astype(jnp.bfloat16), turn)
         cols = pl.ds(pl.multiple_of((place[0] ^ r) * width, width), width)
@@ -273,44 +297,41 @@
         packed[at * PACK + 24 : at * PACK + 32] = jnp.zeros((8, LANES), jnp.float32)
 
 
-def block_kernel(place, columns, grads, mate, came, *refs, start):
+def block_kernel(place, columns, mate, came, *refs, parts):
+    grads, refs = refs[:parts], refs[parts:]
     wide = len(refs) > 5
-    own = refs[-1]
     if wide:
-        packed, packed_came, outs, first, second = refs[0], refs[1], refs[2:6], refs[6], refs[7]
+        packed, packed_came, outs, own, extra = refs[0], refs[1], refs[2:6], refs[6], refs[7]
         whole = packed[...] + packed_came[...]
+        half = whole.shape[0]
         head = whole.astype(jnp.bfloat16).astype(jnp.float32)
         rest = whole - head
         low = low_lanes(whole.shape)
-        first[...] = jnp.where(low, head, pltpu.roll(rest, LANES // 2, 1))
-        second[...] = jnp.where(low, pltpu.roll(head, LANES // 2, 1), rest)
+        extra[:half] = jnp.where(low, head, pltpu.roll(rest, LANES // 2, 1))
+        extra[half:] = jnp.where(low, pltpu.roll(head, LANES // 2, 1), rest)
     else:
-        outs = refs[:4]
+        outs, own = refs[:4], refs[4]
     rows = outs[0].shape[0]
-    units = grads.shape[1]
-    own[...] = dot(columns[0, start : start + 4 * rows], grads[...])
+    units = own.shape[1]
+    product_kernel(columns, *grads, own, block=0)
     for step, out in enumerate(outs):
-        at = pl.multiple_of((place[1] + step) % 4 * rows, rows)
-        here = pl.ds(at, rows)
-        out[:, :units] = added(own[here], mate[pl.ds(start + at, rows)], came[here]).astype(jnp.bfloat16)
+        here = pl.ds(pl.multiple_of((place[1] + step) % 4 * rows, rows), rows)
+        out[:, :units] = added(own[here], mate[here], came[here]).astype(jnp.bfloat16)
         if wide:
-            out[:, units : units + LANES] = first[here].astype(jnp.bfloat16)
-            out[:, units + LANES :] = second[here].astype(jnp.bfloat16)
+            out[:, units:] = extra[here].astype(jnp.bfloat16)
 
 
 def quarter_kernel(*refs):
     head, tail, out = refs[:4], refs[4:8], refs[8]
     rows, units = head[0].shape
-    size = 16
+    size = 32
 
     def step(at, _):
         here = pl.ds(pl.multiple_of(at * size, size), size)
-        there = pl.ds(pl.multiple_of(rows + at * size, size), size)
         out[here, :units] = added(*[part[here] for part in head]).astype(jnp.bfloat16)
-        out[there, :units] = added(*[part[here, :units] for part in tail]).astype(jnp.bfloat16)
-        for goal, start in ((here, units), (there, units + LANES)):
-            cells = added(*[part[here, start : start + LANES] for part in tail])
-            out[goal, units:] = paired(cells).astype(jnp.bfloat16)
+        cells = added(*[part[here] for part in tail])
+        out[here, units : 2 * units] = cells[:, :units].astype(jnp.bfloat16)
+        out[here, 2 * units :] = paired(cells[:, units:]).astype(jnp.bfloat16)
         return 0
 
     lax.fori_loop(0, rows // size, step, 0)
@@ -329,15 +350,12 @@
 
 
 def final_kernel(place, q0, q1, q2, q3, weight_out, taps_out, table_out, packed, *, factor):
-    rows = q0.shape[0] // 2
+    rows = q0.shape[0]
     units = weight_out.shape[1]
     for step, part in enumerate((q0, q1, q2, q3)):
-        at = pl.multiple_of((place[1] + 4 - step) % 4 * rows, rows)
-        for half in range(2):
-            here = slice(half * rows, (half + 1) * rows)
-            there = pl.ds(half * 4 * rows + at, rows)
-            weight_out[there] = part[here, :units].astype(jnp.float32) * factor
-            packed[there] = part[here, units:].astype(jnp.float32)
+        there = pl.ds(pl.multiple_of((place[1] + 4 - step) % 4 * rows, rows), rows)
+        weight_out[there] = part[:, :units].astype(jnp.float32) * factor
+        packed[there] = part[:, units:].astype(jnp.float32)
     cells = packed[...]
     whole = cells + pltpu.roll(cells, LANES // 2, 1)
     half = whole.shape[0] // 2
@@ -384,8 +402,10 @@
     total = rows + 2 * EDGE
     me = 2 * lax.axis_index("xl") + lax.axis_index("c")
     place = jnp.stack([me, lax.axis_index("y")]).astype(jnp.int32)
-    weights = [weight, swap_core(weight), side(weight)]
-    weights.append(swap_core(weights[2]))
+    half = width // 2
+    w_core = swap_core(weight)
+    w_side = [side(weight[at * half : (at + 1) * half]) for at in range(2)]
+    w_last = [swap_core(w_side[at]) for at in range(2)]
     top = pl.BlockSpec((EDGE, features), lambda at: (0, 0))
     bottom = pl.BlockSpec((EDGE, features), lambda at: (rows // EDGE - 1, 0))
     up_top = pl.BlockSpec((EDGE, units), lambda at: (0, 0))
@@ -441,76 +461,103 @@
         up_centre,
         before,
         after,
-        weights[0],
-        weights[1],
+        weight,
+        w_core,
         scalar=True,
     )
-    partial = call(middle_kernel, wide, stacks, partial, weights[2])
-    block_result, grads, sums = call(
-        strand_kernel,
-        (array((rows, units)), array((2 * rows, units)), array((8, units), jnp.float32)),
-        stacks,
-        partial,
-        weights[3],
-        ups,
-        taps,
-        scratch=(pltpu.VMEM((2 * total, units), jnp.float32), pltpu.VMEM((2, total, LANES), jnp.float32)),
-    )
-
-    half = width // 2
-    chunk = array((half, units))
-    goes = call(product_kernel, chunk, columns, grads, block=3, start=0)
-    goes = [goes, call(later_product_kernel, chunk, columns, grads, goes, unread=(2,), block=3, start=half)]
-    mate = call(later_product_kernel, array((width, units)), columns, grads, goes[1], unread=(2,), block=1, start=0)
-    came = [swap_core(goes[at]) for at in range(2)]
-    mate = swap_core(mate)
-    sides = [call(side_kernel, chunk, columns, grads, came[at], block=2, start=at * half) for at in range(2)]
-    came = [side(sides[at]) for at in range(2)]
-    grad_hidden, packed = call(
+    for at in range(2):
+        partial = call(middle_kernel, wide, stacks, partial, w_side[at], start=at * half)
+    ends = (0, units // 2, units // 4 * 3, units)
+    parts = []
+    for at in range(3):
+        size = ends[at + 1] - ends[at]
+        parts.append(
+            call(
+                strand_kernel,
+                (
+                    array((2 * rows, size)),
+                    array((rows, size), jnp.float32),
+                    array((rows, size), jnp.float32),
+                    array((8, size), jnp.float32),
+                ),
+                stacks,
+                partial,
+                *w_last,
+                ups,
+                taps,
+                scratch=(pltpu.VMEM((2 * total, size), jnp.float32), pltpu.VMEM((2, total, LANES), jnp.float32)),
+                first=ends[at],
+            )
+        )
+    grads = [[parts[0][0]], [parts[1][0], parts[2][0]]]
+    chunk = array((width, units // 2))
+    came = []
+    mates = []
+    for at in range(2):
+        goes = call(product_kernel, chunk, columns, *grads[at], block=3)
+        goes = swap_core(goes)
+        merged = call(merge_kernel, chunk, columns, goes, *grads[at], block=2)
+        came.append(side(merged))
+        mate = call(product_kernel, chunk, columns, *grads[at], block=1)
+        mates.append(swap_core(mate))
+    grad_hidden, block_result, packed = call(
         back_kernel,
-        (array((rows, features)), array((units // LANES * PACK, LANES), jnp.float32)),
+        (
+            array((rows, features)),
+            array((rows, units)),
+            array((units // LANES * PACK, LANES), jnp.float32),
+        ),
         place,
-        grads,
         hot,
-        sums,
-        *weights,
-        sides[1],
+        weight,
+        w_core,
+        *w_side,
+        *w_last,
+        merged,
+        *[cells for part in parts for cells in part],
         scalar=True,
         unread=(8,),
-        scratch=(pltpu.VMEM((16, features), jnp.float32), pltpu.VMEM((4, 2 * rows, width), jnp.float32)),
+        scratch=(
+            pltpu.VMEM((16, features), jnp.float32),
+            pltpu.VMEM((4, 2 * rows, width), jnp.float32),
+            pltpu.VMEM((2 * rows, units), jnp.bfloat16),
+            pltpu.VMEM((8, units), jnp.float32),
+        ),
     )
     packed = packed + swap_core(packed)
-    part = half // 4
+    packed_came = side(packed)
+    part = width // 4
+    own = pltpu.VMEM(chunk.shape, jnp.float32)
     head = call(
         block_kernel,
-        (array((part, units)),) * 4,
+        (array((part, units // 2)),) * 4,
         place,
         columns,
-        grads,
-        mate,
+        mates[0],
         came[0],
+        *grads[0],
         scalar=True,
-        scratch=(pltpu.VMEM((half, units), jnp.float32),),
-        start=0,
+        scratch=(own,),
+        parts=1,
     )
     head = [head[0]] + [along_y(head[step], step) for step in (1, 2, 3)]
     tail = call(
         block_kernel,
-        (array((part, units + 2 * LANES)),) * 4,
+        (array((part, units // 2 + LANES)),) * 4,
         place,
         columns,
-        grads,
-        mate,
+        mates[1],
         came[1],
+        *grads[1],
         packed,
-        side(packed),
+        packed_came,
         scalar=True,
-        scratch=(pltpu.VMEM(packed.shape, jnp.float32),) * 2 + (pltpu.VMEM((half, units), jnp.float32),),
-        start=half,
+        scratch=(own, pltpu.VMEM((width, LANES), jnp.float32)),
+        parts=2,
     )
     tail = [tail[0]] + [along_y(tail[step], step) for step in (1, 2, 3)]
-    quarter = call(quarter_kernel, array((2 * part, units + LANES)), *head, *tail)
-    pieces = quarter.reshape(16, part // 8, -1)
+    quarter = call(quarter_kernel, array((part, units + LANES)), *head, *tail)
+    pieces = quarter.reshape(16, part // 16, -1)
     pieces = lax.all_to_all(pieces, ("xh", "z"), split_axis=0, concat_axis=0, tiled=True)
     pieces = call(piece_kernel, array(pieces.shape), pieces)
     pieces = lax.all_to_all(pieces, ("xh", "z"), split_axis=0, concat_axis=0, tiled=True)

time: 133 us -> 136 us (1.023)
  starting transfers between devices: 27.8 us -> 30.1 us
  local copies, waits for them, and re-layouts: 0.02 us -> 1.95 us
    ppermute x21 -> x24, starting transfers between devices: 27.8 us -> 30.1 us  [shift(): return lax.ppermute(cells, axes if len(axes) > 1 else axes[0], pairs)]
    ppermute x21 -> x24, waiting for transfers between devices: 42.1 us -> 41 us  [shift(): return lax.ppermute(cells, axes if len(axes) > 1 else axes[0], pairs)]
    pallas_call x15 -> x19, Pallas kernels: 24.6 us -> 23.6 us  [call(): pl.pallas_call(functools.partial(kernel, **fixed), out_shape=outs, in_spe...]
  transfers between devices with their start and end apart: 21 -> 24, of which waited for: 8 -> 9; matrix products, arithmetic and copies ran while one was open for 0% -> 1% of each run, Pallas kernels for 12% -> 14%
where the time goes in v5:
time: 136 us
  waiting for transfers between devices  41 us (30%)
  blocking collectives  36.5 us (27%)
  starting transfers between devices  30.1 us (22%)
  Pallas kernels  25.3 us (19%)
  local copies, waits for them, and re-layouts  1.95 us (1%)
    ppermute x24, waiting for transfers between devices, shift(): return lax.ppermute(cells, axes if len(axes) > 1 else axes[0], pairs)  41 us
    all_to_all x2, blocking collectives, step(): lax.all_to_all(pieces, ('xh', 'z'), split_axis=0, concat_axis=0, tiled=True)  36.5 us
    ppermute x24, starting transfers between devices, shift(): return lax.ppermute(cells, axes if len(axes) > 1 else axes[0], pairs)  30.1 us
    pallas_call x19, Pallas kernels, call(): pl.pallas_call(functools.partial(kernel, **fixed), out_shape=outs, in_spe...  23.6 us
  transfers between devices with their start and end apart: 24, of which 9 were waited for; matrix products, arithmetic and copies ran while one was open for 1% of the time, Pallas kernels for 14%

profile of v5, /device:TPU:2, one launch (start us, length us, event | category | flops | bytes accessed | tf_op | source)
XLA Modules:
  0.0 135.9 jit_solution(8908700837550878931)
XLA Ops:
  2.1 1.6 %collective-permute-start.1 = (bf16[256,1024]{1,0:T(8,128)(2,1)S(1)}, bf16[256,1024]{1,0:T(8,128)(2,1)S(1)}, u32[]{:S(2)}, u32[]{:S(2)}) collective-permute-start(bf16[256,1024]{1,0:T(8,128)(2,1)S(1)} %get-tuple-element.78), channel_id=1, source_target_pairs={{0,128},{32,160},{64,224},{96,192},{128,32},{160,0},{192,64},{224,... | collective-permute-start | bytes 1572872 | tf_op jit(solution)/shard_map/ppermute | solution.py:29
  4.8 6.7 %collective-permute-done.1.w.w2 = bf16[256,1024]{1,0:T(8,128)(2,1)S(1)} collective-permute-done((bf16[256,1024]{1,0:T(8,128)(2,1)S(1)}, bf16[256,1024]{1,0:T(8,128)(2,1)S(1)}, u32[]{:S(2)}, u32[]{:S(2)}) %collective-permute-start.1) | collective-permute-done | bytes 524320 | tf_op jit(solution)/shard_map/ppermute | solution.py:29
  11.5 5.7 %collective-permute-done.2.w.w2_rest = bf16[256,1024]{1,0:T(8,128)(2,1)} collective-permute-done((bf16[256,1024]{1,0:T(8,128)(2,1)S(1)}, bf16[256,1024]{1,0:T(8,128)(2,1)}, u32[]{:S(2)}, u32[]{:S(2)}) %collective-permute-start.2) | collective-permute-done | bytes 524320 | tf_op jit(solution)/shard_map/ppermute | solution.py:29
  17.3 1.7 %shard_map.102 = (bf16[8,3072]{1,0:T(8,128)(2,1)}, bf16[8,3072]{1,0:T(8,128)(2,1)}) custom-call(s32[1,128]{1,0:T(1,128)} %codes.3, bf16[128,2048]{1,0:T(8,128)(2,1)} %bitcast.8, bf16[128,2048]{1,0:T(8,128)(2,1)} %bitcast.9, bf16[128,1024]{1,0:T(8,128)(2,1)} %bitcast.11, bf16[128,1024]{1,0:T(8,128)(2,1)} %bitcast.12, f32[5,2048]{1,0:T(8,128)} %table.1), custom_call_target="tpu_custom_call" | custom-call | tf_op jit(solution)/shard_map/pallas_call | solution.py:414
  19.0 3.2 %collective-permute-start.5 = (bf16[8,3072]{1,0:T(8,128)(2,1)}, bf16[8,3072]{1,0:T(8,128)(2,1)S(1)}, u32[]{:S(2)}, u32[]{:S(2)}) collective-permute-start(bf16[8,3072]{1,0:T(8,128)(2,1)} %get-tuple-element.45), channel_id=1, source_target_pairs={{0,1},{1,2},{2,3},{3,4},{4,5},{5,6},{6,7},{7,8},{8,9},{9,10},{10,1... | collective-permute-start | bytes 147464 | tf_op jit(solution)/shard_map/ppermute | solution.py:29
  24.3 1.7 %shard_map.101 = (bf16[4,256,512]{2,1,0:T(8,128)(2,1)S(1)}, bf16[4,512,256]{2,1,0:T(8,128)(2,1)S(1)}, f32[256,1024]{1,0:T(8,128)S(1)}, f32[7,1024]{1,0:T(8,128)S(1)}, bf16[16,384]{1,0:T(8,128)(2,1)S(1)}) custom-call(s32[2]{0:T(128)S(1)} %pad_add_fusion.place, s32[1,128]{1,0:T(1,128)S(1)} %copy-done.5, f32[7,1024]{1,0:T(8,128)S(1)} %copy-done.4, ...), custom_call_target="tpu_custom_call" | custom-call | tf_op jit(solution)/shard_map/pallas_call | solution.py:380
  25.9 2.6 %collective-permute-done.6.after = bf16[8,3072]{1,0:T(8,128)(2,1)} collective-permute-done((bf16[8,3072]{1,0:T(8,128)(2,1)}, bf16[8,3072]{1,0:T(8,128)(2,1)}, u32[]{:S(2)}, u32[]{:S(2)}) %collective-permute-start.6) | collective-permute-done | bytes 49184 | tf_op jit(solution)/shard_map/ppermute | solution.py:29
  28.5 3.0 %shard_map.103 = (bf16[4,288,512]{2,1,0:T(8,128)(2,1)S(1)}, f32[288,1024]{1,0:T(8,128)S(1)}, f32[288,1024]{1,0:T(8,128)S(1)}) custom-call(s32[2]{0:T(128)S(1)} %pad_add_fusion.place, bf16[4,256,512]{2,1,0:T(8,128)(2,1)S(1)} %get-tuple-element.43.centre, f32[256,1024]{1,0:T(8,128)S(1)} %get-tuple-element.44.up_centre, ...), custom_call_target="tpu_custom_call" | custom-call | tf_op jit(solution)/shard_map/pallas_call | solution.py:380
  32.3 1.9 %shard_map.105.partial = f32[288,1024]{1,0:T(8,128)S(1)} custom-call(bf16[4,288,512]{2,1,0:T(8,128)(2,1)S(1)} %get-tuple-element.47.stacks, f32[288,1024]{1,0:T(8,128)S(1)} %shard_map.104.partial, bf16[256,1024]{1,0:T(8,128)(2,1)} %collective-permute-done.2.w.w2_rest), custom_call_target="tpu_custom_call" | custom-call | tf_op jit(solution)/shard_map/pallas_call | solution.py:380
  34.2 2.7 %shard_map.110 = (bf16[256,512]{1,0:T(8,128)(2,1)S(1)}, f32[128,512]{1,0:T(8,128)S(1)}, f32[128,512]{1,0:T(8,128)S(1)}, f32[8,512]{1,0:T(8,128)S(1)}) custom-call(bf16[4,288,512]{2,1,0:T(8,128)(2,1)S(1)} %get-tuple-element.47.stacks, f32[288,1024]{1,0:T(8,128)S(1)} %shard_map.105.partial, bf16[256,1024]{1,0:T(8,128)(2,1)S(1)} %collective-permute-done.3.w3, ...), custom_call_target="tpu_custom_call" | custom-call | tf_op jit(solution)/shard_map/pallas_call | solution.py:380
  41.6 7.8 %collective-permute-start.10 = (bf16[512,512]{1,0:T(8,128)(2,1)S(1)}, bf16[512,512]{1,0:T(8,128)(2,1)S(1)}, u32[]{:S(2)}, u32[]{:S(2)}) collective-permute-start(bf16[512,512]{1,0:T(8,128)(2,1)S(1)} %shard_map.114), channel_id=1, source_target_pairs={{0,128},{32,160},{64,224},{96,192},{128,32},{160,0},{192,64},{224,... | collective-permute-start | bytes 1572872 | tf_op jit(solution)/shard_map/ppermute | solution.py:29
  51.2 4.3 %shard_map.111 = (bf16[128,2048]{1,0:T(8,128)(2,1)}, bf16[128,1024]{1,0:T(8,128)(2,1)}, f32[256,128]{1,0:T(8,128)S(1)}) custom-call(s32[2]{0:T(128)S(1)} %pad_add_fusion.place, bf16[16,384]{1,0:T(8,128)(2,1)S(1)} %get-tuple-element.41.hot, bf16[512,1024]{1,0:T(8,128)(2,1)S(1)} %copy-done, bf16[512,1024]{1,0:T(8,128)(2,1)} %collective-permute-done.w1, ...), custom_call_target="tpu_custom_call" | custom-call | tf_op jit(solution)/shard_map/pallas_call | solution.py:380
  59.3 3.8 %collective-permute-done.17.refs_3_ = f32[256,128]{1,0:T(8,128)S(1)} collective-permute-done((f32[256,128]{1,0:T(8,128)S(1)}, f32[256,128]{1,0:T(8,128)S(1)}, u32[]{:S(2)}, u32[]{:S(2)}) %collective-permute-start.17) | collective-permute-done | bytes 131104 | tf_op jit(solution)/shard_map/ppermute | solution.py:29
  64.3 1.4 %collective-permute-start.19 = (bf16[128,640]{1,0:T(8,128)(2,1)S(1)}, bf16[128,640]{1,0:T(8,128)(2,1)S(1)}, u32[]{:S(2)}, u32[]{:S(2)}) collective-permute-start(bf16[128,640]{1,0:T(8,128)(2,1)S(1)} %get-tuple-element.72), channel_id=1, source_target_pairs={{0,2},{1,3},{2,0},{3,1},{4,6},{5,7},{6,4},{7,5},{8,10},{9,11},{10,... | collective-permute-start | bytes 491528 | tf_op jit(solution)/shard_map/ppermute | solution.py:29
  65.6 1.8 %collective-permute-start.20 = (bf16[128,640]{1,0:T(8,128)(2,1)S(1)}, bf16[128,640]{1,0:T(8,128)(2,1)S(1)}, u32[]{:S(2)}, u32[]{:S(2)}) collective-permute-start(bf16[128,640]{1,0:T(8,128)(2,1)S(1)} %get-tuple-element.73), channel_id=1, source_target_pairs={{0,3},{1,0},{2,1},{3,2},{4,7},{5,4},{6,5},{7,6},{8,11},{9,8},{10,9... | collective-permute-start | bytes 491528 | tf_op jit(solution)/shard_map/ppermute | solution.py:29
  67.5 2.9 %collective-permute-start.12 = (bf16[128,512]{1,0:T(8,128)(2,1)S(1)}, bf16[128,512]{1,0:T(8,128)(2,1)S(1)}, u32[]{:S(2)}, u32[]{:S(2)}) collective-permute-start(bf16[128,512]{1,0:T(8,128)(2,1)S(1)} %get-tuple-element.67), channel_id=1, source_target_pairs={{0,2},{1,3},{2,0},{3,1},{4,6},{5,7},{6,4},{7,5},{8,10},{9,11},{10,... | collective-permute-start | bytes 393224 | tf_op jit(solution)/shard_map/ppermute | solution.py:29
  71.0 4.7 %collective-permute-done.12.refs_2_ = bf16[128,512]{1,0:T(8,128)(2,1)S(1)} collective-permute-done((bf16[128,512]{1,0:T(8,128)(2,1)S(1)}, bf16[128,512]{1,0:T(8,128)(2,1)S(1)}, u32[]{:S(2)}, u32[]{:S(2)}) %collective-permute-start.12) | collective-permute-done | bytes 131104 | tf_op jit(solution)/shard_map/ppermute | solution.py:29
  75.8 5.4 %collective-permute-done.13.refs_3_ = bf16[128,512]{1,0:T(8,128)(2,1)S(1)} collective-permute-done((bf16[128,512]{1,0:T(8,128)(2,1)S(1)}, bf16[128,512]{1,0:T(8,128)(2,1)S(1)}, u32[]{:S(2)}, u32[]{:S(2)}) %collective-permute-start.13) | collective-permute-done | bytes 131104 | tf_op jit(solution)/shard_map/ppermute | solution.py:29
  81.7 20.3 %all_to_all.10.parts = bf16[16,8,1152]{2,1,0:T(8,128)(2,1)S(1)} all-to-all(bf16[16,8,1152]{2,1,0:T(8,128)(2,1)S(1)} %bitcast.18), channel_id=1, replica_groups=mesh['xl'=2,'c'=2,'xh'=2,'z'=8,'y'=4] {'xh','z'}, dimensions={0} | all-to-all | bytes 589824 | tf_op jit(solution)/shard_map/all_to_all | solution.py:561
  102.1 16.2 %all_to_all.11 = bf16[16,8,1152]{2,1,0:T(8,128)(2,1)S(1)} all-to-all(bf16[16,8,1152]{2,1,0:T(8,128)(2,1)S(1)} %shard_map.119), channel_id=1, replica_groups=mesh['xl'=2,'c'=2,'xh'=2,'z'=8,'y'=4] {'xh','z'}, dimensions={0} | all-to-all | bytes 589824 | tf_op jit(solution)/shard_map/all_to_all | solution.py:563
  118.9 3.9 %collective-permute-start.22 = (bf16[128,1152]{1,0:T(8,128)(2,1)S(1)}, bf16[128,1152]{1,0:T(8,128)(2,1)S(1)}, u32[]{:S(2)}, u32[]{:S(2)}) collective-permute-start(bf16[128,1152]{1,0:T(8,128)(2,1)S(1)} %bitcast.15), channel_id=1, source_target_pairs={{0,2},{1,3},{2,0},{3,1},{4,6},{5,7},{6,4},{7,5},{8,10},{9,11},{10,... | collective-permute-start | bytes 884744 | tf_op jit(solution)/shard_map/ppermute | solution.py:29
  122.8 5.5 %collective-permute-done.21.q1 = bf16[128,1152]{1,0:T(8,128)(2,1)S(1)} collective-permute-done((bf16[128,1152]{1,0:T(8,128)(2,1)S(1)}, bf16[128,1152]{1,0:T(8,128)(2,1)S(1)}, u32[]{:S(2)}, u32[]{:S(2)}) %collective-permute-start.21) | collective-permute-done | bytes 294944 | tf_op jit(solution)/shard_map/ppermute | solution.py:29
  128.3 5.5 %collective-permute-done.22.q2 = bf16[128,1152]{1,0:T(8,128)(2,1)S(1)} collective-permute-done((bf16[128,1152]{1,0:T(8,128)(2,1)S(1)}, bf16[128,1152]{1,0:T(8,128)(2,1)S(1)}, u32[]{:S(2)}, u32[]{:S(2)}) %collective-permute-start.22) | collective-permute-done | bytes 294944 | tf_op jit(solution)/shard_map/ppermute | solution.py:29
  133.8 2.1 %shard_map.120 = (f32[512,1024]{1,0:T(8,128)}, f32[7,1024]{1,0:T(8,128)}, f32[5,2048]{1,0:T(8,128)}) custom-call(s32[2]{0:T(128)S(1)} %pad_add_fusion.place, bf16[128,1152]{1,0:T(8,128)(2,1)S(1)} %bitcast.17, bf16[128,1152]{1,0:T(8,128)(2,1)S(1)} %collective-permute-done.21.q1, bf16[128,1152]{1,0:T(8,128)(2,1)S(1)} %collective-permute-done.22.q2, ...), custom_call_target="tpu_custom_call" | custom-call | tf_op jit(solution)/shard_map/pallas_call | solution.py:380
  (61 shorter events, 18.5 us)
Async XLA Ops:
  0.6 27.9 %collective-permute-start = (bf16[512,1024]{1,0:T(8,128)(2,1)}, bf16[512,1024]{1,0:T(8,128)(2,1)}, u32[]{:S(2)}, u32[]{:S(2)}) collective-permute-start(bf16[512,1024]{1,0:T(8,128)(2,1)} %w0.3), channel_id=1, source_target_pairs={{0,64},{64,0},{1,65},{65,1},{2,66},{66,2},{3,67},{67,3},{4,68},{68... | collective-permute-start | bytes 3145736 | tf_op jit(solution)/shard_map/ppermute | solution.py:29
  2.1 9.5 %collective-permute-start.1 = (bf16[256,1024]{1,0:T(8,128)(2,1)S(1)}, bf16[256,1024]{1,0:T(8,128)(2,1)S(1)}, u32[]{:S(2)}, u32[]{:S(2)}) collective-permute-start(bf16[256,1024]{1,0:T(8,128)(2,1)S(1)} %get-tuple-element.78), channel_id=1, source_target_pairs={{0,128},{32,160},{64,224},{96,192},{128,32},{160,0},{192,64},{224,... | collective-permute-start | bytes 1572872 | tf_op jit(solution)/shard_map/ppermute | solution.py:29
  3.6 13.6 %collective-permute-start.2 = (bf16[256,1024]{1,0:T(8,128)(2,1)S(1)}, bf16[256,1024]{1,0:T(8,128)(2,1)}, u32[]{:S(2)}, u32[]{:S(2)}) collective-permute-start(bf16[256,1024]{1,0:T(8,128)(2,1)S(1)} %get-tuple-element.77), channel_id=1, source_target_pairs={{0,128},{32,160},{64,224},{96,192},{128,32},{160,0},{192,64},{224,... | collective-permute-start | bytes 1572872 | tf_op jit(solution)/shard_map/ppermute | solution.py:29
  11.5 22.6 %collective-permute-start.3 = (bf16[256,1024]{1,0:T(8,128)(2,1)S(1)}, bf16[256,1024]{1,0:T(8,128)(2,1)S(1)}, u32[]{:S(2)}, u32[]{:S(2)}) collective-permute-start(bf16[256,1024]{1,0:T(8,128)(2,1)S(1)} %collective-permute-done.1.w.w2), channel_id=1, source_target_pairs={{0,64},{64,0},{1,65},{65,1},{2,66},{66,2},{3,67},{67,3},{4,68},{68... | collective-permute-start | bytes 1572872 | tf_op jit(solution)/shard_map/ppermute | solution.py:29
  17.3 16.9 %collective-permute-start.4 = (bf16[256,1024]{1,0:T(8,128)(2,1)}, bf16[256,1024]{1,0:T(8,128)(2,1)S(1)}, u32[]{:S(2)}, u32[]{:S(2)}) collective-permute-start(bf16[256,1024]{1,0:T(8,128)(2,1)} %collective-permute-done.2.w.w2_rest), channel_id=1, source_target_pairs={{0,64},{64,0},{1,65},{65,1},{2,66},{66,2},{3,67},{67,3},{4,68},{68... | collective-permute-start | bytes 1572872 | tf_op jit(solution)/shard_map/ppermute | solution.py:29
  19.0 7.0 %collective-permute-start.5 = (bf16[8,3072]{1,0:T(8,128)(2,1)}, bf16[8,3072]{1,0:T(8,128)(2,1)S(1)}, u32[]{:S(2)}, u32[]{:S(2)}) collective-permute-start(bf16[8,3072]{1,0:T(8,128)(2,1)} %get-tuple-element.45), channel_id=1, source_target_pairs={{0,1},{1,2},{2,3},{3,4},{4,5},{5,6},{6,7},{7,8},{8,9},{9,10},{10,1... | collective-permute-start | bytes 147464 | tf_op jit(solution)/shard_map/ppermute | solution.py:29
  22.2 6.3 %collective-permute-start.6 = (bf16[8,3072]{1,0:T(8,128)(2,1)}, bf16[8,3072]{1,0:T(8,128)(2,1)}, u32[]{:S(2)}, u32[]{:S(2)}) collective-permute-start(bf16[8,3072]{1,0:T(8,128)(2,1)} %get-tuple-element.46), channel_id=1, source_target_pairs={{1,0},{2,1},{3,2},{4,3},{5,4},{6,5},{7,6},{8,7},{9,8},{10,9},{11,1... | collective-permute-start | bytes 147464 | tf_op jit(solution)/shard_map/ppermute | solution.py:29
  37.2 4.1 %collective-permute-start.9 = (bf16[512,512]{1,0:T(8,128)(2,1)S(1)}, bf16[512,512]{1,0:T(8,128)(2,1)S(1)}, u32[]{:S(2)}, u32[]{:S(2)}) collective-permute-start(bf16[512,512]{1,0:T(8,128)(2,1)S(1)} %shard_map.113), channel_id=1, source_target_pairs={{0,64},{64,0},{1,65},{65,1},{2,66},{66,2},{3,67},{67,3},{4,68},{68... | collective-permute-start | bytes 1572872 | tf_op jit(solution)/shard_map/ppermute | solution.py:29
  40.3 9.4 %collective-permute-start.7 = (bf16[512,512]{1,0:T(8,128)(2,1)S(1)}, bf16[512,512]{1,0:T(8,128)(2,1)S(1)}, u32[]{:S(2)}, u32[]{:S(2)}) collective-permute-start(bf16[512,512]{1,0:T(8,128)(2,1)S(1)} %shard_map.108), channel_id=1, source_target_pairs={{0,64},{64,0},{1,65},{65,1},{2,66},{66,2},{3,67},{67,3},{4,68},{68... | collective-permute-start | bytes 1572872 | tf_op jit(solution)/shard_map/ppermute | solution.py:29
  41.2 16.9 %collective-permute-start.8 = (bf16[512,512]{1,0:T(8,128)(2,1)S(1)}, bf16[512,512]{1,0:T(8,128)(2,1)S(1)}, u32[]{:S(2)}, u32[]{:S(2)}) collective-permute-start(bf16[512,512]{1,0:T(8,128)(2,1)S(1)} %shard_map.112), channel_id=1, source_target_pairs={{0,64},{64,0},{1,65},{65,1},{2,66},{66,2},{3,67},{67,3},{4,68},{68... | collective-permute-start | bytes 1572872 | tf_op jit(solution)/shard_map/ppermute | solution.py:29
  41.6 16.5 %collective-permute-start.10 = (bf16[512,512]{1,0:T(8,128)(2,1)S(1)}, bf16[512,512]{1,0:T(8,128)(2,1)S(1)}, u32[]{:S(2)}, u32[]{:S(2)}) collective-permute-start(bf16[512,512]{1,0:T(8,128)(2,1)S(1)} %shard_map.114), channel_id=1, source_target_pairs={{0,128},{32,160},{64,224},{96,192},{128,32},{160,0},{192,64},{224,... | collective-permute-start | bytes 1572872 | tf_op jit(solution)/shard_map/ppermute | solution.py:29
  49.7 9.6 %collective-permute-start.14 = (bf16[512,512]{1,0:T(8,128)(2,1)S(1)}, bf16[512,512]{1,0:T(8,128)(2,1)S(1)}, u32[]{:S(2)}, u32[]{:S(2)}) collective-permute-start(bf16[512,512]{1,0:T(8,128)(2,1)S(1)} %shard_map.116), channel_id=1, source_target_pairs={{0,64},{64,0},{1,65},{65,1},{2,66},{66,2},{3,67},{67,3},{4,68},{68... | collective-permute-start | bytes 1572872 | tf_op jit(solution)/shard_map/ppermute | solution.py:29
  50.1 13.0 %collective-permute-start.15 = (bf16[512,512]{1,0:T(8,128)(2,1)S(1)}, bf16[512,512]{1,0:T(8,128)(2,1)S(1)}, u32[]{:S(2)}, u32[]{:S(2)}) collective-permute-start(bf16[512,512]{1,0:T(8,128)(2,1)S(1)} %shard_map.109.later), channel_id=1, source_target_pairs={{0,128},{32,160},{64,224},{96,192},{128,32},{160,0},{192,64},{224,... | collective-permute-start | bytes 1572872 | tf_op jit(solution)/shard_map/ppermute | solution.py:29
  55.6 1.3 collective-permute-start.16
  56.9 6.2 %collective-permute-start.17 = (f32[256,128]{1,0:T(8,128)S(1)}, f32[256,128]{1,0:T(8,128)S(1)}, u32[]{:S(2)}, u32[]{:S(2)}) collective-permute-start(f32[256,128]{1,0:T(8,128)S(1)} %add.7.refs_2_), channel_id=1, source_target_pairs={{0,128},{32,160},{64,224},{96,192},{128,32},{160,0},{192,64},{224,... | collective-permute-start | bytes 393224 | tf_op jit(solution)/shard_map/ppermute | solution.py:29
  59.2 11.2 %collective-permute-start.11 = (bf16[128,512]{1,0:T(8,128)(2,1)S(1)}, bf16[128,512]{1,0:T(8,128)(2,1)S(1)}, u32[]{:S(2)}, u32[]{:S(2)}) collective-permute-start(bf16[128,512]{1,0:T(8,128)(2,1)S(1)} %get-tuple-element.66), channel_id=1, source_target_pairs={{0,1},{1,2},{2,3},{3,0},{4,5},{5,6},{6,7},{7,4},{8,9},{9,10},{10,1... | collective-permute-start | bytes 393224 | tf_op jit(solution)/shard_map/ppermute | solution.py:29
  64.2 17.0 %collective-permute-start.18 = (bf16[128,640]{1,0:T(8,128)(2,1)S(1)}, bf16[128,640]{1,0:T(8,128)(2,1)S(1)}, u32[]{:S(2)}, u32[]{:S(2)}) collective-permute-start(bf16[128,640]{1,0:T(8,128)(2,1)S(1)} %get-tuple-element.71), channel_id=1, source_target_pairs={{0,1},{1,2},{2,3},{3,0},{4,5},{5,6},{6,7},{7,4},{8,9},{9,10},{10,1... | collective-permute-start | bytes 491528 | tf_op jit(solution)/shard_map/ppermute | solution.py:29
  64.3 16.9 %collective-permute-start.19 = (bf16[128,640]{1,0:T(8,128)(2,1)S(1)}, bf16[128,640]{1,0:T(8,128)(2,1)S(1)}, u32[]{:S(2)}, u32[]{:S(2)}) collective-permute-start(bf16[128,640]{1,0:T(8,128)(2,1)S(1)} %get-tuple-element.72), channel_id=1, source_target_pairs={{0,2},{1,3},{2,0},{3,1},{4,6},{5,7},{6,4},{7,5},{8,10},{9,11},{10,... | collective-permute-start | bytes 491528 | tf_op jit(solution)/shard_map/ppermute | solution.py:29
  65.6 15.6 %collective-permute-start.20 = (bf16[128,640]{1,0:T(8,128)(2,1)S(1)}, bf16[128,640]{1,0:T(8,128)(2,1)S(1)}, u32[]{:S(2)}, u32[]{:S(2)}) collective-permute-start(bf16[128,640]{1,0:T(8,128)(2,1)S(1)} %get-tuple-element.73), channel_id=1, source_target_pairs={{0,3},{1,0},{2,1},{3,2},{4,7},{5,4},{6,5},{7,6},{8,11},{9,8},{10,9... | collective-permute-start | bytes 491528 | tf_op jit(solution)/shard_map/ppermute | solution.py:29
  67.5 8.3 %collective-permute-start.12 = (bf16[128,512]{1,0:T(8,128)(2,1)S(1)}, bf16[128,512]{1,0:T(8,128)(2,1)S(1)}, u32[]{:S(2)}, u32[]{:S(2)}) collective-permute-start(bf16[128,512]{1,0:T(8,128)(2,1)S(1)} %get-tuple-element.67), channel_id=1, source_target_pairs={{0,2},{1,3},{2,0},{3,1},{4,6},{5,7},{6,4},{7,5},{8,10},{9,11},{10,... | collective-permute-start | bytes 393224 | tf_op jit(solution)/shard_map/ppermute | solution.py:29
  70.4 10.8 %collective-permute-start.13 = (bf16[128,512]{1,0:T(8,128)(2,1)S(1)}, bf16[128,512]{1,0:T(8,128)(2,1)S(1)}, u32[]{:S(2)}, u32[]{:S(2)}) collective-permute-start(bf16[128,512]{1,0:T(8,128)(2,1)S(1)} %get-tuple-element.68), channel_id=1, source_target_pairs={{0,3},{1,0},{2,1},{3,2},{4,7},{5,4},{6,5},{7,6},{8,11},{9,8},{10,9... | collective-permute-start | bytes 393224 | tf_op jit(solution)/shard_map/ppermute | solution.py:29
  118.3 9.9 %collective-permute-start.21 = (bf16[128,1152]{1,0:T(8,128)(2,1)S(1)}, bf16[128,1152]{1,0:T(8,128)(2,1)S(1)}, u32[]{:S(2)}, u32[]{:S(2)}) collective-permute-start(bf16[128,1152]{1,0:T(8,128)(2,1)S(1)} %bitcast.14), channel_id=1, source_target_pairs={{0,1},{1,2},{2,3},{3,0},{4,5},{5,6},{6,7},{7,4},{8,9},{9,10},{10,1... | collective-permute-start | bytes 884744 | tf_op jit(solution)/shard_map/ppermute | solution.py:29
  118.9 14.9 %collective-permute-start.22 = (bf16[128,1152]{1,0:T(8,128)(2,1)S(1)}, bf16[128,1152]{1,0:T(8,128)(2,1)S(1)}, u32[]{:S(2)}, u32[]{:S(2)}) collective-permute-start(bf16[128,1152]{1,0:T(8,128)(2,1)S(1)} %bitcast.15), channel_id=1, source_target_pairs={{0,2},{1,3},{2,0},{3,1},{4,6},{5,7},{6,4},{7,5},{8,10},{9,11},{10,... | collective-permute-start | bytes 884744 | tf_op jit(solution)/shard_map/ppermute | solution.py:29
  122.8 11.0 %collective-permute-start.23 = (bf16[128,1152]{1,0:T(8,128)(2,1)S(1)}, bf16[128,1152]{1,0:T(8,128)(2,1)S(1)}, u32[]{:S(2)}, u32[]{:S(2)}) collective-permute-start(bf16[128,1152]{1,0:T(8,128)(2,1)S(1)} %bitcast.16), channel_id=1, source_target_pairs={{0,3},{1,0},{2,1},{3,2},{4,7},{5,4},{6,5},{7,6},{8,11},{9,8},{10,9... | collective-permute-start | bytes 884744 | tf_op jit(solution)/shard_map/ppermute | solution.py:29
  (6 other events, 98.2 us)

commit v6 on v5

--- a/solution.py
+++ b/solution.py
@@ -176,22 +176,21 @@
     lax.fori_loop(0, out.shape[1] // 256, step, 0)
 
 
-def middle_kernel(stacks, partial, w, out, *, start):
-    add_products(out, partial, ((stacks.at[2, :, start : start + w.shape[0]], w),))
-
-
-def strand_kernel(stacks, partial, w3, w3_rest, ups, taps, grads, ahead, behind, sums, values, mixes, *, first):
+def middle_kernel(stacks, partial, w2, out):
+    add_products(out, partial, ((stacks.at[2], w2),))
+
+
+def strand_kernel(stacks, partial, w3, ups, taps, grads, ahead, behind, sums, values, mixes, *, first):
     total = stacks.shape[1] // 2
     rows = total - 2 * EDGE
     units = sums.shape[1]
-    split = w3.shape[0]
     count = units // LANES
     turn = turning(LANES)
 
     def project(at, _):
         near = pl.ds(pl.multiple_of(at * 256, 256), 256)
         cols = pl.ds(pl.multiple_of(first + at * 256, 256), 256)
-        acc = partial[:, cols] + dot(stacks[3, :, :split], w3[:, cols]) + dot(stacks[3, :, split:], w3_rest[:, cols])
+        acc = partial[:, cols] + dot(stacks[3], w3[:, cols])
         acc = acc.astype(jnp.bfloat16).astype(jnp.float32)
         for way in range(2):
             base = way * total
@@ -241,82 +240,111 @@
     lax.fori_loop(0, count, work, 0)
 
 
-def product_kernel(columns, *refs, block):
-    grads, out = refs[:-1], refs[-1]
+def product_kernel(columns, *refs, block, parts):
+    grads, refs = refs[:parts], refs[parts:]
+    out = refs[-1]
     start = 0
     for part in grads:
         stop = start + part.shape[1]
         out[:, start:stop] = dot(columns[block], part[...]).astype(out.dtype)
         start = stop
-
-
-def merge_kernel(columns, came, *refs, block):
-    grads, out = refs[:-1], refs[-1]
+    if len(refs) > 1:
+        out[:, start:] = refs[0][...]
+
+
+def merge_kernel(columns, came, *refs, block, parts):
+    grads, refs = refs[:parts], refs[parts:]
+    out = refs[-1]
     start = 0
     for part in grads:
         stop = start + part.shape[1]
         own = dot(columns[block], part[...])
         out[:, start:stop] = (own + came[:, start:stop].astype(jnp.float32)).astype(jnp.bfloat16)
         start = stop
-
-
-def back_kernel(place, hot, w0, w1, w2, w2_rest, w3, w3_rest, later, *refs):
-    parts, (out, block, packed, table, backs, grads, sums) = refs[:12], refs[12:]
+    if len(refs) > 1:
+        out[:, start:] = paired(added(refs[0][...], came[:, start:])).astype(jnp.bfloat16)
+
+
+def small_kernel(place, hot, w0, w1, w2, w3, *refs):
+    parts, (out, grads, sums, table) = refs[:6], refs[6:]
+    rows = hot.shape[1] // 3
+    start = 0
+    for at in range(3):
+        part, part_sums = parts[at * 2], parts[at * 2 + 1]
+        stop = start + part.shape[1]
+        grads[:8, start:stop] = dot(hot[:, :rows], part[:rows])[:8]
+        grads[8:, start:stop] = dot(hot[:, :rows], part[rows:])[:8]
+        sums[:, start:stop] = part_sums[...]
+        start = stop
+    split = jnp.concatenate(thirds(grads[...]), axis=0)
+    turn = turning(256)
+    width = w0.shape[0]
+    dims = (((1,), (1,)), ((), ()))
+    backs = []
+    for w in (w0, w1, w2, w3):
+        back = lax.dot_general(split, w[...], dims, preferred_element_type=jnp.float32)
+        backs.append(back[:16] + back[16:32] + back[32:])
+    for r in range(4):
+        cols = pl.ds(pl.multiple_of((place[0] ^ r) * width, width), width)
+        there = turned(jnp.concatenate(thirds(backs[3 - r][8:]), axis=0), turn)
+        table[:, cols] = backs[r][:8] + there[:8] + there[8:16] + there[16:]
+    units = sums.shape[1]
+    count = units // LANES
+    for at in range(count):
+        pack = jnp.concatenate(
+            [
+                sums[:, at * LANES : (at + 1) * LANES],
+                table[:, at * LANES : (at + 1) * LANES],
+                table[:, units + at * LANES : units + (at + 1) * LANES],
+                jnp.zeros((8, LANES), jnp.float32),
+            ],
+            axis=0,
+        )
+        head = pack.astype(jnp.bfloat16).astype(jnp.float32)
+        rest = pack - head
+        low = low_lanes(pack.shape)
+        first = jnp.where(low, head, pltpu.roll(rest, LANES // 2, 1))
+        second = jnp.where(low, pltpu.roll(head, LANES // 2, 1), rest)
+        out[at * PACK : (at + 1) * PACK] = first.astype(jnp.bfloat16)
+        out[(count + at) * PACK : (count + at + 1) * PACK] = second.astype(jnp.bfloat16)
+
+
+def back_kernel(place, w0, w1, w2, w3, later, *refs):
+    parts, (out, block, backs, grads) = refs[:9], refs[9:]
     rows = out.shape[0]
     width = w0.shape[0]
     turn = turning(256)
     dims = (((1,), (1,)), ((), ()))
     start = 0
     for at in range(3):
-        part, part_sums = parts[at * 4], parts[at * 4 + 3]
+        part = parts[at * 3]
         stop = start + part.shape[1]
         grads[:, start:stop] = part[...]
-        sums[:, start:stop] = part_sums[...]
         start = stop
-    forward = jnp.concatenate([parts[at * 4 + 1][...] for at in range(3)], axis=1)
-    backward = jnp.concatenate([parts[at * 4 + 2][...] for at in (2, 1, 0)], axis=1)
+    forward = jnp.concatenate([parts[at * 3 + 1][...] for at in range(3)], axis=1)
+    backward = jnp.concatenate([parts[at * 3 + 2][...] for at in (2, 1, 0)], axis=1)
     block[...] = (forward + backward).astype(jnp.bfloat16)
-    for r, group in enumerate(((w0,), (w1,), (w2, w2_rest), (w3, w3_rest))):
-        size = width // len(group)
-        for at, w in enumerate(group):
-            backs[r, :, at * size : (at + 1) * size] = lax.dot_general(
-                grads[...], w[...], dims, preferred_element_type=jnp.float32
-            )
+    for r, w in enumerate((w0, w1, w2, w3)):
+        backs[r] = lax.dot_general(grads[...], w[...], dims, preferred_element_type=jnp.float32)
     for r in range(4):
         whole = backs[r, :rows] + turned(backs[3 - r, rows:].astype(jnp.bfloat16), turn)
-        cols = pl.ds(pl.multiple_of((place[0] ^ r) * width, width), width)
-        out[:, cols] = whole.astype(jnp.bfloat16)
-        table[:, cols] = dot(hot[...], jnp.concatenate(thirds(whole), axis=0))
-    count = sums.shape[1] // LANES
-    half = table.shape[1] // 2
-    for at in range(count):
-        cols = slice(at * LANES, (at + 1) * LANES)
-        packed[at * PACK : at * PACK + 8] = sums[:, cols]
-        packed[at * PACK + 8 : at * PACK + 16] = table[:8, cols]
-        packed[at * PACK + 16 : at * PACK + 24] = table[:8, half + at * LANES : half + (at + 1) * LANES]
-        packed[at * PACK + 24 : at * PACK + 32] = jnp.zeros((8, LANES), jnp.float32)
+        out[:, pl.ds(pl.multiple_of((place[0] ^ r) * width, width), width)] = whole.astype(jnp.bfloat16)
 
 
 def block_kernel(place, columns, mate, came, *refs, parts):
     grads, refs = refs[:parts], refs[parts:]
     wide = len(refs) > 5
     if wide:
-        packed, packed_came, outs, own, extra = refs[0], refs[1], refs[2:6], refs[6], refs[7]
-        whole = packed[...] + packed_came[...]
-        half = whole.shape[0]
-        head = whole.astype(jnp.bfloat16).astype(jnp.float32)
-        rest = whole - head
-        low = low_lanes(whole.shape)
-        extra[:half] = jnp.where(low, head, pltpu.roll(rest, LANES // 2, 1))
-        extra[half:] = jnp.where(low, pltpu.roll(head, LANES // 2, 1), rest)
+        merged, outs, own, extra = refs[0], refs[1:5], refs[5], refs[6]
+        extra[...] = paired(added(merged[:, own.shape[1] :], came[:, own.shape[1] :]))
     else:
         outs, own = refs[:4], refs[4]
     rows = outs[0].shape[0]
     units = own.shape[1]
-    product_kernel(columns, *grads, own, block=0)
+    product_kernel(columns, *grads, own, block=0, parts=parts)
     for step, out in enumerate(outs):
         here = pl.ds(pl.multiple_of((place[1] + step) % 4 * rows, rows), rows)
-        out[:, :units] = added(own[here], mate[here], came[here]).astype(jnp.bfloat16)
+        out[:, :units] = added(own[here], mate[here], came[here, :units]).astype(jnp.bfloat16)
         if wide:
             out[:, units:] = extra[here].astype(jnp.bfloat16)
 
@@ -402,10 +430,8 @@
     total = rows + 2 * EDGE
     me = 2 * lax.axis_index("xl") + lax.axis_index("c")
     place = jnp.stack([me, lax.axis_index("y")]).astype(jnp.int32)
-    half = width // 2
-    w_core = swap_core(weight)
-    w_side = [side(weight[at * half : (at + 1) * half]) for at in range(2)]
-    w_last = [swap_core(w_side[at]) for at in range(2)]
+    weights = [weight, swap_core(weight), side(weight)]
+    weights.append(swap_core(weights[2]))
     top = pl.BlockSpec((EDGE, features), lambda at: (0, 0))
     bottom = pl.BlockSpec((EDGE, features), lambda at: (rows // EDGE - 1, 0))
     up_top = pl.BlockSpec((EDGE, units), lambda at: (0, 0))
@@ -461,12 +487,10 @@
         up_centre,
         before,
         after,
-        weight,
-        w_core,
+        *weights[:2],
         scalar=True,
     )
-    for at in range(2):
-        partial = call(middle_kernel, wide, stacks, partial, w_side[at], start=at * half)
+    partial = call(middle_kernel, wide, stacks, partial, weights[2])
     ends = (0, units // 2, units // 4 * 3, units)
     parts = []
     for at in range(3):
@@ -482,7 +506,7 @@
                 ),
                 stacks,
                 partial,
-                *w_last,
+                weights[3],
                 ups,
                 taps,
                 scratch=(pltpu.VMEM((2 * total, size), jnp.float32), pltpu.VMEM((2, total, LANES), jnp.float32)),
@@ -490,42 +514,33 @@
             )
         )
     grads = [[parts[0][0]], [parts[1][0], parts[2][0]]]
+    extra = call(
+        small_kernel,
+        array((width, LANES)),
+        place,
+        hot,
+        *weights,
+        *[cells for part in parts for cells in (part[0], part[3])],
+        scalar=True,
+        scratch=(
+            pltpu.VMEM((16, units), jnp.float32),
+            pltpu.VMEM((8, units), jnp.float32),
+            pltpu.VMEM((8, features), jnp.float32),
+        ),
+    )
     chunk = array((width, units // 2))
     came = []
     mates = []
     for at in range(2):
-        goes = call(product_kernel, chunk, columns, *grads[at], block=3)
+        count = len(grads[at])
+        rest = [extra] * at
+        large = array((width, units // 2 + LANES * at))
+        goes = call(product_kernel, large, columns, *grads[at], *rest, block=3, parts=count)
         goes = swap_core(goes)
-        merged = call(merge_kernel, chunk, columns, goes, *grads[at], block=2)
+        merged = call(merge_kernel, large, columns, goes, *grads[at], *rest, block=2, parts=count)
         came.append(side(merged))
-        mate = call(product_kernel, chunk, columns, *grads[at], block=1)
+        mate = call(product_kernel, chunk, columns, *grads[at], block=1, parts=count)
         mates.append(swap_core(mate))
-    grad_hidden, block_result, packed = call(
-        back_kernel,
-        (
-            array((rows, features)),
-            array((rows, units)),
-            array((units // LANES * PACK, LANES), jnp.float32),
-        ),
-        place,
-        hot,
-        weight,
-        w_core,
-        *w_side,
-        *w_last,
-        merged,
-        *[cells for part in parts for cells in part],
-        scalar=True,
-        unread=(8,),
-        scratch=(
-            pltpu.VMEM((16, features), jnp.float32),
-            pltpu.VMEM((4, 2 * rows, width), jnp.float32),
-            pltpu.VMEM((2 * rows, units), jnp.bfloat16),
-            pltpu.VMEM((8, units), jnp.float32),
-        ),
-    )
-    packed = packed + swap_core(packed)
-    packed_came = side(packed)
     part = width // 4
     own = pltpu.VMEM(chunk.shape, jnp.float32)
     head = call(
@@ -549,11 +564,21 @@
         mates[1],
         came[1],
         *grads[1],
-        packed,
-        packed_came,
+        merged,
         scalar=True,
         scratch=(own, pltpu.VMEM((width, LANES), jnp.float32)),
         parts=2,
+    )
+    grad_hidden, block_result = call(
+        back_kernel,
+        (array((rows, features)), array((rows, units))),
+        place,
+        *weights,
+        tail[0],
+        *[cells for part in parts for cells in part[:3]],
+        scalar=True,
+        unread=(5,),
+        scratch=(pltpu.VMEM((4, 2 * rows, width), jnp.float32), pltpu.VMEM((2 * rows, units), jnp.bfloat16)),
     )
     tail = [tail[0]] + [along_y(tail[step], step) for step in (1, 2, 3)]
     quarter = call(quarter_kernel, array((part, units + LANES)), *head, *tail)

time: 136 us -> 141 us (1.037)
  waiting for transfers between devices: 41 us -> 44.9 us
  blocking collectives: 36.5 us -> 34.5 us
  Pallas kernels: 25.3 us -> 26.8 us
    ppermute x24 -> x20, waiting for transfers between devices: 41 us -> 44.9 us  [shift(): return lax.ppermute(cells, axes if len(axes) > 1 else axes[0], pairs)]
    all_to_all x2, blocking collectives: 36.5 us -> 34.5 us  [step(): lax.all_to_all(pieces, ('xh', 'z'), split_axis=0, concat_axis=0, tiled=True)]
    pallas_call x19, Pallas kernels: 23.6 us -> 25.1 us  [call(): pl.pallas_call(functools.partial(kernel, **fixed), out_shape=outs, in_spe...]
    ppermute x24 -> x20, starting transfers between devices: 30.1 us -> 31.5 us  [shift(): return lax.ppermute(cells, axes if len(axes) > 1 else axes[0], pairs)]
  transfers between devices with their start and end apart: 24 -> 20, of which waited for: 9 -> 10; matrix products, arithmetic and copies ran while one was open for 1% -> 0% of each run, Pallas kernels for 14% -> 11%
where the time goes in v6:
time: 141 us; the launch traced here: 140 us
  waiting for transfers between devices  44.9 us (32%)
  blocking collectives  34.5 us (24%)
  starting transfers between devices  31.5 us (22%)
  Pallas kernels  26.8 us (19%)
  local copies, waits for them, and re-layouts  1.71 us (1%)
    ppermute x20, waiting for transfers between devices, shift(): return lax.ppermute(cells, axes if len(axes) > 1 else axes[0], pairs)  44.9 us
    all_to_all x2, blocking collectives, step(): lax.all_to_all(pieces, ('xh', 'z'), split_axis=0, concat_axis=0, tiled=True)  34.5 us
    ppermute x20, starting transfers between devices, shift(): return lax.ppermute(cells, axes if len(axes) > 1 else axes[0], pairs)  31.5 us
    pallas_call x19, Pallas kernels, call(): pl.pallas_call(functools.partial(kernel, **fixed), out_shape=outs, in_spe...  25.1 us
  transfers between devices with their start and end apart: 20, of which 10 were waited for; matrix products, arithmetic and copies ran while one was open for 0% of the time, Pallas kernels for 11%

profile of v6, /device:TPU:2, one launch (start us, length us, event | category | flops | bytes accessed | tf_op | source)
XLA Modules:
  0.0 140.4 jit_solution(103479818346017563)
XLA Ops:
  0.7 1.6 %collective-permute-start.1 = (bf16[512,1024]{1,0:T(8,128)(2,1)}, bf16[512,1024]{1,0:T(8,128)(2,1)}, u32[]{:S(2)}, u32[]{:S(2)}) collective-permute-start(bf16[512,1024]{1,0:T(8,128)(2,1)} %w0.5), channel_id=1, source_target_pairs={{0,128},{32,160},{64,224},{96,192},{128,32},{160,0},{192,64},{224,... | collective-permute-start | bytes 3145736 | tf_op jit(solution)/shard_map/ppermute | solution.py:29
  2.2 13.8 %collective-permute-done.1.w2 = bf16[512,1024]{1,0:T(8,128)(2,1)} collective-permute-done((bf16[512,1024]{1,0:T(8,128)(2,1)}, bf16[512,1024]{1,0:T(8,128)(2,1)}, u32[]{:S(2)}, u32[]{:S(2)}) %collective-permute-start.1) | collective-permute-done | bytes 1048608 | tf_op jit(solution)/shard_map/ppermute | solution.py:29
  16.1 1.7 %shard_map.102 = (bf16[8,3072]{1,0:T(8,128)(2,1)}, bf16[8,3072]{1,0:T(8,128)(2,1)}) custom-call(s32[1,128]{1,0:T(1,128)} %codes.3, bf16[128,2048]{1,0:T(8,128)(2,1)} %bitcast.8, bf16[128,2048]{1,0:T(8,128)(2,1)} %bitcast.9, bf16[128,1024]{1,0:T(8,128)(2,1)} %bitcast.11, bf16[128,1024]{1,0:T(8,128)(2,1)} %bitcast.12, f32[5,2048]{1,0:T(8,128)} %table.1), custom_call_target="tpu_custom_call" | custom-call | tf_op jit(solution)/shard_map/pallas_call | solution.py:440
  17.8 3.2 %collective-permute-start.3 = (bf16[8,3072]{1,0:T(8,128)(2,1)}, bf16[8,3072]{1,0:T(8,128)(2,1)S(1)}, u32[]{:S(2)}, u32[]{:S(2)}) collective-permute-start(bf16[8,3072]{1,0:T(8,128)(2,1)} %get-tuple-element.43), channel_id=1, source_target_pairs={{0,1},{1,2},{2,3},{3,4},{4,5},{5,6},{6,7},{7,8},{8,9},{9,10},{10,1... | collective-permute-start | bytes 147464 | tf_op jit(solution)/shard_map/ppermute | solution.py:29
  24.1 1.7 %shard_map.101 = (bf16[4,256,512]{2,1,0:T(8,128)(2,1)S(1)}, bf16[4,512,256]{2,1,0:T(8,128)(2,1)S(1)}, f32[256,1024]{1,0:T(8,128)S(1)}, f32[7,1024]{1,0:T(8,128)S(1)}, bf16[16,384]{1,0:T(8,128)(2,1)S(1)}) custom-call(s32[2]{0:T(128)S(1)} %pad_add_fusion.place, s32[1,128]{1,0:T(1,128)S(1)} %copy-done.5, f32[7,1024]{1,0:T(8,128)S(1)} %copy-done.4, ...), custom_call_target="tpu_custom_call" | custom-call | tf_op jit(solution)/shard_map/pallas_call | solution.py:408
  25.8 1.5 %collective-permute-done.4.after = bf16[8,3072]{1,0:T(8,128)(2,1)} collective-permute-done((bf16[8,3072]{1,0:T(8,128)(2,1)}, bf16[8,3072]{1,0:T(8,128)(2,1)}, u32[]{:S(2)}, u32[]{:S(2)}) %collective-permute-start.4) | collective-permute-done | bytes 49184 | tf_op jit(solution)/shard_map/ppermute | solution.py:29
  27.3 2.5 %shard_map.103 = (bf16[4,288,512]{2,1,0:T(8,128)(2,1)S(1)}, f32[288,1024]{1,0:T(8,128)S(1)}, f32[288,1024]{1,0:T(8,128)S(1)}) custom-call(s32[2]{0:T(128)S(1)} %pad_add_fusion.place, bf16[4,256,512]{2,1,0:T(8,128)(2,1)S(1)} %get-tuple-element.41.centre, f32[256,1024]{1,0:T(8,128)S(1)} %get-tuple-element.42.up_centre, ...), custom_call_target="tpu_custom_call" | custom-call | tf_op jit(solution)/shard_map/pallas_call | solution.py:408
  29.9 2.2 %shard_map.104.partial = f32[288,1024]{1,0:T(8,128)S(1)} custom-call(bf16[4,288,512]{2,1,0:T(8,128)(2,1)S(1)} %get-tuple-element.45.stacks, f32[288,1024]{1,0:T(8,128)S(1)} %get-tuple-element.46.partial, bf16[512,1024]{1,0:T(8,128)(2,1)} %collective-permute-done.1.w2), custom_call_target="tpu_custom_call" | custom-call | tf_op jit(solution)/shard_map/pallas_call | solution.py:408
  34.8 2.7 %shard_map.108 = (bf16[256,512]{1,0:T(8,128)(2,1)S(1)}, f32[128,512]{1,0:T(8,128)S(1)}, f32[128,512]{1,0:T(8,128)S(1)}, f32[8,512]{1,0:T(8,128)S(1)}) custom-call(bf16[4,288,512]{2,1,0:T(8,128)(2,1)S(1)} %get-tuple-element.45.stacks, f32[288,1024]{1,0:T(8,128)S(1)} %shard_map.104.partial, bf16[512,1024]{1,0:T(8,128)(2,1)S(1)} %collective-permute-done.2.w3, ...), custom_call_target="tpu_custom_call" | custom-call | tf_op jit(solution)/shard_map/pallas_call | solution.py:408
  37.5 3.0 %shard_map.109.refs_2_ = bf16[512,128]{1,0:T(8,128)(2,1)S(1)} custom-call(s32[2]{0:T(128)S(1)} %pad_add_fusion.place, bf16[16,384]{1,0:T(8,128)(2,1)S(1)} %get-tuple-element.51.hot, bf16[512,1024]{1,0:T(8,128)(2,1)S(1)} %copy-done, bf16[512,1024]{1,0:T(8,128)(2,1)S(1)} %collective-permute-done.w1, bf16[512,1024]{1,0:T(8,128)(2,1)} %collective-permute-done.1.w2, ...), custom_call_target="tpu_custom_call" | custom-call | tf_op jit(solution)/shard_map/pallas_call | solution.py:408
  43.4 8.6 %collective-permute-start.7 = (bf16[512,640]{1,0:T(8,128)(2,1)S(1)}, bf16[512,640]{1,0:T(8,128)(2,1)S(1)}, u32[]{:S(2)}, u32[]{:S(2)}) collective-permute-start(bf16[512,640]{1,0:T(8,128)(2,1)S(1)} %shard_map.111.refs_2_), channel_id=1, source_target_pairs={{0,128},{32,160},{64,224},{96,192},{128,32},{160,0},{192,64},{224,... | collective-permute-start | bytes 1966088 | tf_op jit(solution)/shard_map/ppermute | solution.py:29
  54.5 11.2 %collective-permute-done.10.came = bf16[512,512]{1,0:T(8,128)(2,1)S(1)} collective-permute-done((bf16[512,512]{1,0:T(8,128)(2,1)S(1)}, bf16[512,512]{1,0:T(8,128)(2,1)S(1)}, u32[]{:S(2)}, u32[]{:S(2)}) %collective-permute-start.10) | collective-permute-done | bytes 524320 | tf_op jit(solution)/shard_map/ppermute | solution.py:29
  68.0 4.7 %collective-permute-start.15 = (bf16[128,640]{1,0:T(8,128)(2,1)S(1)}, bf16[128,640]{1,0:T(8,128)(2,1)S(1)}, u32[]{:S(2)}, u32[]{:S(2)}) collective-permute-start(bf16[128,640]{1,0:T(8,128)(2,1)S(1)} %get-tuple-element.70), channel_id=1, source_target_pairs={{0,2},{1,3},{2,0},{3,1},{4,6},{5,7},{6,4},{7,5},{8,10},{9,11},{10,... | collective-permute-start | bytes 491528 | tf_op jit(solution)/shard_map/ppermute | solution.py:29
  72.6 1.6 %collective-permute-start.12 = (bf16[128,512]{1,0:T(8,128)(2,1)S(1)}, bf16[128,512]{1,0:T(8,128)(2,1)S(1)}, u32[]{:S(2)}, u32[]{:S(2)}) collective-permute-start(bf16[128,512]{1,0:T(8,128)(2,1)S(1)} %get-tuple-element.67), channel_id=1, source_target_pairs={{0,2},{1,3},{2,0},{3,1},{4,6},{5,7},{6,4},{7,5},{8,10},{9,11},{10,... | collective-permute-start | bytes 393224 | tf_op jit(solution)/shard_map/ppermute | solution.py:29
  74.4 3.0 %collective-permute-start.13 = (bf16[128,512]{1,0:T(8,128)(2,1)S(1)}, bf16[128,512]{1,0:T(8,128)(2,1)S(1)}, u32[]{:S(2)}, u32[]{:S(2)}) collective-permute-start(bf16[128,512]{1,0:T(8,128)(2,1)S(1)} %get-tuple-element.68), channel_id=1, source_target_pairs={{0,3},{1,0},{2,1},{3,2},{4,7},{5,4},{6,5},{7,6},{8,11},{9,8},{10,9... | collective-permute-start | bytes 393224 | tf_op jit(solution)/shard_map/ppermute | solution.py:29
  77.3 5.3 %collective-permute-done.12.refs_2_ = bf16[128,512]{1,0:T(8,128)(2,1)S(1)} collective-permute-done((bf16[128,512]{1,0:T(8,128)(2,1)S(1)}, bf16[128,512]{1,0:T(8,128)(2,1)S(1)}, u32[]{:S(2)}, u32[]{:S(2)}) %collective-permute-start.12) | collective-permute-done | bytes 131104 | tf_op jit(solution)/shard_map/ppermute | solution.py:29
  82.7 2.2 %collective-permute-done.13.refs_3_ = bf16[128,512]{1,0:T(8,128)(2,1)S(1)} collective-permute-done((bf16[128,512]{1,0:T(8,128)(2,1)S(1)}, bf16[128,512]{1,0:T(8,128)(2,1)S(1)}, u32[]{:S(2)}, u32[]{:S(2)}) %collective-permute-start.13) | collective-permute-done | bytes 131104 | tf_op jit(solution)/shard_map/ppermute | solution.py:29
  85.4 18.5 %all_to_all.10.parts = bf16[16,8,1152]{2,1,0:T(8,128)(2,1)S(1)} all-to-all(bf16[16,8,1152]{2,1,0:T(8,128)(2,1)S(1)} %bitcast.18), channel_id=1, replica_groups=mesh['xl'=2,'c'=2,'xh'=2,'z'=8,'y'=4] {'xh','z'}, dimensions={0} | all-to-all | bytes 589824 | tf_op jit(solution)/shard_map/all_to_all | solution.py:586
  104.0 16.0 %all_to_all.11 = bf16[16,8,1152]{2,1,0:T(8,128)(2,1)S(1)} all-to-all(bf16[16,8,1152]{2,1,0:T(8,128)(2,1)S(1)} %shard_map.119), channel_id=1, replica_groups=mesh['xl'=2,'c'=2,'xh'=2,'z'=8,'y'=4] {'xh','z'}, dimensions={0} | all-to-all | bytes 589824 | tf_op jit(solution)/shard_map/all_to_all | solution.py:588
  120.0 4.0 %collective-permute-start.19 = (bf16[128,1152]{1,0:T(8,128)(2,1)S(1)}, bf16[128,1152]{1,0:T(8,128)(2,1)S(1)}, u32[]{:S(2)}, u32[]{:S(2)}) collective-permute-start(bf16[128,1152]{1,0:T(8,128)(2,1)S(1)} %bitcast.14), channel_id=1, source_target_pairs={{0,3},{1,0},{2,1},{3,2},{4,7},{5,4},{6,5},{7,6},{8,11},{9,8},{10,9... | collective-permute-start | bytes 884744 | tf_op jit(solution)/shard_map/ppermute | solution.py:29
  125.2 3.7 %shard_map.113 = (bf16[128,2048]{1,0:T(8,128)(2,1)}, bf16[128,1024]{1,0:T(8,128)(2,1)}) custom-call(s32[2]{0:T(128)S(1)} %pad_add_fusion.place, bf16[512,1024]{1,0:T(8,128)(2,1)S(1)} %copy-done, bf16[512,1024]{1,0:T(8,128)(2,1)S(1)} %collective-permute-done.w1, bf16[512,1024]{1,0:T(8,128)(2,1)} %collective-permute-done.1.w2, ...), custom_call_target="tpu_custom_call" | custom-call | tf_op jit(solution)/shard_map/pallas_call | solution.py:408
  128.8 5.8 %collective-permute-done.19.q3 = bf16[128,1152]{1,0:T(8,128)(2,1)S(1)} collective-permute-done((bf16[128,1152]{1,0:T(8,128)(2,1)S(1)}, bf16[128,1152]{1,0:T(8,128)(2,1)S(1)}, u32[]{:S(2)}, u32[]{:S(2)}) %collective-permute-start.19) | collective-permute-done | bytes 294944 | tf_op jit(solution)/shard_map/ppermute | solution.py:29
  135.2 3.1 %collective-permute-done.17.q1 = bf16[128,1152]{1,0:T(8,128)(2,1)S(1)} collective-permute-done((bf16[128,1152]{1,0:T(8,128)(2,1)S(1)}, bf16[128,1152]{1,0:T(8,128)(2,1)S(1)}, u32[]{:S(2)}, u32[]{:S(2)}) %collective-permute-start.17) | collective-permute-done | bytes 294944 | tf_op jit(solution)/shard_map/ppermute | solution.py:29
  138.3 2.1 %shard_map.120 = (f32[512,1024]{1,0:T(8,128)}, f32[7,1024]{1,0:T(8,128)}, f32[5,2048]{1,0:T(8,128)}) custom-call(s32[2]{0:T(128)S(1)} %pad_add_fusion.place, bf16[128,1152]{1,0:T(8,128)(2,1)S(1)} %bitcast.17, bf16[128,1152]{1,0:T(8,128)(2,1)S(1)} %collective-permute-done.17.q1, bf16[128,1152]{1,0:T(8,128)(2,1)S(1)} %collective-permute-done.18.q2, ...), custom_call_target="tpu_custom_call" | custom-call | tf_op jit(solution)/shard_map/pallas_call | solution.py:408
  (51 shorter events, 15.8 us)
Async XLA Ops:
  0.6 21.8 %copy-start.3 = (f32[5,2048]{1,0:T(8,128)S(1)}, f32[5,2048]{1,0:T(8,128)}, u32[]{:S(2)}) copy-start(f32[5,2048]{1,0:T(8,128)} %table.1) | copy-start | bytes 122884
  0.6 21.8 %copy-start.2 = (bf16[1,128,1024]{2,1,0:T(8,128)(2,1)S(1)}, bf16[1,128,1024]{2,1,0:T(8,128)(2,1)}, u32[]{:S(2)}) copy-start(bf16[1,128,1024]{2,1,0:T(8,128)(2,1)} %param.11) | copy-start | bytes 786436
  0.7 21.8 %copy-start.4 = (f32[7,1024]{1,0:T(8,128)S(1)}, f32[7,1024]{1,0:T(8,128)}, u32[]{:S(2)}) copy-start(f32[7,1024]{1,0:T(8,128)} %taps.1) | copy-start | bytes 86020
  0.7 15.4 %collective-permute-start.1 = (bf16[512,1024]{1,0:T(8,128)(2,1)}, bf16[512,1024]{1,0:T(8,128)(2,1)}, u32[]{:S(2)}, u32[]{:S(2)}) collective-permute-start(bf16[512,1024]{1,0:T(8,128)(2,1)} %w0.5), channel_id=1, source_target_pairs={{0,128},{32,160},{64,224},{96,192},{128,32},{160,0},{192,64},{224,... | collective-permute-start | bytes 3145736 | tf_op jit(solution)/shard_map/ppermute | solution.py:29
  2.2 25.1 %collective-permute-start = (bf16[512,1024]{1,0:T(8,128)(2,1)}, bf16[512,1024]{1,0:T(8,128)(2,1)S(1)}, u32[]{:S(2)}, u32[]{:S(2)}) collective-permute-start(bf16[512,1024]{1,0:T(8,128)(2,1)} %w0.5), channel_id=1, source_target_pairs={{0,64},{64,0},{1,65},{65,1},{2,66},{66,2},{3,67},{67,3},{4,68},{68... | collective-permute-start | bytes 3145736 | tf_op jit(solution)/shard_map/ppermute | solution.py:29
  16.1 16.0 %collective-permute-start.2 = (bf16[512,1024]{1,0:T(8,128)(2,1)}, bf16[512,1024]{1,0:T(8,128)(2,1)S(1)}, u32[]{:S(2)}, u32[]{:S(2)}) collective-permute-start(bf16[512,1024]{1,0:T(8,128)(2,1)} %collective-permute-done.1.w2), channel_id=1, source_target_pairs={{0,64},{64,0},{1,65},{65,1},{2,66},{66,2},{3,67},{67,3},{4,68},{68... | collective-permute-start | bytes 3145736 | tf_op jit(solution)/shard_map/ppermute | solution.py:29
  16.1 11.3 %copy-start = (bf16[512,1024]{1,0:T(8,128)(2,1)S(1)}, bf16[512,1024]{1,0:T(8,128)(2,1)}, u32[]{:S(2)}) copy-start(bf16[512,1024]{1,0:T(8,128)(2,1)} %w0.5) | copy-start | bytes 3145732
  17.8 8.0 %collective-permute-start.3 = (bf16[8,3072]{1,0:T(8,128)(2,1)}, bf16[8,3072]{1,0:T(8,128)(2,1)S(1)}, u32[]{:S(2)}, u32[]{:S(2)}) collective-permute-start(bf16[8,3072]{1,0:T(8,128)(2,1)} %get-tuple-element.43), channel_id=1, source_target_pairs={{0,1},{1,2},{2,3},{3,4},{4,5},{5,6},{6,7},{7,8},{8,9},{9,10},{10,1... | collective-permute-start | bytes 147464 | tf_op jit(solution)/shard_map/ppermute | solution.py:29
  21.0 6.3 %collective-permute-start.4 = (bf16[8,3072]{1,0:T(8,128)(2,1)}, bf16[8,3072]{1,0:T(8,128)(2,1)}, u32[]{:S(2)}, u32[]{:S(2)}) collective-permute-start(bf16[8,3072]{1,0:T(8,128)(2,1)} %get-tuple-element.44), channel_id=1, source_target_pairs={{1,0},{2,1},{3,2},{4,3},{5,4},{6,5},{7,6},{8,7},{9,8},{10,9},{11,1... | collective-permute-start | bytes 147464 | tf_op jit(solution)/shard_map/ppermute | solution.py:29
  40.9 2.2 %collective-permute-start.6 = (bf16[512,640]{1,0:T(8,128)(2,1)S(1)}, bf16[512,640]{1,0:T(8,128)(2,1)S(1)}, u32[]{:S(2)}, u32[]{:S(2)}) collective-permute-start(bf16[512,640]{1,0:T(8,128)(2,1)S(1)} %shard_map.110), channel_id=1, source_target_pairs={{0,64},{64,0},{1,65},{65,1},{2,66},{66,2},{3,67},{67,3},{4,68},{68... | collective-permute-start | bytes 1966088 | tf_op jit(solution)/shard_map/ppermute | solution.py:29
  41.3 11.1 %collective-permute-start.9 = (bf16[512,512]{1,0:T(8,128)(2,1)S(1)}, bf16[512,512]{1,0:T(8,128)(2,1)S(1)}, u32[]{:S(2)}, u32[]{:S(2)}) collective-permute-start(bf16[512,512]{1,0:T(8,128)(2,1)S(1)} %shard_map.115), channel_id=1, source_target_pairs={{0,64},{64,0},{1,65},{65,1},{2,66},{66,2},{3,67},{67,3},{4,68},{68... | collective-permute-start | bytes 1572872 | tf_op jit(solution)/shard_map/ppermute | solution.py:29
  43.4 23.5 %collective-permute-start.7 = (bf16[512,640]{1,0:T(8,128)(2,1)S(1)}, bf16[512,640]{1,0:T(8,128)(2,1)S(1)}, u32[]{:S(2)}, u32[]{:S(2)}) collective-permute-start(bf16[512,640]{1,0:T(8,128)(2,1)S(1)} %shard_map.111.refs_2_), channel_id=1, source_target_pairs={{0,128},{32,160},{64,224},{96,192},{128,32},{160,0},{192,64},{224,... | collective-permute-start | bytes 1966088 | tf_op jit(solution)/shard_map/ppermute | solution.py:29
  52.2 2.2 %collective-permute-start.8 = (bf16[512,512]{1,0:T(8,128)(2,1)S(1)}, bf16[512,512]{1,0:T(8,128)(2,1)S(1)}, u32[]{:S(2)}, u32[]{:S(2)}) collective-permute-start(bf16[512,512]{1,0:T(8,128)(2,1)S(1)} %shard_map.114), channel_id=1, source_target_pairs={{0,64},{64,0},{1,65},{65,1},{2,66},{66,2},{3,67},{67,3},{4,68},{68... | collective-permute-start | bytes 1572872 | tf_op jit(solution)/shard_map/ppermute | solution.py:29
  52.7 13.0 %collective-permute-start.10 = (bf16[512,512]{1,0:T(8,128)(2,1)S(1)}, bf16[512,512]{1,0:T(8,128)(2,1)S(1)}, u32[]{:S(2)}, u32[]{:S(2)}) collective-permute-start(bf16[512,512]{1,0:T(8,128)(2,1)S(1)} %shard_map.116), channel_id=1, source_target_pairs={{0,128},{32,160},{64,224},{96,192},{128,32},{160,0},{192,64},{224,... | collective-permute-start | bytes 1572872 | tf_op jit(solution)/shard_map/ppermute | solution.py:29
  53.9 12.9 %collective-permute-start.5 = (bf16[512,512]{1,0:T(8,128)(2,1)S(1)}, bf16[512,512]{1,0:T(8,128)(2,1)S(1)}, u32[]{:S(2)}, u32[]{:S(2)}) collective-permute-start(bf16[512,512]{1,0:T(8,128)(2,1)S(1)} %shard_map.107), channel_id=1, source_target_pairs={{0,64},{64,0},{1,65},{65,1},{2,66},{66,2},{3,67},{67,3},{4,68},{68... | collective-permute-start | bytes 1572872 | tf_op jit(solution)/shard_map/ppermute | solution.py:29
  66.7 7.7 %collective-permute-start.11 = (bf16[128,512]{1,0:T(8,128)(2,1)S(1)}, bf16[128,512]{1,0:T(8,128)(2,1)S(1)}, u32[]{:S(2)}, u32[]{:S(2)}) collective-permute-start(bf16[128,512]{1,0:T(8,128)(2,1)S(1)} %get-tuple-element.66), channel_id=1, source_target_pairs={{0,1},{1,2},{2,3},{3,0},{4,5},{5,6},{6,7},{7,4},{8,9},{9,10},{10,1... | collective-permute-start | bytes 393224 | tf_op jit(solution)/shard_map/ppermute | solution.py:29
  67.9 17.0 %collective-permute-start.14 = (bf16[128,640]{1,0:T(8,128)(2,1)S(1)}, bf16[128,640]{1,0:T(8,128)(2,1)S(1)}, u32[]{:S(2)}, u32[]{:S(2)}) collective-permute-start(bf16[128,640]{1,0:T(8,128)(2,1)S(1)} %get-tuple-element.69), channel_id=1, source_target_pairs={{0,1},{1,2},{2,3},{3,0},{4,5},{5,6},{6,7},{7,4},{8,9},{9,10},{10,1... | collective-permute-start | bytes 491528 | tf_op jit(solution)/shard_map/ppermute | solution.py:29
  68.0 16.9 %collective-permute-start.15 = (bf16[128,640]{1,0:T(8,128)(2,1)S(1)}, bf16[128,640]{1,0:T(8,128)(2,1)S(1)}, u32[]{:S(2)}, u32[]{:S(2)}) collective-permute-start(bf16[128,640]{1,0:T(8,128)(2,1)S(1)} %get-tuple-element.70), channel_id=1, source_target_pairs={{0,2},{1,3},{2,0},{3,1},{4,6},{5,7},{6,4},{7,5},{8,10},{9,11},{10,... | collective-permute-start | bytes 491528 | tf_op jit(solution)/shard_map/ppermute | solution.py:29
  72.6 12.3 %collective-permute-start.16 = (bf16[128,640]{1,0:T(8,128)(2,1)S(1)}, bf16[128,640]{1,0:T(8,128)(2,1)S(1)}, u32[]{:S(2)}, u32[]{:S(2)}) collective-permute-start(bf16[128,640]{1,0:T(8,128)(2,1)S(1)} %get-tuple-element.71), channel_id=1, source_target_pairs={{0,3},{1,0},{2,1},{3,2},{4,7},{5,4},{6,5},{7,6},{8,11},{9,8},{10,9... | collective-permute-start | bytes 491528 | tf_op jit(solution)/shard_map/ppermute | solution.py:29
  72.6 10.0 %collective-permute-start.12 = (bf16[128,512]{1,0:T(8,128)(2,1)S(1)}, bf16[128,512]{1,0:T(8,128)(2,1)S(1)}, u32[]{:S(2)}, u32[]{:S(2)}) collective-permute-start(bf16[128,512]{1,0:T(8,128)(2,1)S(1)} %get-tuple-element.67), channel_id=1, source_target_pairs={{0,2},{1,3},{2,0},{3,1},{4,6},{5,7},{6,4},{7,5},{8,10},{9,11},{10,... | collective-permute-start | bytes 393224 | tf_op jit(solution)/shard_map/ppermute | solution.py:29
  74.4 10.5 %collective-permute-start.13 = (bf16[128,512]{1,0:T(8,128)(2,1)S(1)}, bf16[128,512]{1,0:T(8,128)(2,1)S(1)}, u32[]{:S(2)}, u32[]{:S(2)}) collective-permute-start(bf16[128,512]{1,0:T(8,128)(2,1)S(1)} %get-tuple-element.68), channel_id=1, source_target_pairs={{0,3},{1,0},{2,1},{3,2},{4,7},{5,4},{6,5},{7,6},{8,11},{9,8},{10,9... | collective-permute-start | bytes 393224 | tf_op jit(solution)/shard_map/ppermute | solution.py:29
  120.0 14.6 %collective-permute-start.19 = (bf16[128,1152]{1,0:T(8,128)(2,1)S(1)}, bf16[128,1152]{1,0:T(8,128)(2,1)S(1)}, u32[]{:S(2)}, u32[]{:S(2)}) collective-permute-start(bf16[128,1152]{1,0:T(8,128)(2,1)S(1)} %bitcast.14), channel_id=1, source_target_pairs={{0,3},{1,0},{2,1},{3,2},{4,7},{5,4},{6,5},{7,6},{8,11},{9,8},{10,9... | collective-permute-start | bytes 884744 | tf_op jit(solution)/shard_map/ppermute | solution.py:29
  124.0 11.2 %collective-permute-start.18 = (bf16[128,1152]{1,0:T(8,128)(2,1)S(1)}, bf16[128,1152]{1,0:T(8,128)(2,1)S(1)}, u32[]{:S(2)}, u32[]{:S(2)}) collective-permute-start(bf16[128,1152]{1,0:T(8,128)(2,1)S(1)} %bitcast.15), channel_id=1, source_target_pairs={{0,2},{1,3},{2,0},{3,1},{4,6},{5,7},{6,4},{7,5},{8,10},{9,11},{10,... | collective-permute-start | bytes 884744 | tf_op jit(solution)/shard_map/ppermute | solution.py:29
  125.2 13.1 %collective-permute-start.17 = (bf16[128,1152]{1,0:T(8,128)(2,1)S(1)}, bf16[128,1152]{1,0:T(8,128)(2,1)S(1)}, u32[]{:S(2)}, u32[]{:S(2)}) collective-permute-start(bf16[128,1152]{1,0:T(8,128)(2,1)S(1)} %bitcast.16), channel_id=1, source_target_pairs={{0,1},{1,2},{2,3},{3,0},{4,5},{5,6},{6,7},{7,4},{8,9},{9,10},{10,1... | collective-permute-start | bytes 884744 | tf_op jit(solution)/shard_map/ppermute | solution.py:29
  (2 other events, 1.7 us)

commit v7 on v6

--- a/solution.py
+++ b/solution.py
@@ -377,12 +377,31 @@
         out[at, :, units:] = packed
 
 
-def final_kernel(place, q0, q1, q2, q3, weight_out, taps_out, table_out, packed, *, factor):
+def write_quarters(place, quarters, weight_out, cells, done, factor):
+    rows = cells.shape[1]
+    units = cells.shape[2]
+    copies = []
+    for at, (step, part) in enumerate(quarters):
+        cells[at] = part[:, :units].astype(jnp.float32) * factor
+        there = pl.ds(pl.multiple_of((place[1] + 4 - step) % 4 * rows, rows), rows)
+        copies.append(pltpu.make_async_copy(cells.at[at], weight_out.at[there], done.at[at]))
+        copies[-1].start()
+    return copies
+
+
+def first_kernel(place, q0, q3, weight_out, cells, done, *, factor):
+    for copy in write_quarters(place, ((0, q0), (3, q3)), weight_out, cells, done, factor):
+        copy.wait()
+
+
+def final_kernel(
+    place, q0, q1, q2, q3, begun, weight_out, taps_out, table_out, packed, cells, done, *, factor
+):
+    copies = write_quarters(place, ((1, q1), (2, q2)), weight_out, cells, done, factor)
     rows = q0.shape[0]
-    units = weight_out.shape[1]
+    units = cells.shape[2]
     for step, part in enumerate((q0, q1, q2, q3)):
         there = pl.ds(pl.multiple_of((place[1] + 4 - step) % 4 * rows, rows), rows)
-        weight_out[there] = part[:, :units].astype(jnp.float32) * factor
         packed[there] = part[:, units:].astype(jnp.float32)
     cells = packed[...]
     whole = cells + pltpu.roll(cells, LANES // 2, 1)
@@ -396,9 +415,11 @@
         table_out[:, cols] = whole[at * PACK + 8 : at * PACK + 8 + symbols]
         cols = slice(units + at * LANES, units + (at + 1) * LANES)
         table_out[:, cols] = whole[at * PACK + 16 : at * PACK + 16 + symbols]
-
-
-def call(kernel, outs, *args, scratch=(), scalar=False, unread=(), **fixed):
+    for copy in copies:
+        copy.wait()
+
+
+def call(kernel, outs, *args, scratch=(), scalar=False, unread=(), far=(), aliases=None, **fixed):
     inside = pl.BlockSpec(memory_space=pltpu.VMEM)
     specs = [inside] * len(args)
     if scalar:
@@ -409,7 +430,8 @@
         functools.partial(kernel, **fixed),
         out_shape=outs,
         in_specs=specs,
-        out_specs=jax.tree.map(lambda _: inside, outs),
+        out_specs=far or jax.tree.map(lambda _: inside, outs),
+        input_output_aliases=aliases or {},
         scratch_shapes=list(scratch),
         compiler_params=pltpu.CompilerParams(vmem_limit_bytes=20 * 2**20),
     )(*args)
@@ -588,13 +610,31 @@
     pieces = lax.all_to_all(pieces, ("xh", "z"), split_axis=0, concat_axis=0, tiled=True)
     quarter = pieces.reshape(quarter.shape)
     quarters = [quarter] + [along_y(quarter, step) for step in (1, 2, 3)]
+    inside = pl.BlockSpec(memory_space=pltpu.VMEM)
+    outside = pl.BlockSpec(memory_space=pl.ANY)
+    spare = (pltpu.VMEM((2, part, units), jnp.float32), pltpu.SemaphoreType.DMA((2,)))
+    begun = call(
+        first_kernel,
+        array((width, units), jnp.float32),
+        place,
+        quarters[0],
+        quarters[3],
+        scalar=True,
+        far=outside,
+        scratch=spare,
+        factor=factor,
+    )
     grad_weight, grad_kernel, grad_embedding = call(
         final_kernel,
         (array((width, units), jnp.float32), array(kernel.shape, jnp.float32), array(embedding.shape, jnp.float32)),
         place,
         *quarters,
-        scalar=True,
-        scratch=(pltpu.VMEM((width, LANES), jnp.float32),),
+        begun,
+        scalar=True,
+        unread=(5,),
+        far=[outside, inside, inside],
+        aliases={5: 0},
+        scratch=(pltpu.VMEM((width, LANES), jnp.float32), *spare),
         factor=factor,
     )
     return block_result[None], grad_hidden[None], grad_weight, grad_kernel, grad_embedding

time: 141 us -> 142 us (level)
  Pallas kernels: 26.8 us -> 28.5 us
  waiting for transfers between devices: 44.9 us -> 43.4 us
    pallas_call x19 -> x20, Pallas kernels: 25.1 us -> 26.8 us  [call(): pl.pallas_call(functools.partial(kernel, **fixed), out_shape=outs, in_spe...]
    ppermute x20, waiting for transfers between devices: 44.9 us -> 43.4 us  [shift(): return lax.ppermute(cells, axes if len(axes) > 1 else axes[0], pairs)]
  transfers between devices with their start and end apart: 20 -> 20, of which waited for: 10 -> 9; matrix products, arithmetic and copies ran while one was open for 0% -> 0% of each run, Pallas kernels for 11% -> 12%
where the time goes in v7:
time: 142 us; the launch traced here: 141 us
  waiting for transfers between devices  43.4 us (31%)
  blocking collectives  34.5 us (24%)
  starting transfers between devices  31.5 us (22%)
  Pallas kernels  28.5 us (20%)
  local copies, waits for them, and re-layouts  1.71 us (1%)
    ppermute x20, waiting for transfers between devices, shift(): return lax.ppermute(cells, axes if len(axes) > 1 else axes[0], pairs)  43.4 us
    all_to_all x2, blocking collectives, step(): lax.all_to_all(pieces, ('xh', 'z'), split_axis=0, concat_axis=0, tiled=True)  34.5 us
    ppermute x20, starting transfers between devices, shift(): return lax.ppermute(cells, axes if len(axes) > 1 else axes[0], pairs)  31.5 us
    pallas_call x20, Pallas kernels, call(): pl.pallas_call(functools.partial(kernel, **fixed), out_shape=outs, in_spe...  26.8 us
  transfers between devices with their start and end apart: 20, of which 9 were waited for; matrix products, arithmetic and copies ran while one was open for 0% of the time, Pallas kernels for 12%

profile of v7, /device:TPU:2, one launch (start us, length us, event | category | flops | bytes accessed | tf_op | source)
XLA Modules:
  0.0 140.7 jit_solution(13212727986243285197)
XLA Ops:
  0.7 1.6 %collective-permute-start.1 = (bf16[512,1024]{1,0:T(8,128)(2,1)}, bf16[512,1024]{1,0:T(8,128)(2,1)}, u32[]{:S(2)}, u32[]{:S(2)}) collective-permute-start(bf16[512,1024]{1,0:T(8,128)(2,1)} %w0.5), channel_id=1, source_target_pairs={{0,128},{32,160},{64,224},{96,192},{128,32},{160,0},{192,64},{224,... | collective-permute-start | bytes 3145736 | tf_op jit(solution)/shard_map/ppermute | solution.py:29
  2.2 13.8 %collective-permute-done.1.w2 = bf16[512,1024]{1,0:T(8,128)(2,1)} collective-permute-done((bf16[512,1024]{1,0:T(8,128)(2,1)}, bf16[512,1024]{1,0:T(8,128)(2,1)}, u32[]{:S(2)}, u32[]{:S(2)}) %collective-permute-start.1) | collective-permute-done | bytes 1048608 | tf_op jit(solution)/shard_map/ppermute | solution.py:29
  16.1 1.7 %shard_map.102 = (bf16[8,3072]{1,0:T(8,128)(2,1)}, bf16[8,3072]{1,0:T(8,128)(2,1)}) custom-call(s32[1,128]{1,0:T(1,128)} %codes.3, bf16[128,2048]{1,0:T(8,128)(2,1)} %bitcast.8, bf16[128,2048]{1,0:T(8,128)(2,1)} %bitcast.9, bf16[128,1024]{1,0:T(8,128)(2,1)} %bitcast.16, bf16[128,1024]{1,0:T(8,128)(2,1)} %bitcast.17, f32[5,2048]{1,0:T(8,128)} %table.1), custom_call_target="tpu_custom_call" | custom-call | tf_op jit(solution)/shard_map/pallas_call | solution.py:462
  17.8 3.2 %collective-permute-start.3 = (bf16[8,3072]{1,0:T(8,128)(2,1)}, bf16[8,3072]{1,0:T(8,128)(2,1)S(1)}, u32[]{:S(2)}, u32[]{:S(2)}) collective-permute-start(bf16[8,3072]{1,0:T(8,128)(2,1)} %get-tuple-element.43), channel_id=1, source_target_pairs={{0,1},{1,2},{2,3},{3,4},{4,5},{5,6},{6,7},{7,8},{8,9},{9,10},{10,1... | collective-permute-start | bytes 147464 | tf_op jit(solution)/shard_map/ppermute | solution.py:29
  24.1 1.7 %shard_map.101 = (bf16[4,256,512]{2,1,0:T(8,128)(2,1)S(1)}, bf16[4,512,256]{2,1,0:T(8,128)(2,1)S(1)}, f32[256,1024]{1,0:T(8,128)S(1)}, f32[7,1024]{1,0:T(8,128)S(1)}, bf16[16,384]{1,0:T(8,128)(2,1)S(1)}) custom-call(s32[2]{0:T(128)S(1)} %pad_add_fusion.place, s32[1,128]{1,0:T(1,128)S(1)} %copy-done.5, f32[7,1024]{1,0:T(8,128)S(1)} %copy-done.4, ...), custom_call_target="tpu_custom_call" | custom-call | tf_op jit(solution)/shard_map/pallas_call | solution.py:429
  27.3 2.5 %shard_map.103 = (bf16[4,288,512]{2,1,0:T(8,128)(2,1)S(1)}, f32[288,1024]{1,0:T(8,128)S(1)}, f32[288,1024]{1,0:T(8,128)S(1)}) custom-call(s32[2]{0:T(128)S(1)} %pad_add_fusion.place, bf16[4,256,512]{2,1,0:T(8,128)(2,1)S(1)} %get-tuple-element.41.centre, f32[256,1024]{1,0:T(8,128)S(1)} %get-tuple-element.42.up_centre, ...), custom_call_target="tpu_custom_call" | custom-call | tf_op jit(solution)/shard_map/pallas_call | solution.py:429
  29.9 2.2 %shard_map.104.partial = f32[288,1024]{1,0:T(8,128)S(1)} custom-call(bf16[4,288,512]{2,1,0:T(8,128)(2,1)S(1)} %get-tuple-element.45.stacks, f32[288,1024]{1,0:T(8,128)S(1)} %get-tuple-element.46.partial, bf16[512,1024]{1,0:T(8,128)(2,1)} %collective-permute-done.1.w2), custom_call_target="tpu_custom_call" | custom-call | tf_op jit(solution)/shard_map/pallas_call | solution.py:429
  34.8 2.7 %shard_map.108 = (bf16[256,512]{1,0:T(8,128)(2,1)S(1)}, f32[128,512]{1,0:T(8,128)S(1)}, f32[128,512]{1,0:T(8,128)S(1)}, f32[8,512]{1,0:T(8,128)S(1)}) custom-call(bf16[4,288,512]{2,1,0:T(8,128)(2,1)S(1)} %get-tuple-element.45.stacks, f32[288,1024]{1,0:T(8,128)S(1)} %shard_map.104.partial, bf16[512,1024]{1,0:T(8,128)(2,1)S(1)} %collective-permute-done.2.w3, ...), custom_call_target="tpu_custom_call" | custom-call | tf_op jit(solution)/shard_map/pallas_call | solution.py:429
  37.5 3.0 %shard_map.109.refs_2_ = bf16[512,128]{1,0:T(8,128)(2,1)S(1)} custom-call(s32[2]{0:T(128)S(1)} %pad_add_fusion.place, bf16[16,384]{1,0:T(8,128)(2,1)S(1)} %get-tuple-element.51.hot, bf16[512,1024]{1,0:T(8,128)(2,1)S(1)} %copy-done, bf16[512,1024]{1,0:T(8,128)(2,1)S(1)} %collective-permute-done.w1, bf16[512,1024]{1,0:T(8,128)(2,1)} %collective-permute-done.1.w2, ...), custom_call_target="tpu_custom_call" | custom-call | tf_op jit(solution)/shard_map/pallas_call | solution.py:429
  43.4 8.6 %collective-permute-start.7 = (bf16[512,640]{1,0:T(8,128)(2,1)S(1)}, bf16[512,640]{1,0:T(8,128)(2,1)S(1)}, u32[]{:S(2)}, u32[]{:S(2)}) collective-permute-start(bf16[512,640]{1,0:T(8,128)(2,1)S(1)} %shard_map.111.refs_2_), channel_id=1, source_target_pairs={{0,128},{32,160},{64,224},{96,192},{128,32},{160,0},{192,64},{224,... | collective-permute-start | bytes 1966088 | tf_op jit(solution)/shard_map/ppermute | solution.py:29
  54.5 11.2 %collective-permute-done.10.came = bf16[512,512]{1,0:T(8,128)(2,1)S(1)} collective-permute-done((bf16[512,512]{1,0:T(8,128)(2,1)S(1)}, bf16[512,512]{1,0:T(8,128)(2,1)S(1)}, u32[]{:S(2)}, u32[]{:S(2)}) %collective-permute-start.10) | collective-permute-done | bytes 524320 | tf_op jit(solution)/shard_map/ppermute | solution.py:29
  68.0 4.7 %collective-permute-start.15 = (bf16[128,640]{1,0:T(8,128)(2,1)S(1)}, bf16[128,640]{1,0:T(8,128)(2,1)S(1)}, u32[]{:S(2)}, u32[]{:S(2)}) collective-permute-start(bf16[128,640]{1,0:T(8,128)(2,1)S(1)} %get-tuple-element.70), channel_id=1, source_target_pairs={{0,2},{1,3},{2,0},{3,1},{4,6},{5,7},{6,4},{7,5},{8,10},{9,11},{10,... | collective-permute-start | bytes 491528 | tf_op jit(solution)/shard_map/ppermute | solution.py:29
  72.6 1.6 %collective-permute-start.12 = (bf16[128,512]{1,0:T(8,128)(2,1)S(1)}, bf16[128,512]{1,0:T(8,128)(2,1)S(1)}, u32[]{:S(2)}, u32[]{:S(2)}) collective-permute-start(bf16[128,512]{1,0:T(8,128)(2,1)S(1)} %get-tuple-element.67), channel_id=1, source_target_pairs={{0,2},{1,3},{2,0},{3,1},{4,6},{5,7},{6,4},{7,5},{8,10},{9,11},{10,... | collective-permute-start | bytes 393224 | tf_op jit(solution)/shard_map/ppermute | solution.py:29
  74.4 3.0 %collective-permute-start.13 = (bf16[128,512]{1,0:T(8,128)(2,1)S(1)}, bf16[128,512]{1,0:T(8,128)(2,1)S(1)}, u32[]{:S(2)}, u32[]{:S(2)}) collective-permute-start(bf16[128,512]{1,0:T(8,128)(2,1)S(1)} %get-tuple-element.68), channel_id=1, source_target_pairs={{0,3},{1,0},{2,1},{3,2},{4,7},{5,4},{6,5},{7,6},{8,11},{9,8},{10,9... | collective-permute-start | bytes 393224 | tf_op jit(solution)/shard_map/ppermute | solution.py:29
  77.3 5.3 %collective-permute-done.12.refs_2_ = bf16[128,512]{1,0:T(8,128)(2,1)S(1)} collective-permute-done((bf16[128,512]{1,0:T(8,128)(2,1)S(1)}, bf16[128,512]{1,0:T(8,128)(2,1)S(1)}, u32[]{:S(2)}, u32[]{:S(2)}) %collective-permute-start.12) | collective-permute-done | bytes 131104 | tf_op jit(solution)/shard_map/ppermute | solution.py:29
  82.7 2.2 %collective-permute-done.13.refs_3_ = bf16[128,512]{1,0:T(8,128)(2,1)S(1)} collective-permute-done((bf16[128,512]{1,0:T(8,128)(2,1)S(1)}, bf16[128,512]{1,0:T(8,128)(2,1)S(1)}, u32[]{:S(2)}, u32[]{:S(2)}) %collective-permute-start.13) | collective-permute-done | bytes 131104 | tf_op jit(solution)/shard_map/ppermute | solution.py:29
  85.4 18.5 %all_to_all.10.parts = bf16[16,8,1152]{2,1,0:T(8,128)(2,1)S(1)} all-to-all(bf16[16,8,1152]{2,1,0:T(8,128)(2,1)S(1)} %bitcast.19), channel_id=1, replica_groups=mesh['xl'=2,'c'=2,'xh'=2,'z'=8,'y'=4] {'xh','z'}, dimensions={0} | all-to-all | bytes 589824 | tf_op jit(solution)/shard_map/all_to_all | solution.py:608
  104.0 16.0 %all_to_all.11 = bf16[16,8,1152]{2,1,0:T(8,128)(2,1)S(1)} all-to-all(bf16[16,8,1152]{2,1,0:T(8,128)(2,1)S(1)} %shard_map.119), channel_id=1, replica_groups=mesh['xl'=2,'c'=2,'xh'=2,'z'=8,'y'=4] {'xh','z'}, dimensions={0} | all-to-all | bytes 589824 | tf_op jit(solution)/shard_map/all_to_all | solution.py:610
  120.0 4.0 %collective-permute-start.19 = (bf16[128,1152]{1,0:T(8,128)(2,1)S(1)}, bf16[128,1152]{1,0:T(8,128)(2,1)S(1)}, u32[]{:S(2)}, u32[]{:S(2)}) collective-permute-start(bf16[128,1152]{1,0:T(8,128)(2,1)S(1)} %bitcast.11), channel_id=1, source_target_pairs={{0,3},{1,0},{2,1},{3,2},{4,7},{5,4},{6,5},{7,6},{8,11},{9,8},{10,9... | collective-permute-start | bytes 884744 | tf_op jit(solution)/shard_map/ppermute | solution.py:29
  125.2 3.7 %shard_map.113 = (bf16[128,2048]{1,0:T(8,128)(2,1)}, bf16[128,1024]{1,0:T(8,128)(2,1)}) custom-call(s32[2]{0:T(128)S(1)} %pad_add_fusion.place, bf16[512,1024]{1,0:T(8,128)(2,1)S(1)} %copy-done, bf16[512,1024]{1,0:T(8,128)(2,1)S(1)} %collective-permute-done.w1, bf16[512,1024]{1,0:T(8,128)(2,1)} %collective-permute-done.1.w2, ...), custom_call_target="tpu_custom_call" | custom-call | tf_op jit(solution)/shard_map/pallas_call | solution.py:429
  128.8 5.8 %collective-permute-done.19.q3 = bf16[128,1152]{1,0:T(8,128)(2,1)S(1)} collective-permute-done((bf16[128,1152]{1,0:T(8,128)(2,1)S(1)}, bf16[128,1152]{1,0:T(8,128)(2,1)S(1)}, u32[]{:S(2)}, u32[]{:S(2)}) %collective-permute-start.19) | collective-permute-done | bytes 294944 | tf_op jit(solution)/shard_map/ppermute | solution.py:29
  134.6 1.6 %shard_map.120.begun = f32[512,1024]{1,0:T(8,128)} custom-call(s32[2]{0:T(128)S(1)} %pad_add_fusion.place, bf16[128,1152]{1,0:T(8,128)(2,1)S(1)} %bitcast.14, bf16[128,1152]{1,0:T(8,128)(2,1)S(1)} %collective-permute-done.19.q3), custom_call_target="tpu_custom_call" | custom-call | tf_op jit(solution)/shard_map/pallas_call | solution.py:429
  136.2 2.1 %collective-permute-done.17.q1 = bf16[128,1152]{1,0:T(8,128)(2,1)S(1)} collective-permute-done((bf16[128,1152]{1,0:T(8,128)(2,1)S(1)}, bf16[128,1152]{1,0:T(8,128)(2,1)S(1)}, u32[]{:S(2)}, u32[]{:S(2)}) %collective-permute-start.17) | collective-permute-done | bytes 294944 | tf_op jit(solution)/shard_map/ppermute | solution.py:29
  138.3 2.3 %shard_map.121 = (f32[512,1024]{1,0:T(8,128)}, f32[7,1024]{1,0:T(8,128)}, f32[5,2048]{1,0:T(8,128)}) custom-call(s32[2]{0:T(128)S(1)} %pad_add_fusion.place, bf16[128,1152]{1,0:T(8,128)(2,1)S(1)} %bitcast.15, bf16[128,1152]{1,0:T(8,128)(2,1)S(1)} %collective-permute-done.17.q1, ...), custom_call_target="tpu_custom_call", output_to_operand_aliasing={{0}: (5, {})} | custom-call | tf_op jit(solution)/shard_map/pallas_call | solution.py:429
  (52 shorter events, 16.8 us)
Async XLA Ops:
  0.6 21.8 %copy-start.3 = (f32[5,2048]{1,0:T(8,128)S(1)}, f32[5,2048]{1,0:T(8,128)}, u32[]{:S(2)}) copy-start(f32[5,2048]{1,0:T(8,128)} %table.1) | copy-start | bytes 122884
  0.6 21.8 %copy-start.2 = (bf16[1,128,1024]{2,1,0:T(8,128)(2,1)S(1)}, bf16[1,128,1024]{2,1,0:T(8,128)(2,1)}, u32[]{:S(2)}) copy-start(bf16[1,128,1024]{2,1,0:T(8,128)(2,1)} %param.11) | copy-start | bytes 786436
  0.7 21.8 %copy-start.4 = (f32[7,1024]{1,0:T(8,128)S(1)}, f32[7,1024]{1,0:T(8,128)}, u32[]{:S(2)}) copy-start(f32[7,1024]{1,0:T(8,128)} %taps.1) | copy-start | bytes 86020
  0.7 15.4 %collective-permute-start.1 = (bf16[512,1024]{1,0:T(8,128)(2,1)}, bf16[512,1024]{1,0:T(8,128)(2,1)}, u32[]{:S(2)}, u32[]{:S(2)}) collective-permute-start(bf16[512,1024]{1,0:T(8,128)(2,1)} %w0.5), channel_id=1, source_target_pairs={{0,128},{32,160},{64,224},{96,192},{128,32},{160,0},{192,64},{224,... | collective-permute-start | bytes 3145736 | tf_op jit(solution)/shard_map/ppermute | solution.py:29
  2.2 25.1 %collective-permute-start = (bf16[512,1024]{1,0:T(8,128)(2,1)}, bf16[512,1024]{1,0:T(8,128)(2,1)S(1)}, u32[]{:S(2)}, u32[]{:S(2)}) collective-permute-start(bf16[512,1024]{1,0:T(8,128)(2,1)} %w0.5), channel_id=1, source_target_pairs={{0,64},{64,0},{1,65},{65,1},{2,66},{66,2},{3,67},{67,3},{4,68},{68... | collective-permute-start | bytes 3145736 | tf_op jit(solution)/shard_map/ppermute | solution.py:29
  16.1 16.0 %collective-permute-start.2 = (bf16[512,1024]{1,0:T(8,128)(2,1)}, bf16[512,1024]{1,0:T(8,128)(2,1)S(1)}, u32[]{:S(2)}, u32[]{:S(2)}) collective-permute-start(bf16[512,1024]{1,0:T(8,128)(2,1)} %collective-permute-done.1.w2), channel_id=1, source_target_pairs={{0,64},{64,0},{1,65},{65,1},{2,66},{66,2},{3,67},{67,3},{4,68},{68... | collective-permute-start | bytes 3145736 | tf_op jit(solution)/shard_map/ppermute | solution.py:29
  16.1 11.3 %copy-start = (bf16[512,1024]{1,0:T(8,128)(2,1)S(1)}, bf16[512,1024]{1,0:T(8,128)(2,1)}, u32[]{:S(2)}) copy-start(bf16[512,1024]{1,0:T(8,128)(2,1)} %w0.5) | copy-start | bytes 3145732
  17.8 8.0 %collective-permute-start.3 = (bf16[8,3072]{1,0:T(8,128)(2,1)}, bf16[8,3072]{1,0:T(8,128)(2,1)S(1)}, u32[]{:S(2)}, u32[]{:S(2)}) collective-permute-start(bf16[8,3072]{1,0:T(8,128)(2,1)} %get-tuple-element.43), channel_id=1, source_target_pairs={{0,1},{1,2},{2,3},{3,4},{4,5},{5,6},{6,7},{7,8},{8,9},{9,10},{10,1... | collective-permute-start | bytes 147464 | tf_op jit(solution)/shard_map/ppermute | solution.py:29
  21.0 6.3 %collective-permute-start.4 = (bf16[8,3072]{1,0:T(8,128)(2,1)}, bf16[8,3072]{1,0:T(8,128)(2,1)}, u32[]{:S(2)}, u32[]{:S(2)}) collective-permute-start(bf16[8,3072]{1,0:T(8,128)(2,1)} %get-tuple-element.44), channel_id=1, source_target_pairs={{1,0},{2,1},{3,2},{4,3},{5,4},{6,5},{7,6},{8,7},{9,8},{10,9},{11,1... | collective-permute-start | bytes 147464 | tf_op jit(solution)/shard_map/ppermute | solution.py:29
  40.9 2.2 %collective-permute-start.6 = (bf16[512,640]{1,0:T(8,128)(2,1)S(1)}, bf16[512,640]{1,0:T(8,128)(2,1)S(1)}, u32[]{:S(2)}, u32[]{:S(2)}) collective-permute-start(bf16[512,640]{1,0:T(8,128)(2,1)S(1)} %shard_map.110), channel_id=1, source_target_pairs={{0,64},{64,0},{1,65},{65,1},{2,66},{66,2},{3,67},{67,3},{4,68},{68... | collective-permute-start | bytes 1966088 | tf_op jit(solution)/shard_map/ppermute | solution.py:29
  41.3 11.1 %collective-permute-start.9 = (bf16[512,512]{1,0:T(8,128)(2,1)S(1)}, bf16[512,512]{1,0:T(8,128)(2,1)S(1)}, u32[]{:S(2)}, u32[]{:S(2)}) collective-permute-start(bf16[512,512]{1,0:T(8,128)(2,1)S(1)} %shard_map.115), channel_id=1, source_target_pairs={{0,64},{64,0},{1,65},{65,1},{2,66},{66,2},{3,67},{67,3},{4,68},{68... | collective-permute-start | bytes 1572872 | tf_op jit(solution)/shard_map/ppermute | solution.py:29
  43.4 23.5 %collective-permute-start.7 = (bf16[512,640]{1,0:T(8,128)(2,1)S(1)}, bf16[512,640]{1,0:T(8,128)(2,1)S(1)}, u32[]{:S(2)}, u32[]{:S(2)}) collective-permute-start(bf16[512,640]{1,0:T(8,128)(2,1)S(1)} %shard_map.111.refs_2_), channel_id=1, source_target_pairs={{0,128},{32,160},{64,224},{96,192},{128,32},{160,0},{192,64},{224,... | collective-permute-start | bytes 1966088 | tf_op jit(solution)/shard_map/ppermute | solution.py:29
  52.2 2.2 %collective-permute-start.8 = (bf16[512,512]{1,0:T(8,128)(2,1)S(1)}, bf16[512,512]{1,0:T(8,128)(2,1)S(1)}, u32[]{:S(2)}, u32[]{:S(2)}) collective-permute-start(bf16[512,512]{1,0:T(8,128)(2,1)S(1)} %shard_map.114), channel_id=1, source_target_pairs={{0,64},{64,0},{1,65},{65,1},{2,66},{66,2},{3,67},{67,3},{4,68},{68... | collective-permute-start | bytes 1572872 | tf_op jit(solution)/shard_map/ppermute | solution.py:29
  52.7 13.0 %collective-permute-start.10 = (bf16[512,512]{1,0:T(8,128)(2,1)S(1)}, bf16[512,512]{1,0:T(8,128)(2,1)S(1)}, u32[]{:S(2)}, u32[]{:S(2)}) collective-permute-start(bf16[512,512]{1,0:T(8,128)(2,1)S(1)} %shard_map.116), channel_id=1, source_target_pairs={{0,128},{32,160},{64,224},{96,192},{128,32},{160,0},{192,64},{224,... | collective-permute-start | bytes 1572872 | tf_op jit(solution)/shard_map/ppermute | solution.py:29
  53.9 12.9 %collective-permute-start.5 = (bf16[512,512]{1,0:T(8,128)(2,1)S(1)}, bf16[512,512]{1,0:T(8,128)(2,1)S(1)}, u32[]{:S(2)}, u32[]{:S(2)}) collective-permute-start(bf16[512,512]{1,0:T(8,128)(2,1)S(1)} %shard_map.107), channel_id=1, source_target_pairs={{0,64},{64,0},{1,65},{65,1},{2,66},{66,2},{3,67},{67,3},{4,68},{68... | collective-permute-start | bytes 1572872 | tf_op jit(solution)/shard_map/ppermute | solution.py:29
  66.7 7.7 %collective-permute-start.11 = (bf16[128,512]{1,0:T(8,128)(2,1)S(1)}, bf16[128,512]{1,0:T(8,128)(2,1)S(1)}, u32[]{:S(2)}, u32[]{:S(2)}) collective-permute-start(bf16[128,512]{1,0:T(8,128)(2,1)S(1)} %get-tuple-element.66), channel_id=1, source_target_pairs={{0,1},{1,2},{2,3},{3,0},{4,5},{5,6},{6,7},{7,4},{8,9},{9,10},{10,1... | collective-permute-start | bytes 393224 | tf_op jit(solution)/shard_map/ppermute | solution.py:29
  67.9 17.0 %collective-permute-start.14 = (bf16[128,640]{1,0:T(8,128)(2,1)S(1)}, bf16[128,640]{1,0:T(8,128)(2,1)S(1)}, u32[]{:S(2)}, u32[]{:S(2)}) collective-permute-start(bf16[128,640]{1,0:T(8,128)(2,1)S(1)} %get-tuple-element.69), channel_id=1, source_target_pairs={{0,1},{1,2},{2,3},{3,0},{4,5},{5,6},{6,7},{7,4},{8,9},{9,10},{10,1... | collective-permute-start | bytes 491528 | tf_op jit(solution)/shard_map/ppermute | solution.py:29
  68.0 16.9 %collective-permute-start.15 = (bf16[128,640]{1,0:T(8,128)(2,1)S(1)}, bf16[128,640]{1,0:T(8,128)(2,1)S(1)}, u32[]{:S(2)}, u32[]{:S(2)}) collective-permute-start(bf16[128,640]{1,0:T(8,128)(2,1)S(1)} %get-tuple-element.70), channel_id=1, source_target_pairs={{0,2},{1,3},{2,0},{3,1},{4,6},{5,7},{6,4},{7,5},{8,10},{9,11},{10,... | collective-permute-start | bytes 491528 | tf_op jit(solution)/shard_map/ppermute | solution.py:29
  72.6 12.3 %collective-permute-start.16 = (bf16[128,640]{1,0:T(8,128)(2,1)S(1)}, bf16[128,640]{1,0:T(8,128)(2,1)S(1)}, u32[]{:S(2)}, u32[]{:S(2)}) collective-permute-start(bf16[128,640]{1,0:T(8,128)(2,1)S(1)} %get-tuple-element.71), channel_id=1, source_target_pairs={{0,3},{1,0},{2,1},{3,2},{4,7},{5,4},{6,5},{7,6},{8,11},{9,8},{10,9... | collective-permute-start | bytes 491528 | tf_op jit(solution)/shard_map/ppermute | solution.py:29
  72.6 10.0 %collective-permute-start.12 = (bf16[128,512]{1,0:T(8,128)(2,1)S(1)}, bf16[128,512]{1,0:T(8,128)(2,1)S(1)}, u32[]{:S(2)}, u32[]{:S(2)}) collective-permute-start(bf16[128,512]{1,0:T(8,128)(2,1)S(1)} %get-tuple-element.67), channel_id=1, source_target_pairs={{0,2},{1,3},{2,0},{3,1},{4,6},{5,7},{6,4},{7,5},{8,10},{9,11},{10,... | collective-permute-start | bytes 393224 | tf_op jit(solution)/shard_map/ppermute | solution.py:29
  74.4 10.5 %collective-permute-start.13 = (bf16[128,512]{1,0:T(8,128)(2,1)S(1)}, bf16[128,512]{1,0:T(8,128)(2,1)S(1)}, u32[]{:S(2)}, u32[]{:S(2)}) collective-permute-start(bf16[128,512]{1,0:T(8,128)(2,1)S(1)} %get-tuple-element.68), channel_id=1, source_target_pairs={{0,3},{1,0},{2,1},{3,2},{4,7},{5,4},{6,5},{7,6},{8,11},{9,8},{10,9... | collective-permute-start | bytes 393224 | tf_op jit(solution)/shard_map/ppermute | solution.py:29
  120.0 14.6 %collective-permute-start.19 = (bf16[128,1152]{1,0:T(8,128)(2,1)S(1)}, bf16[128,1152]{1,0:T(8,128)(2,1)S(1)}, u32[]{:S(2)}, u32[]{:S(2)}) collective-permute-start(bf16[128,1152]{1,0:T(8,128)(2,1)S(1)} %bitcast.11), channel_id=1, source_target_pairs={{0,3},{1,0},{2,1},{3,2},{4,7},{5,4},{6,5},{7,6},{8,11},{9,8},{10,9... | collective-permute-start | bytes 884744 | tf_op jit(solution)/shard_map/ppermute | solution.py:29
  124.0 12.2 %collective-permute-start.18 = (bf16[128,1152]{1,0:T(8,128)(2,1)S(1)}, bf16[128,1152]{1,0:T(8,128)(2,1)S(1)}, u32[]{:S(2)}, u32[]{:S(2)}) collective-permute-start(bf16[128,1152]{1,0:T(8,128)(2,1)S(1)} %bitcast.12), channel_id=1, source_target_pairs={{0,2},{1,3},{2,0},{3,1},{4,6},{5,7},{6,4},{7,5},{8,10},{9,11},{10,... | collective-permute-start | bytes 884744 | tf_op jit(solution)/shard_map/ppermute | solution.py:29
  125.2 13.1 %collective-permute-start.17 = (bf16[128,1152]{1,0:T(8,128)(2,1)S(1)}, bf16[128,1152]{1,0:T(8,128)(2,1)S(1)}, u32[]{:S(2)}, u32[]{:S(2)}) collective-permute-start(bf16[128,1152]{1,0:T(8,128)(2,1)S(1)} %bitcast.13), channel_id=1, source_target_pairs={{0,1},{1,2},{2,3},{3,0},{4,5},{5,6},{6,7},{7,4},{8,9},{9,10},{10,1... | collective-permute-start | bytes 884744 | tf_op jit(solution)/shard_map/ppermute | solution.py:29
  (2 other events, 1.7 us)

commit v8 on v6

--- a/solution.py
+++ b/solution.py
@@ -140,28 +140,27 @@
     ups[rows:] = turned(up[...], turn)
 
 
-def early_kernel(place, centre, up_centre, before, after, w0, w1, stacks, ups, partial):
-    rows = up_centre.shape[0] // 2
-    features = 4 * centre.shape[2]
-    width = centre.shape[2]
-    total = rows + 2 * EDGE
+def early_kernel(centre, w0, w1, partial):
+    add_products(partial, None, ((centre.at[0], w0), (centre.at[1], w1)))
+
+
+def halo_kernel(place, before, after, w0, w1, halos, ups, partial):
+    width = halos.shape[2]
+    features = 4 * width
+    size = 2 * EDGE
     turn = turning(256)
     for r in range(4):
         cols = pl.ds(pl.multiple_of((place[0] ^ r) * width, width), width)
-        halo = jnp.concatenate([before[:, cols].astype(jnp.float32), after[:, cols].astype(jnp.float32)], axis=0)
-        halo = halo.astype(jnp.bfloat16)
-        stacks[r, : 2 * rows] = centre[r]
-        stacks[r, 2 * rows : 2 * rows + 2 * EDGE] = halo
-        stacks[3 - r, 2 * rows + 2 * EDGE :] = turned(halo, turn).astype(jnp.bfloat16)
-    for way in range(2):
-        base = way * total
-        ups[base + EDGE : base + EDGE + rows] = up_centre[way * rows : (way + 1) * rows]
-        for part, start in ((before, base), (after, base + EDGE + rows)):
-            cells = part[:, features:].astype(jnp.float32)
-            if way == 1:
-                cells = turned(cells.astype(jnp.bfloat16), turn)
-            ups[start : start + EDGE] = cells
-    add_products(partial, None, ((stacks.at[0], w0), (stacks.at[1], w1)))
+        rows = jnp.concatenate([before[:, cols].astype(jnp.float32), after[:, cols].astype(jnp.float32)], axis=0)
+        rows = rows.astype(jnp.bfloat16)
+        halos[r, :size] = rows
+        halos[3 - r, size:] = turned(rows, turn).astype(jnp.bfloat16)
+    up = jnp.concatenate(
+        [before[:, features:].astype(jnp.float32), after[:, features:].astype(jnp.float32)], axis=0
+    ).astype(jnp.bfloat16)
+    ups[:size] = up.astype(jnp.float32)
+    ups[size:] = turned(up, turn)
+    add_products(partial, None, ((halos.at[0], w0), (halos.at[1], w1)))
 
 
 def add_products(out, start, pairs):
@@ -176,21 +175,35 @@
     lax.fori_loop(0, out.shape[1] // 256, step, 0)
 
 
-def middle_kernel(stacks, partial, w2, out):
-    add_products(out, partial, ((stacks.at[2], w2),))
-
-
-def strand_kernel(stacks, partial, w3, ups, taps, grads, ahead, behind, sums, values, mixes, *, first):
-    total = stacks.shape[1] // 2
-    rows = total - 2 * EDGE
+def middle_kernel(centre, halos, partial, partial_halo, w2, out, rows):
+    size = centre.shape[1]
+    rows[:size] = centre[2]
+    rows[size:] = halos[2]
+
+    def step(at, _):
+        cols = pl.ds(pl.multiple_of(at * 256, 256), 256)
+        start = jnp.concatenate([partial[:, cols], partial_halo[:, cols]], axis=0)
+        out[:, cols] = start + dot(rows[...], w2[:, cols])
+        return 0
+
+    lax.fori_loop(0, out.shape[1] // 256, step, 0)
+
+
+def strand_kernel(
+    centre, halos, partial, w3, ups, ups_halo, taps, grads, ahead, behind, sums, values, mixes, stack, *, first
+):
+    rows = centre.shape[1] // 2
+    total = rows + 2 * EDGE
     units = sums.shape[1]
+    stack[: 2 * rows] = centre[3]
+    stack[2 * rows :] = halos[3]
     count = units // LANES
     turn = turning(LANES)
 
     def project(at, _):
         near = pl.ds(pl.multiple_of(at * 256, 256), 256)
         cols = pl.ds(pl.multiple_of(first + at * 256, 256), 256)
-        acc = partial[:, cols] + dot(stacks[3], w3[:, cols])
+        acc = partial[:, cols] + dot(stack[...], w3[:, cols])
         acc = acc.astype(jnp.bfloat16).astype(jnp.float32)
         for way in range(2):
             base = way * total
@@ -212,7 +225,15 @@
             linear = values[base : base + total, near]
             logistic = jax.nn.sigmoid(linear)
             gating = linear * logistic
-            up = ups[base : base + total, cols]
+            halo = way * 2 * EDGE
+            up = jnp.concatenate(
+                [
+                    ups_halo[halo : halo + EDGE, cols],
+                    ups[way * rows : (way + 1) * rows, cols],
+                    ups_halo[halo + EDGE : halo + 2 * EDGE, cols],
+                ],
+                axis=0,
+            )
             grad_mix = up * gating
             mixes[way] = grad_mix
             mid = slice(EDGE, EDGE + rows)
@@ -404,7 +425,7 @@
     if scalar:
         specs[0] = pl.BlockSpec(memory_space=pltpu.SMEM)
     for at in unread:
-        specs[at] = pl.BlockSpec(memory_space=pl.ANY)
+        specs[at] = pl.BlockSpec(memory_space=pltpu.HBM if kernel is centre_kernel else pl.ANY)
     return pl.pallas_call(
         functools.partial(kernel, **fixed),
         out_shape=outs,
@@ -478,19 +499,30 @@
             pltpu.SemaphoreType.DMA((3,)),
         ),
     )
-    wide = array((2 * total, units), jnp.float32)
-    stacks, ups, partial = call(
-        early_kernel,
-        (array((4, 2 * total, width)), wide, wide),
+    partial = call(early_kernel, array((2 * rows, units), jnp.float32), centre, *weights[:2])
+    halos, ups_halo, partial_halo = call(
+        halo_kernel,
+        (
+            array((4, 4 * EDGE, width)),
+            array((4 * EDGE, units), jnp.float32),
+            array((4 * EDGE, units), jnp.float32),
+        ),
         place,
-        centre,
-        up_centre,
         before,
         after,
         *weights[:2],
         scalar=True,
     )
-    partial = call(middle_kernel, wide, stacks, partial, weights[2])
+    partial = call(
+        middle_kernel,
+        array((2 * total, units), jnp.float32),
+        centre,
+        halos,
+        partial,
+        partial_halo,
+        weights[2],
+        scratch=(pltpu.VMEM((2 * total, width), jnp.bfloat16),),
+    )
     ends = (0, units // 2, units // 4 * 3, units)
     parts = []
     for at in range(3):
@@ -504,12 +536,18 @@
                     array((rows, size), jnp.float32),
                     array((8, size), jnp.float32),
                 ),
-                stacks,
+                centre,
+                halos,
                 partial,
                 weights[3],
-                ups,
+                up_centre,
+                ups_halo,
                 taps,
-                scratch=(pltpu.VMEM((2 * total, size), jnp.float32), pltpu.VMEM((2, total, LANES), jnp.float32)),
+                scratch=(
+                    pltpu.VMEM((2 * total, size), jnp.float32),
+                    pltpu.VMEM((2, total, LANES), jnp.float32),
+                    pltpu.VMEM((2 * total, width), jnp.bfloat16),
+                ),
                 first=ends[at],
             )
         )

time: 141 us -> 144 us (1.021)
  local copies, waits for them, and re-layouts: 1.71 us -> 4.25 us
  waiting for transfers between devices: 44.9 us -> 43.4 us
    unnamed x12, local copies, waits for them, and re-layouts: 1.71 us -> 4.25 us
    ppermute x20, waiting for transfers between devices: 44.9 us -> 43.4 us  [shift(): return lax.ppermute(cells, axes if len(axes) > 1 else axes[0], pairs)]
    pallas_call x19 -> x20, Pallas kernels: 25.1 us -> 25.6 us  [call(): pl.pallas_call(functools.partial(kernel, **fixed), out_shape=outs, in_spe...]
  transfers between devices with their start and end apart: 20 -> 20, of which waited for: 10 -> 9; matrix products, arithmetic and copies ran while one was open for 0% -> 0% of each run, Pallas kernels for 11% -> 11%
where the time goes in v8:
time: 144 us; the launch traced here: 143 us
  waiting for transfers between devices  43.4 us (30%)
  blocking collectives  34.5 us (24%)
  starting transfers between devices  32.8 us (23%)
  Pallas kernels  27.2 us (19%)
  local copies, waits for them, and re-layouts  4.25 us (3%)
    ppermute x20, waiting for transfers between devices, shift(): return lax.ppermute(cells, axes if len(axes) > 1 else axes[0], pairs)  43.4 us
    all_to_all x2, blocking collectives, step(): lax.all_to_all(pieces, ('xh', 'z'), split_axis=0, concat_axis=0, tiled=True)  34.5 us
    ppermute x20, starting transfers between devices, shift(): return lax.ppermute(cells, axes if len(axes) > 1 else axes[0], pairs)  32.8 us
    pallas_call x20, Pallas kernels, call(): pl.pallas_call(functools.partial(kernel, **fixed), out_shape=outs, in_spe...  25.6 us
    unnamed x12, local copies, waits for them, and re-layouts  4.25 us
  transfers between devices with their start and end apart: 20, of which 9 were waited for; matrix products, arithmetic and copies ran while one was open for 0% of the time, Pallas kernels for 11%

profile of v8, /device:TPU:2, one launch (start us, length us, event | category | flops | bytes accessed | tf_op | source)
XLA Modules:
  0.0 143.1 jit_solution(4612756879467672728)
XLA Ops:
  0.6 1.6 %collective-permute-start.1 = (bf16[512,1024]{1,0:T(8,128)(2,1)}, bf16[512,1024]{1,0:T(8,128)(2,1)}, u32[]{:S(2)}, u32[]{:S(2)}) collective-permute-start(bf16[512,1024]{1,0:T(8,128)(2,1)} %w0.7), channel_id=1, source_target_pairs={{0,128},{32,160},{64,224},{96,192},{128,32},{160,0},{192,64},{224,... | collective-permute-start | bytes 3145736 | tf_op jit(solution)/shard_map/ppermute | solution.py:29
  2.2 13.8 %collective-permute-done.1.w2 = bf16[512,1024]{1,0:T(8,128)(2,1)} collective-permute-done((bf16[512,1024]{1,0:T(8,128)(2,1)}, bf16[512,1024]{1,0:T(8,128)(2,1)}, u32[]{:S(2)}, u32[]{:S(2)}) %collective-permute-start.1) | collective-permute-done | bytes 1048608 | tf_op jit(solution)/shard_map/ppermute | solution.py:29
  16.1 1.6 %shard_map.102 = (bf16[8,3072]{1,0:T(8,128)(2,1)}, bf16[8,3072]{1,0:T(8,128)(2,1)}) custom-call(s32[1,128]{1,0:T(1,128)} %codes.3, bf16[128,2048]{1,0:T(8,128)(2,1)} %bitcast.8, bf16[128,2048]{1,0:T(8,128)(2,1)} %bitcast.9, bf16[128,1024]{1,0:T(8,128)(2,1)} %bitcast.11, bf16[128,1024]{1,0:T(8,128)(2,1)} %bitcast.12, f32[5,2048]{1,0:T(8,128)} %table.1), custom_call_target="tpu_custom_call" | custom-call | tf_op jit(solution)/shard_map/pallas_call | solution.py:461
  17.7 3.2 %collective-permute-start.3 = (bf16[8,3072]{1,0:T(8,128)(2,1)}, bf16[8,3072]{1,0:T(8,128)(2,1)S(1)}, u32[]{:S(2)}, u32[]{:S(2)}) collective-permute-start(bf16[8,3072]{1,0:T(8,128)(2,1)} %get-tuple-element.42), channel_id=1, source_target_pairs={{0,1},{1,2},{2,3},{3,4},{4,5},{5,6},{6,7},{7,8},{8,9},{9,10},{10,1... | collective-permute-start | bytes 147464 | tf_op jit(solution)/shard_map/ppermute | solution.py:29
  26.6 1.7 %shard_map.101 = (bf16[4,256,512]{2,1,0:T(8,128)(2,1)S(1)}, bf16[4,512,256]{2,1,0:T(8,128)(2,1)S(1)}, f32[256,1024]{1,0:T(8,128)S(1)}, f32[7,1024]{1,0:T(8,128)S(1)}, bf16[16,384]{1,0:T(8,128)(2,1)S(1)}) custom-call(s32[2]{0:T(128)S(1)} %pad_add_fusion.place, s32[1,128]{1,0:T(1,128)S(1)} %copy-done.5, f32[7,1024]{1,0:T(8,128)S(1)} %copy-done.4, ...), custom_call_target="tpu_custom_call" | custom-call | tf_op jit(solution)/shard_map/pallas_call | solution.py:429
  29.5 1.7 %shard_map.103 = (bf16[4,32,512]{2,1,0:T(8,128)(2,1)S(1)}, f32[32,1024]{1,0:T(8,128)S(1)}, f32[32,1024]{1,0:T(8,128)S(1)}) custom-call(s32[2]{0:T(128)S(1)} %pad_add_fusion.place, bf16[8,3072]{1,0:T(8,128)(2,1)S(1)} %collective-permute-done.3.before, bf16[8,3072]{1,0:T(8,128)(2,1)S(1)} %collective-permute-done.4.after, bf16[512,1024]{1,0:T(8,128)(2,1)S(1)} %copy-done, ...), custom_call_target="tpu_custom_call" | custom-call | tf_op jit(solution)/shard_map/pallas_call | solution.py:429
  31.2 2.2 %shard_map.105.partial = f32[288,1024]{1,0:T(8,128)S(1)} custom-call(bf16[4,256,512]{2,1,0:T(8,128)(2,1)S(1)} %get-tuple-element.41.centre, bf16[4,32,512]{2,1,0:T(8,128)(2,1)S(1)} %get-tuple-element.44.halos, f32[256,1024]{1,0:T(8,128)S(1)} %shard_map.104.partial, f32[32,1024]{1,0:T(8,128)S(1)} %get-tuple-element.45.partial_halo, ...), custom_call_target="tpu_custom_call" | custom-call | tf_op jit(solution)/shard_map/pallas_call | solution.py:429
  33.5 1.3 shard_map.107
  36.2 2.8 %shard_map.109 = (bf16[256,512]{1,0:T(8,128)(2,1)S(1)}, f32[128,512]{1,0:T(8,128)S(1)}, f32[128,512]{1,0:T(8,128)S(1)}, f32[8,512]{1,0:T(8,128)S(1)}) custom-call(bf16[4,256,512]{2,1,0:T(8,128)(2,1)S(1)} %get-tuple-element.41.centre, bf16[4,32,512]{2,1,0:T(8,128)(2,1)S(1)} %get-tuple-element.44.halos, f32[288,1024]{1,0:T(8,128)S(1)} %shard_map.105.partial, ...), custom_call_target="tpu_custom_call" | custom-call | tf_op jit(solution)/shard_map/pallas_call | solution.py:429
  38.9 3.0 %shard_map.110.refs_2_ = bf16[512,128]{1,0:T(8,128)(2,1)S(1)} custom-call(s32[2]{0:T(128)S(1)} %pad_add_fusion.place, bf16[16,384]{1,0:T(8,128)(2,1)S(1)} %get-tuple-element.51.hot, bf16[512,1024]{1,0:T(8,128)(2,1)S(1)} %copy-done, bf16[512,1024]{1,0:T(8,128)(2,1)S(1)} %collective-permute-done.w1, bf16[512,1024]{1,0:T(8,128)(2,1)} %collective-permute-done.1.w2, ...), custom_call_target="tpu_custom_call" | custom-call | tf_op jit(solution)/shard_map/pallas_call | solution.py:429
  44.8 10.1 %collective-permute-start.7 = (bf16[512,640]{1,0:T(8,128)(2,1)S(1)}, bf16[512,640]{1,0:T(8,128)(2,1)S(1)}, u32[]{:S(2)}, u32[]{:S(2)}) collective-permute-start(bf16[512,640]{1,0:T(8,128)(2,1)S(1)} %shard_map.112.refs_2_), channel_id=1, source_target_pairs={{0,128},{32,160},{64,224},{96,192},{128,32},{160,0},{192,64},{224,... | collective-permute-start | bytes 1966088 | tf_op jit(solution)/shard_map/ppermute | solution.py:29
  57.3 11.2 %collective-permute-done.10.came = bf16[512,512]{1,0:T(8,128)(2,1)S(1)} collective-permute-done((bf16[512,512]{1,0:T(8,128)(2,1)S(1)}, bf16[512,512]{1,0:T(8,128)(2,1)S(1)}, u32[]{:S(2)}, u32[]{:S(2)}) %collective-permute-start.10) | collective-permute-done | bytes 524320 | tf_op jit(solution)/shard_map/ppermute | solution.py:29
  70.9 4.7 %collective-permute-start.15 = (bf16[128,640]{1,0:T(8,128)(2,1)S(1)}, bf16[128,640]{1,0:T(8,128)(2,1)S(1)}, u32[]{:S(2)}, u32[]{:S(2)}) collective-permute-start(bf16[128,640]{1,0:T(8,128)(2,1)S(1)} %get-tuple-element.70), channel_id=1, source_target_pairs={{0,2},{1,3},{2,0},{3,1},{4,6},{5,7},{6,4},{7,5},{8,10},{9,11},{10,... | collective-permute-start | bytes 491528 | tf_op jit(solution)/shard_map/ppermute | solution.py:29
  75.6 1.6 %collective-permute-start.12 = (bf16[128,512]{1,0:T(8,128)(2,1)S(1)}, bf16[128,512]{1,0:T(8,128)(2,1)S(1)}, u32[]{:S(2)}, u32[]{:S(2)}) collective-permute-start(bf16[128,512]{1,0:T(8,128)(2,1)S(1)} %get-tuple-element.67), channel_id=1, source_target_pairs={{0,2},{1,3},{2,0},{3,1},{4,6},{5,7},{6,4},{7,5},{8,10},{9,11},{10,... | collective-permute-start | bytes 393224 | tf_op jit(solution)/shard_map/ppermute | solution.py:29
  77.3 3.0 %collective-permute-start.13 = (bf16[128,512]{1,0:T(8,128)(2,1)S(1)}, bf16[128,512]{1,0:T(8,128)(2,1)S(1)}, u32[]{:S(2)}, u32[]{:S(2)}) collective-permute-start(bf16[128,512]{1,0:T(8,128)(2,1)S(1)} %get-tuple-element.68), channel_id=1, source_target_pairs={{0,3},{1,0},{2,1},{3,2},{4,7},{5,4},{6,5},{7,6},{8,11},{9,8},{10,9... | collective-permute-start | bytes 393224 | tf_op jit(solution)/shard_map/ppermute | solution.py:29
  80.3 5.3 %collective-permute-done.12.refs_2_ = bf16[128,512]{1,0:T(8,128)(2,1)S(1)} collective-permute-done((bf16[128,512]{1,0:T(8,128)(2,1)S(1)}, bf16[128,512]{1,0:T(8,128)(2,1)S(1)}, u32[]{:S(2)}, u32[]{:S(2)}) %collective-permute-start.12) | collective-permute-done | bytes 131104 | tf_op jit(solution)/shard_map/ppermute | solution.py:29
  85.6 2.2 %collective-permute-done.13.refs_3_ = bf16[128,512]{1,0:T(8,128)(2,1)S(1)} collective-permute-done((bf16[128,512]{1,0:T(8,128)(2,1)S(1)}, bf16[128,512]{1,0:T(8,128)(2,1)S(1)}, u32[]{:S(2)}, u32[]{:S(2)}) %collective-permute-start.13) | collective-permute-done | bytes 131104 | tf_op jit(solution)/shard_map/ppermute | solution.py:29
  88.3 18.5 %all_to_all.10.parts = bf16[16,8,1152]{2,1,0:T(8,128)(2,1)S(1)} all-to-all(bf16[16,8,1152]{2,1,0:T(8,128)(2,1)S(1)} %bitcast.18), channel_id=1, replica_groups=mesh['xl'=2,'c'=2,'xh'=2,'z'=8,'y'=4] {'xh','z'}, dimensions={0} | all-to-all | bytes 589824 | tf_op jit(solution)/shard_map/all_to_all | solution.py:624
  106.9 16.0 %all_to_all.11 = bf16[16,8,1152]{2,1,0:T(8,128)(2,1)S(1)} all-to-all(bf16[16,8,1152]{2,1,0:T(8,128)(2,1)S(1)} %shard_map.120), channel_id=1, replica_groups=mesh['xl'=2,'c'=2,'xh'=2,'z'=8,'y'=4] {'xh','z'}, dimensions={0} | all-to-all | bytes 589824 | tf_op jit(solution)/shard_map/all_to_all | solution.py:626
  122.9 4.1 %collective-permute-start.19 = (bf16[128,1152]{1,0:T(8,128)(2,1)S(1)}, bf16[128,1152]{1,0:T(8,128)(2,1)S(1)}, u32[]{:S(2)}, u32[]{:S(2)}) collective-permute-start(bf16[128,1152]{1,0:T(8,128)(2,1)S(1)} %bitcast.14), channel_id=1, source_target_pairs={{0,3},{1,0},{2,1},{3,2},{4,7},{5,4},{6,5},{7,6},{8,11},{9,8},{10,9... | collective-permute-start | bytes 884744 | tf_op jit(solution)/shard_map/ppermute | solution.py:29
  127.9 3.7 %shard_map.114 = (bf16[128,2048]{1,0:T(8,128)(2,1)}, bf16[128,1024]{1,0:T(8,128)(2,1)}) custom-call(s32[2]{0:T(128)S(1)} %pad_add_fusion.place, bf16[512,1024]{1,0:T(8,128)(2,1)S(1)} %copy-done, bf16[512,1024]{1,0:T(8,128)(2,1)S(1)} %collective-permute-done.w1, bf16[512,1024]{1,0:T(8,128)(2,1)} %collective-permute-done.1.w2, ...), custom_call_target="tpu_custom_call" | custom-call | tf_op jit(solution)/shard_map/pallas_call | solution.py:429
  131.5 6.0 %collective-permute-done.19.q3 = bf16[128,1152]{1,0:T(8,128)(2,1)S(1)} collective-permute-done((bf16[128,1152]{1,0:T(8,128)(2,1)S(1)}, bf16[128,1152]{1,0:T(8,128)(2,1)S(1)}, u32[]{:S(2)}, u32[]{:S(2)}) %collective-permute-start.19) | collective-permute-done | bytes 294944 | tf_op jit(solution)/shard_map/ppermute | solution.py:29
  138.2 2.8 %collective-permute-done.17.q1 = bf16[128,1152]{1,0:T(8,128)(2,1)S(1)} collective-permute-done((bf16[128,1152]{1,0:T(8,128)(2,1)S(1)}, bf16[128,1152]{1,0:T(8,128)(2,1)S(1)}, u32[]{:S(2)}, u32[]{:S(2)}) %collective-permute-start.17) | collective-permute-done | bytes 294944 | tf_op jit(solution)/shard_map/ppermute | solution.py:29
  141.0 2.1 %shard_map.121 = (f32[512,1024]{1,0:T(8,128)}, f32[7,1024]{1,0:T(8,128)}, f32[5,2048]{1,0:T(8,128)}) custom-call(s32[2]{0:T(128)S(1)} %pad_add_fusion.place, bf16[128,1152]{1,0:T(8,128)(2,1)S(1)} %bitcast.17, bf16[128,1152]{1,0:T(8,128)(2,1)S(1)} %collective-permute-done.17.q1, bf16[128,1152]{1,0:T(8,128)(2,1)S(1)} %collective-permute-done.18.q2, ...), custom_call_target="tpu_custom_call" | custom-call | tf_op jit(solution)/shard_map/pallas_call | solution.py:429
  (52 shorter events, 17.9 us)
Async XLA Ops:
  0.6 27.6 %copy-start = (bf16[512,1024]{1,0:T(8,128)(2,1)S(1)}, bf16[512,1024]{1,0:T(8,128)(2,1)}, u32[]{:S(2)}) copy-start(bf16[512,1024]{1,0:T(8,128)(2,1)} %w0.7) | copy-start | bytes 3145732
  0.6 15.4 %collective-permute-start.1 = (bf16[512,1024]{1,0:T(8,128)(2,1)}, bf16[512,1024]{1,0:T(8,128)(2,1)}, u32[]{:S(2)}, u32[]{:S(2)}) collective-permute-start(bf16[512,1024]{1,0:T(8,128)(2,1)} %w0.7), channel_id=1, source_target_pairs={{0,128},{32,160},{64,224},{96,192},{128,32},{160,0},{192,64},{224,... | collective-permute-start | bytes 3145736 | tf_op jit(solution)/shard_map/ppermute | solution.py:29
  2.2 26.0 %collective-permute-start = (bf16[512,1024]{1,0:T(8,128)(2,1)}, bf16[512,1024]{1,0:T(8,128)(2,1)S(1)}, u32[]{:S(2)}, u32[]{:S(2)}) collective-permute-start(bf16[512,1024]{1,0:T(8,128)(2,1)} %w0.7), channel_id=1, source_target_pairs={{0,64},{64,0},{1,65},{65,1},{2,66},{66,2},{3,67},{67,3},{4,68},{68... | collective-permute-start | bytes 3145736 | tf_op jit(solution)/shard_map/ppermute | solution.py:29
  16.1 17.4 %collective-permute-start.2 = (bf16[512,1024]{1,0:T(8,128)(2,1)}, bf16[512,1024]{1,0:T(8,128)(2,1)S(1)}, u32[]{:S(2)}, u32[]{:S(2)}) collective-permute-start(bf16[512,1024]{1,0:T(8,128)(2,1)} %collective-permute-done.1.w2), channel_id=1, source_target_pairs={{0,64},{64,0},{1,65},{65,1},{2,66},{66,2},{3,67},{67,3},{4,68},{68... | collective-permute-start | bytes 3145736 | tf_op jit(solution)/shard_map/ppermute | solution.py:29
  17.7 11.9 %collective-permute-start.3 = (bf16[8,3072]{1,0:T(8,128)(2,1)}, bf16[8,3072]{1,0:T(8,128)(2,1)S(1)}, u32[]{:S(2)}, u32[]{:S(2)}) collective-permute-start(bf16[8,3072]{1,0:T(8,128)(2,1)} %get-tuple-element.42), channel_id=1, source_target_pairs={{0,1},{1,2},{2,3},{3,4},{4,5},{5,6},{6,7},{7,8},{8,9},{9,10},{10,1... | collective-permute-start | bytes 147464 | tf_op jit(solution)/shard_map/ppermute | solution.py:29
  20.9 8.6 %collective-permute-start.4 = (bf16[8,3072]{1,0:T(8,128)(2,1)}, bf16[8,3072]{1,0:T(8,128)(2,1)S(1)}, u32[]{:S(2)}, u32[]{:S(2)}) collective-permute-start(bf16[8,3072]{1,0:T(8,128)(2,1)} %get-tuple-element.43), channel_id=1, source_target_pairs={{1,0},{2,1},{3,2},{4,3},{5,4},{6,5},{7,6},{8,7},{9,8},{10,9},{11,1... | collective-permute-start | bytes 147464 | tf_op jit(solution)/shard_map/ppermute | solution.py:29
  22.3 1.0 copy-start.1
  23.4 0.9 copy-start.2
  24.3 0.8 copy-start.3
  42.3 2.2 %collective-permute-start.6 = (bf16[512,640]{1,0:T(8,128)(2,1)S(1)}, bf16[512,640]{1,0:T(8,128)(2,1)S(1)}, u32[]{:S(2)}, u32[]{:S(2)}) collective-permute-start(bf16[512,640]{1,0:T(8,128)(2,1)S(1)} %shard_map.111), channel_id=1, source_target_pairs={{0,64},{64,0},{1,65},{65,1},{2,66},{66,2},{3,67},{67,3},{4,68},{68... | collective-permute-start | bytes 1966088 | tf_op jit(solution)/shard_map/ppermute | solution.py:29
  42.9 12.4 %collective-permute-start.9 = (bf16[512,512]{1,0:T(8,128)(2,1)S(1)}, bf16[512,512]{1,0:T(8,128)(2,1)S(1)}, u32[]{:S(2)}, u32[]{:S(2)}) collective-permute-start(bf16[512,512]{1,0:T(8,128)(2,1)S(1)} %shard_map.116), channel_id=1, source_target_pairs={{0,64},{64,0},{1,65},{65,1},{2,66},{66,2},{3,67},{67,3},{4,68},{68... | collective-permute-start | bytes 1572872 | tf_op jit(solution)/shard_map/ppermute | solution.py:29
  44.8 25.0 %collective-permute-start.7 = (bf16[512,640]{1,0:T(8,128)(2,1)S(1)}, bf16[512,640]{1,0:T(8,128)(2,1)S(1)}, u32[]{:S(2)}, u32[]{:S(2)}) collective-permute-start(bf16[512,640]{1,0:T(8,128)(2,1)S(1)} %shard_map.112.refs_2_), channel_id=1, source_target_pairs={{0,128},{32,160},{64,224},{96,192},{128,32},{160,0},{192,64},{224,... | collective-permute-start | bytes 1966088 | tf_op jit(solution)/shard_map/ppermute | solution.py:29
  55.2 2.2 %collective-permute-start.8 = (bf16[512,512]{1,0:T(8,128)(2,1)S(1)}, bf16[512,512]{1,0:T(8,128)(2,1)S(1)}, u32[]{:S(2)}, u32[]{:S(2)}) collective-permute-start(bf16[512,512]{1,0:T(8,128)(2,1)S(1)} %shard_map.115), channel_id=1, source_target_pairs={{0,64},{64,0},{1,65},{65,1},{2,66},{66,2},{3,67},{67,3},{4,68},{68... | collective-permute-start | bytes 1572872 | tf_op jit(solution)/shard_map/ppermute | solution.py:29
  55.6 13.0 %collective-permute-start.10 = (bf16[512,512]{1,0:T(8,128)(2,1)S(1)}, bf16[512,512]{1,0:T(8,128)(2,1)S(1)}, u32[]{:S(2)}, u32[]{:S(2)}) collective-permute-start(bf16[512,512]{1,0:T(8,128)(2,1)S(1)} %shard_map.117), channel_id=1, source_target_pairs={{0,128},{32,160},{64,224},{96,192},{128,32},{160,0},{192,64},{224,... | collective-permute-start | bytes 1572872 | tf_op jit(solution)/shard_map/ppermute | solution.py:29
  56.8 12.9 %collective-permute-start.5 = (bf16[512,512]{1,0:T(8,128)(2,1)S(1)}, bf16[512,512]{1,0:T(8,128)(2,1)S(1)}, u32[]{:S(2)}, u32[]{:S(2)}) collective-permute-start(bf16[512,512]{1,0:T(8,128)(2,1)S(1)} %shard_map.108), channel_id=1, source_target_pairs={{0,64},{64,0},{1,65},{65,1},{2,66},{66,2},{3,67},{67,3},{4,68},{68... | collective-permute-start | bytes 1572872 | tf_op jit(solution)/shard_map/ppermute | solution.py:29
  69.6 7.7 %collective-permute-start.11 = (bf16[128,512]{1,0:T(8,128)(2,1)S(1)}, bf16[128,512]{1,0:T(8,128)(2,1)S(1)}, u32[]{:S(2)}, u32[]{:S(2)}) collective-permute-start(bf16[128,512]{1,0:T(8,128)(2,1)S(1)} %get-tuple-element.66), channel_id=1, source_target_pairs={{0,1},{1,2},{2,3},{3,0},{4,5},{5,6},{6,7},{7,4},{8,9},{9,10},{10,1... | collective-permute-start | bytes 393224 | tf_op jit(solution)/shard_map/ppermute | solution.py:29
  70.8 17.0 %collective-permute-start.14 = (bf16[128,640]{1,0:T(8,128)(2,1)S(1)}, bf16[128,640]{1,0:T(8,128)(2,1)S(1)}, u32[]{:S(2)}, u32[]{:S(2)}) collective-permute-start(bf16[128,640]{1,0:T(8,128)(2,1)S(1)} %get-tuple-element.69), channel_id=1, source_target_pairs={{0,1},{1,2},{2,3},{3,0},{4,5},{5,6},{6,7},{7,4},{8,9},{9,10},{10,1... | collective-permute-start | bytes 491528 | tf_op jit(solution)/shard_map/ppermute | solution.py:29
  70.9 16.9 %collective-permute-start.15 = (bf16[128,640]{1,0:T(8,128)(2,1)S(1)}, bf16[128,640]{1,0:T(8,128)(2,1)S(1)}, u32[]{:S(2)}, u32[]{:S(2)}) collective-permute-start(bf16[128,640]{1,0:T(8,128)(2,1)S(1)} %get-tuple-element.70), channel_id=1, source_target_pairs={{0,2},{1,3},{2,0},{3,1},{4,6},{5,7},{6,4},{7,5},{8,10},{9,11},{10,... | collective-permute-start | bytes 491528 | tf_op jit(solution)/shard_map/ppermute | solution.py:29
  75.6 12.2 %collective-permute-start.16 = (bf16[128,640]{1,0:T(8,128)(2,1)S(1)}, bf16[128,640]{1,0:T(8,128)(2,1)S(1)}, u32[]{:S(2)}, u32[]{:S(2)}) collective-permute-start(bf16[128,640]{1,0:T(8,128)(2,1)S(1)} %get-tuple-element.71), channel_id=1, source_target_pairs={{0,3},{1,0},{2,1},{3,2},{4,7},{5,4},{6,5},{7,6},{8,11},{9,8},{10,9... | collective-permute-start | bytes 491528 | tf_op jit(solution)/shard_map/ppermute | solution.py:29
  75.6 10.0 %collective-permute-start.12 = (bf16[128,512]{1,0:T(8,128)(2,1)S(1)}, bf16[128,512]{1,0:T(8,128)(2,1)S(1)}, u32[]{:S(2)}, u32[]{:S(2)}) collective-permute-start(bf16[128,512]{1,0:T(8,128)(2,1)S(1)} %get-tuple-element.67), channel_id=1, source_target_pairs={{0,2},{1,3},{2,0},{3,1},{4,6},{5,7},{6,4},{7,5},{8,10},{9,11},{10,... | collective-permute-start | bytes 393224 | tf_op jit(solution)/shard_map/ppermute | solution.py:29
  77.3 10.5 %collective-permute-start.13 = (bf16[128,512]{1,0:T(8,128)(2,1)S(1)}, bf16[128,512]{1,0:T(8,128)(2,1)S(1)}, u32[]{:S(2)}, u32[]{:S(2)}) collective-permute-start(bf16[128,512]{1,0:T(8,128)(2,1)S(1)} %get-tuple-element.68), channel_id=1, source_target_pairs={{0,3},{1,0},{2,1},{3,2},{4,7},{5,4},{6,5},{7,6},{8,11},{9,8},{10,9... | collective-permute-start | bytes 393224 | tf_op jit(solution)/shard_map/ppermute | solution.py:29
  122.9 14.7 %collective-permute-start.19 = (bf16[128,1152]{1,0:T(8,128)(2,1)S(1)}, bf16[128,1152]{1,0:T(8,128)(2,1)S(1)}, u32[]{:S(2)}, u32[]{:S(2)}) collective-permute-start(bf16[128,1152]{1,0:T(8,128)(2,1)S(1)} %bitcast.14), channel_id=1, source_target_pairs={{0,3},{1,0},{2,1},{3,2},{4,7},{5,4},{6,5},{7,6},{8,11},{9,8},{10,9... | collective-permute-start | bytes 884744 | tf_op jit(solution)/shard_map/ppermute | solution.py:29
  127.0 11.2 %collective-permute-start.18 = (bf16[128,1152]{1,0:T(8,128)(2,1)S(1)}, bf16[128,1152]{1,0:T(8,128)(2,1)S(1)}, u32[]{:S(2)}, u32[]{:S(2)}) collective-permute-start(bf16[128,1152]{1,0:T(8,128)(2,1)S(1)} %bitcast.15), channel_id=1, source_target_pairs={{0,2},{1,3},{2,0},{3,1},{4,6},{5,7},{6,4},{7,5},{8,10},{9,11},{10,... | collective-permute-start | bytes 884744 | tf_op jit(solution)/shard_map/ppermute | solution.py:29
  127.0 14.0 %collective-permute-start.17 = (bf16[128,1152]{1,0:T(8,128)(2,1)S(1)}, bf16[128,1152]{1,0:T(8,128)(2,1)S(1)}, u32[]{:S(2)}, u32[]{:S(2)}) collective-permute-start(bf16[128,1152]{1,0:T(8,128)(2,1)S(1)} %bitcast.16), channel_id=1, source_target_pairs={{0,1},{1,2},{2,3},{3,0},{4,5},{5,6},{6,7},{7,4},{8,9},{9,10},{10,1... | collective-permute-start | bytes 884744 | tf_op jit(solution)/shard_map/ppermute | solution.py:29
  (2 other events, 1.4 us)

commit v9 on v8

--- a/solution.py
+++ b/solution.py
@@ -105,26 +105,42 @@
 
 
 def centre_kernel(
-    place, codes, taps, window_far, table_far, up_far, stacks, columns, ups, taps_near, hot, window, table, up, done
+    place,
+    codes_far,
+    taps_far,
+    window_far,
+    table_far,
+    up_far,
+    stacks,
+    columns,
+    ups,
+    taps,
+    hot,
+    window,
+    table,
+    up,
+    codes,
+    done,
 ):
     loads = [
         pltpu.make_async_copy(far, near, done.at[at])
-        for at, (far, near) in enumerate(((window_far, window), (table_far, table), (up_far, up)))
+        for at, (far, near) in enumerate(
+            ((window_far, window), (table_far, table), (up_far, up), (codes_far, codes), (taps_far, taps))
+        )
     ]
     for load in loads:
         load.start()
-    taps_near[...] = taps[...]
     rows, features = window.shape
+    turn = turning(256)
+    width = features // 4
+    for load in loads:
+        load.wait()
     symbol = lax.broadcasted_iota(jnp.int32, (16, rows), 0)
     one_hot = jnp.where(symbol == codes[...], 1.0, 0.0).astype(jnp.bfloat16)
     for at in range(3):
         hot[:, at * rows : (at + 1) * rows] = one_hot
-    width = features // 4
-    turn = turning(256)
     by_row = jnp.broadcast_to(codes[...].astype(jnp.float32), (rows, rows)).T
     by_row = jnp.concatenate([by_row] * (width // rows), axis=1)
-    for load in loads:
-        load.wait()
     for r in range(4):
         cols = pl.ds(pl.multiple_of((place[0] ^ r) * width, width), width)
         looked = jnp.zeros((rows, width), jnp.float32)
@@ -425,7 +441,7 @@
     if scalar:
         specs[0] = pl.BlockSpec(memory_space=pltpu.SMEM)
     for at in unread:
-        specs[at] = pl.BlockSpec(memory_space=pltpu.HBM if kernel is centre_kernel else pl.ANY)
+        specs[at] = pl.BlockSpec(memory_space=pl.ANY)
     return pl.pallas_call(
         functools.partial(kernel, **fixed),
         out_shape=outs,
@@ -485,18 +501,18 @@
             array((16, 3 * rows)),
         ),
         place,
-        tokens,
-        kernel,
-        window,
-        embedding,
-        upstream,
+        *[
+            pltpu.with_memory_space_constraint(cells, pltpu.HBM)
+            for cells in (tokens, kernel, window, embedding, upstream)
+        ],
         scalar=True,
-        unread=(3, 4, 5),
+        unread=(1, 2, 3, 4, 5),
         scratch=(
             pltpu.VMEM((rows, features), jnp.bfloat16),
             pltpu.VMEM((symbols, features), jnp.float32),
             pltpu.VMEM((rows, units), jnp.bfloat16),
-            pltpu.SemaphoreType.DMA((3,)),
+            pltpu.VMEM(tokens.shape, jnp.int32),
+            pltpu.SemaphoreType.DMA((5,)),
         ),
     )
     partial = call(early_kernel, array((2 * rows, units), jnp.float32), centre, *weights[:2])

time: 144 us -> 141 us (0.979)
  local copies, waits for them, and re-layouts: 4.25 us -> 0.01 us
    unnamed x12 -> x2, local copies, waits for them, and re-layouts: 4.25 us -> 0.01 us
  transfers between devices with their start and end apart: 20 -> 20, of which waited for: 9 -> 10; matrix products, arithmetic and copies ran while one was open for 0% -> 0% of each run, Pallas kernels for 11% -> 12%
where the time goes in v9:
time: 141 us; the launch traced here: 140 us
  waiting for transfers between devices  44.5 us (32%)
  blocking collectives  34.5 us (24%)
  starting transfers between devices  32 us (23%)
  Pallas kernels  28.2 us (20%)
    ppermute x20, waiting for transfers between devices, shift(): return lax.ppermute(cells, axes if len(axes) > 1 else axes[0], pairs)  44.5 us
    all_to_all x2, blocking collectives, step(): lax.all_to_all(pieces, ('xh', 'z'), split_axis=0, concat_axis=0, tiled=True)  34.5 us
    ppermute x20, starting transfers between devices, shift(): return lax.ppermute(cells, axes if len(axes) > 1 else axes[0], pairs)  32 us
    pallas_call x20, Pallas kernels, call(): pl.pallas_call(functools.partial(kernel, **fixed), out_shape=outs, in_spe...  26.6 us
  transfers between devices with their start and end apart: 20, of which 10 were waited for; matrix products, arithmetic and copies ran while one was open for 0% of the time, Pallas kernels for 12%

profile of v9, /device:TPU:2, one launch (start us, length us, event | category | flops | bytes accessed | tf_op | source)
XLA Modules:
  0.0 140.1 jit_solution(10248387389854888446)
XLA Ops:
  0.6 1.6 %collective-permute-start.1 = (bf16[512,1024]{1,0:T(8,128)(2,1)}, bf16[512,1024]{1,0:T(8,128)(2,1)}, u32[]{:S(2)}, u32[]{:S(2)}) collective-permute-start(bf16[512,1024]{1,0:T(8,128)(2,1)} %w0.7), channel_id=1, source_target_pairs={{0,128},{32,160},{64,224},{96,192},{128,32},{160,0},{192,64},{224,... | collective-permute-start | bytes 3145736 | tf_op jit(solution)/shard_map/ppermute | solution.py:29
  2.2 13.8 %collective-permute-done.1.w2 = bf16[512,1024]{1,0:T(8,128)(2,1)} collective-permute-done((bf16[512,1024]{1,0:T(8,128)(2,1)}, bf16[512,1024]{1,0:T(8,128)(2,1)}, u32[]{:S(2)}, u32[]{:S(2)}) %collective-permute-start.1) | collective-permute-done | bytes 1048608 | tf_op jit(solution)/shard_map/ppermute | solution.py:29
  16.1 1.6 %shard_map.102 = (bf16[8,3072]{1,0:T(8,128)(2,1)}, bf16[8,3072]{1,0:T(8,128)(2,1)}) custom-call(s32[1,128]{1,0:T(1,128)} %codes.1, bf16[128,2048]{1,0:T(8,128)(2,1)} %bitcast.13, bf16[128,2048]{1,0:T(8,128)(2,1)} %bitcast.14, bf16[128,1024]{1,0:T(8,128)(2,1)} %bitcast.16, bf16[128,1024]{1,0:T(8,128)(2,1)} %bitcast.17, f32[5,2048]{1,0:T(8,128)} %table.1), custom_call_target="tpu_custom_call" | custom-call | tf_op jit(solution)/shard_map/pallas_call | solution.py:477
  17.7 3.2 %collective-permute-start.3 = (bf16[8,3072]{1,0:T(8,128)(2,1)}, bf16[8,3072]{1,0:T(8,128)(2,1)S(1)}, u32[]{:S(2)}, u32[]{:S(2)}) collective-permute-start(bf16[8,3072]{1,0:T(8,128)(2,1)} %get-tuple-element.42), channel_id=1, source_target_pairs={{0,1},{1,2},{2,3},{3,4},{4,5},{5,6},{6,7},{7,8},{8,9},{9,10},{10,1... | collective-permute-start | bytes 147464 | tf_op jit(solution)/shard_map/ppermute | solution.py:29
  22.3 2.7 %shard_map.101 = (bf16[4,256,512]{2,1,0:T(8,128)(2,1)S(1)}, bf16[4,512,256]{2,1,0:T(8,128)(2,1)S(1)}, f32[256,1024]{1,0:T(8,128)S(1)}, f32[7,1024]{1,0:T(8,128)S(1)}, bf16[16,384]{1,0:T(8,128)(2,1)S(1)}) custom-call(s32[2]{0:T(128)S(1)} %pad_add_fusion.place, s32[1,128]{1,0:T(1,128)} %codes.1, f32[7,1024]{1,0:T(8,128)} %taps_far.1, ...), custom_call_target="tpu_custom_call" | custom-call | tf_op jit(solution)/shard_map/pallas_call | solution.py:445
  27.1 1.7 %shard_map.103 = (bf16[4,32,512]{2,1,0:T(8,128)(2,1)S(1)}, f32[32,1024]{1,0:T(8,128)S(1)}, f32[32,1024]{1,0:T(8,128)S(1)}) custom-call(s32[2]{0:T(128)S(1)} %pad_add_fusion.place, bf16[8,3072]{1,0:T(8,128)(2,1)S(1)} %collective-permute-done.3.before, bf16[8,3072]{1,0:T(8,128)(2,1)S(1)} %collective-permute-done.4.after, bf16[512,1024]{1,0:T(8,128)(2,1)S(1)} %copy-done, ...), custom_call_target="tpu_custom_call" | custom-call | tf_op jit(solution)/shard_map/pallas_call | solution.py:445
  28.8 2.2 %shard_map.105.partial = f32[288,1024]{1,0:T(8,128)S(1)} custom-call(bf16[4,256,512]{2,1,0:T(8,128)(2,1)S(1)} %get-tuple-element.41.centre, bf16[4,32,512]{2,1,0:T(8,128)(2,1)S(1)} %get-tuple-element.44.halos, f32[256,1024]{1,0:T(8,128)S(1)} %shard_map.104.partial, f32[32,1024]{1,0:T(8,128)S(1)} %get-tuple-element.45.partial_halo, ...), custom_call_target="tpu_custom_call" | custom-call | tf_op jit(solution)/shard_map/pallas_call | solution.py:445
  32.4 1.3 shard_map.106
  33.8 2.8 %shard_map.109 = (bf16[256,512]{1,0:T(8,128)(2,1)S(1)}, f32[128,512]{1,0:T(8,128)S(1)}, f32[128,512]{1,0:T(8,128)S(1)}, f32[8,512]{1,0:T(8,128)S(1)}) custom-call(bf16[4,256,512]{2,1,0:T(8,128)(2,1)S(1)} %get-tuple-element.41.centre, bf16[4,32,512]{2,1,0:T(8,128)(2,1)S(1)} %get-tuple-element.44.halos, f32[288,1024]{1,0:T(8,128)S(1)} %shard_map.105.partial, ...), custom_call_target="tpu_custom_call" | custom-call | tf_op jit(solution)/shard_map/pallas_call | solution.py:445
  36.5 3.0 %shard_map.110.refs_2_ = bf16[512,128]{1,0:T(8,128)(2,1)S(1)} custom-call(s32[2]{0:T(128)S(1)} %pad_add_fusion.place, bf16[16,384]{1,0:T(8,128)(2,1)S(1)} %get-tuple-element.51.hot, bf16[512,1024]{1,0:T(8,128)(2,1)S(1)} %copy-done, bf16[512,1024]{1,0:T(8,128)(2,1)S(1)} %collective-permute-done.w1, bf16[512,1024]{1,0:T(8,128)(2,1)} %collective-permute-done.1.w2, ...), custom_call_target="tpu_custom_call" | custom-call | tf_op jit(solution)/shard_map/pallas_call | solution.py:445
  42.3 9.3 %collective-permute-start.7 = (bf16[512,640]{1,0:T(8,128)(2,1)S(1)}, bf16[512,640]{1,0:T(8,128)(2,1)S(1)}, u32[]{:S(2)}, u32[]{:S(2)}) collective-permute-start(bf16[512,640]{1,0:T(8,128)(2,1)S(1)} %shard_map.112.refs_2_), channel_id=1, source_target_pairs={{0,128},{32,160},{64,224},{96,192},{128,32},{160,0},{192,64},{224,... | collective-permute-start | bytes 1966088 | tf_op jit(solution)/shard_map/ppermute | solution.py:29
  54.1 11.2 %collective-permute-done.10.came = bf16[512,512]{1,0:T(8,128)(2,1)S(1)} collective-permute-done((bf16[512,512]{1,0:T(8,128)(2,1)S(1)}, bf16[512,512]{1,0:T(8,128)(2,1)S(1)}, u32[]{:S(2)}, u32[]{:S(2)}) %collective-permute-start.10) | collective-permute-done | bytes 524320 | tf_op jit(solution)/shard_map/ppermute | solution.py:29
  67.7 4.7 %collective-permute-start.15 = (bf16[128,640]{1,0:T(8,128)(2,1)S(1)}, bf16[128,640]{1,0:T(8,128)(2,1)S(1)}, u32[]{:S(2)}, u32[]{:S(2)}) collective-permute-start(bf16[128,640]{1,0:T(8,128)(2,1)S(1)} %get-tuple-element.70), channel_id=1, source_target_pairs={{0,2},{1,3},{2,0},{3,1},{4,6},{5,7},{6,4},{7,5},{8,10},{9,11},{10,... | collective-permute-start | bytes 491528 | tf_op jit(solution)/shard_map/ppermute | solution.py:29
  72.3 1.6 %collective-permute-start.12 = (bf16[128,512]{1,0:T(8,128)(2,1)S(1)}, bf16[128,512]{1,0:T(8,128)(2,1)S(1)}, u32[]{:S(2)}, u32[]{:S(2)}) collective-permute-start(bf16[128,512]{1,0:T(8,128)(2,1)S(1)} %get-tuple-element.67), channel_id=1, source_target_pairs={{0,2},{1,3},{2,0},{3,1},{4,6},{5,7},{6,4},{7,5},{8,10},{9,11},{10,... | collective-permute-start | bytes 393224 | tf_op jit(solution)/shard_map/ppermute | solution.py:29
  74.1 3.0 %collective-permute-start.13 = (bf16[128,512]{1,0:T(8,128)(2,1)S(1)}, bf16[128,512]{1,0:T(8,128)(2,1)S(1)}, u32[]{:S(2)}, u32[]{:S(2)}) collective-permute-start(bf16[128,512]{1,0:T(8,128)(2,1)S(1)} %get-tuple-element.68), channel_id=1, source_target_pairs={{0,3},{1,0},{2,1},{3,2},{4,7},{5,4},{6,5},{7,6},{8,11},{9,8},{10,9... | collective-permute-start | bytes 393224 | tf_op jit(solution)/shard_map/ppermute | solution.py:29
  77.0 5.3 %collective-permute-done.12.refs_2_ = bf16[128,512]{1,0:T(8,128)(2,1)S(1)} collective-permute-done((bf16[128,512]{1,0:T(8,128)(2,1)S(1)}, bf16[128,512]{1,0:T(8,128)(2,1)S(1)}, u32[]{:S(2)}, u32[]{:S(2)}) %collective-permute-start.12) | collective-permute-done | bytes 131104 | tf_op jit(solution)/shard_map/ppermute | solution.py:29
  82.4 2.2 %collective-permute-done.13.refs_3_ = bf16[128,512]{1,0:T(8,128)(2,1)S(1)} collective-permute-done((bf16[128,512]{1,0:T(8,128)(2,1)S(1)}, bf16[128,512]{1,0:T(8,128)(2,1)S(1)}, u32[]{:S(2)}, u32[]{:S(2)}) %collective-permute-start.13) | collective-permute-done | bytes 131104 | tf_op jit(solution)/shard_map/ppermute | solution.py:29
  85.0 18.5 %all_to_all.10.parts = bf16[16,8,1152]{2,1,0:T(8,128)(2,1)S(1)} all-to-all(bf16[16,8,1152]{2,1,0:T(8,128)(2,1)S(1)} %bitcast.12), channel_id=1, replica_groups=mesh['xl'=2,'c'=2,'xh'=2,'z'=8,'y'=4] {'xh','z'}, dimensions={0} | all-to-all | bytes 589824 | tf_op jit(solution)/shard_map/all_to_all | solution.py:640
  103.7 16.0 %all_to_all.11 = bf16[16,8,1152]{2,1,0:T(8,128)(2,1)S(1)} all-to-all(bf16[16,8,1152]{2,1,0:T(8,128)(2,1)S(1)} %shard_map.120), channel_id=1, replica_groups=mesh['xl'=2,'c'=2,'xh'=2,'z'=8,'y'=4] {'xh','z'}, dimensions={0} | all-to-all | bytes 589824 | tf_op jit(solution)/shard_map/all_to_all | solution.py:642
  119.7 4.1 %collective-permute-start.19 = (bf16[128,1152]{1,0:T(8,128)(2,1)S(1)}, bf16[128,1152]{1,0:T(8,128)(2,1)S(1)}, u32[]{:S(2)}, u32[]{:S(2)}) collective-permute-start(bf16[128,1152]{1,0:T(8,128)(2,1)S(1)} %bitcast.8), channel_id=1, source_target_pairs={{0,3},{1,0},{2,1},{3,2},{4,7},{5,4},{6,5},{7,6},{8,11},{9,8},{10,9... | collective-permute-start | bytes 884744 | tf_op jit(solution)/shard_map/ppermute | solution.py:29
  124.6 3.7 %shard_map.114 = (bf16[128,2048]{1,0:T(8,128)(2,1)}, bf16[128,1024]{1,0:T(8,128)(2,1)}) custom-call(s32[2]{0:T(128)S(1)} %pad_add_fusion.place, bf16[512,1024]{1,0:T(8,128)(2,1)S(1)} %copy-done, bf16[512,1024]{1,0:T(8,128)(2,1)S(1)} %collective-permute-done.w1, bf16[512,1024]{1,0:T(8,128)(2,1)} %collective-permute-done.1.w2, ...), custom_call_target="tpu_custom_call" | custom-call | tf_op jit(solution)/shard_map/pallas_call | solution.py:445
  128.3 6.0 %collective-permute-done.19.q3 = bf16[128,1152]{1,0:T(8,128)(2,1)S(1)} collective-permute-done((bf16[128,1152]{1,0:T(8,128)(2,1)S(1)}, bf16[128,1152]{1,0:T(8,128)(2,1)S(1)}, u32[]{:S(2)}, u32[]{:S(2)}) %collective-permute-start.19) | collective-permute-done | bytes 294944 | tf_op jit(solution)/shard_map/ppermute | solution.py:29
  134.9 3.0 %collective-permute-done.17.q1 = bf16[128,1152]{1,0:T(8,128)(2,1)S(1)} collective-permute-done((bf16[128,1152]{1,0:T(8,128)(2,1)S(1)}, bf16[128,1152]{1,0:T(8,128)(2,1)S(1)}, u32[]{:S(2)}, u32[]{:S(2)}) %collective-permute-start.17) | collective-permute-done | bytes 294944 | tf_op jit(solution)/shard_map/ppermute | solution.py:29
  138.0 2.1 %shard_map.121 = (f32[512,1024]{1,0:T(8,128)}, f32[7,1024]{1,0:T(8,128)}, f32[5,2048]{1,0:T(8,128)}) custom-call(s32[2]{0:T(128)S(1)} %pad_add_fusion.place, bf16[128,1152]{1,0:T(8,128)(2,1)S(1)} %bitcast.11, bf16[128,1152]{1,0:T(8,128)(2,1)S(1)} %collective-permute-done.17.q1, bf16[128,1152]{1,0:T(8,128)(2,1)S(1)} %collective-permute-done.18.q2, ...), custom_call_target="tpu_custom_call" | custom-call | tf_op jit(solution)/shard_map/pallas_call | solution.py:445
  (42 shorter events, 14.5 us)
Async XLA Ops:
  0.6 24.4 %copy-start = (bf16[512,1024]{1,0:T(8,128)(2,1)S(1)}, bf16[512,1024]{1,0:T(8,128)(2,1)}, u32[]{:S(2)}) copy-start(bf16[512,1024]{1,0:T(8,128)(2,1)} %w0.7) | copy-start | bytes 3145732
  0.6 15.4 %collective-permute-start.1 = (bf16[512,1024]{1,0:T(8,128)(2,1)}, bf16[512,1024]{1,0:T(8,128)(2,1)}, u32[]{:S(2)}, u32[]{:S(2)}) collective-permute-start(bf16[512,1024]{1,0:T(8,128)(2,1)} %w0.7), channel_id=1, source_target_pairs={{0,128},{32,160},{64,224},{96,192},{128,32},{160,0},{192,64},{224,... | collective-permute-start | bytes 3145736 | tf_op jit(solution)/shard_map/ppermute | solution.py:29
  2.2 22.8 %collective-permute-start = (bf16[512,1024]{1,0:T(8,128)(2,1)}, bf16[512,1024]{1,0:T(8,128)(2,1)S(1)}, u32[]{:S(2)}, u32[]{:S(2)}) collective-permute-start(bf16[512,1024]{1,0:T(8,128)(2,1)} %w0.7), channel_id=1, source_target_pairs={{0,64},{64,0},{1,65},{65,1},{2,66},{66,2},{3,67},{67,3},{4,68},{68... | collective-permute-start | bytes 3145736 | tf_op jit(solution)/shard_map/ppermute | solution.py:29
  16.1 15.0 %collective-permute-start.2 = (bf16[512,1024]{1,0:T(8,128)(2,1)}, bf16[512,1024]{1,0:T(8,128)(2,1)S(1)}, u32[]{:S(2)}, u32[]{:S(2)}) collective-permute-start(bf16[512,1024]{1,0:T(8,128)(2,1)} %collective-permute-done.1.w2), channel_id=1, source_target_pairs={{0,64},{64,0},{1,65},{65,1},{2,66},{66,2},{3,67},{67,3},{4,68},{68... | collective-permute-start | bytes 3145736 | tf_op jit(solution)/shard_map/ppermute | solution.py:29
  17.7 8.6 %collective-permute-start.3 = (bf16[8,3072]{1,0:T(8,128)(2,1)}, bf16[8,3072]{1,0:T(8,128)(2,1)S(1)}, u32[]{:S(2)}, u32[]{:S(2)}) collective-permute-start(bf16[8,3072]{1,0:T(8,128)(2,1)} %get-tuple-element.42), channel_id=1, source_target_pairs={{0,1},{1,2},{2,3},{3,4},{4,5},{5,6},{6,7},{7,8},{8,9},{9,10},{10,1... | collective-permute-start | bytes 147464 | tf_op jit(solution)/shard_map/ppermute | solution.py:29
  20.9 6.2 %collective-permute-start.4 = (bf16[8,3072]{1,0:T(8,128)(2,1)}, bf16[8,3072]{1,0:T(8,128)(2,1)S(1)}, u32[]{:S(2)}, u32[]{:S(2)}) collective-permute-start(bf16[8,3072]{1,0:T(8,128)(2,1)} %get-tuple-element.43), channel_id=1, source_target_pairs={{1,0},{2,1},{3,2},{4,3},{5,4},{6,5},{7,6},{8,7},{9,8},{10,9},{11,1... | collective-permute-start | bytes 147464 | tf_op jit(solution)/shard_map/ppermute | solution.py:29
  39.8 2.2 %collective-permute-start.6 = (bf16[512,640]{1,0:T(8,128)(2,1)S(1)}, bf16[512,640]{1,0:T(8,128)(2,1)S(1)}, u32[]{:S(2)}, u32[]{:S(2)}) collective-permute-start(bf16[512,640]{1,0:T(8,128)(2,1)S(1)} %shard_map.111), channel_id=1, source_target_pairs={{0,64},{64,0},{1,65},{65,1},{2,66},{66,2},{3,67},{67,3},{4,68},{68... | collective-permute-start | bytes 1966088 | tf_op jit(solution)/shard_map/ppermute | solution.py:29
  40.2 11.8 %collective-permute-start.9 = (bf16[512,512]{1,0:T(8,128)(2,1)S(1)}, bf16[512,512]{1,0:T(8,128)(2,1)S(1)}, u32[]{:S(2)}, u32[]{:S(2)}) collective-permute-start(bf16[512,512]{1,0:T(8,128)(2,1)S(1)} %shard_map.116), channel_id=1, source_target_pairs={{0,64},{64,0},{1,65},{65,1},{2,66},{66,2},{3,67},{67,3},{4,68},{68... | collective-permute-start | bytes 1572872 | tf_op jit(solution)/shard_map/ppermute | solution.py:29
  42.3 24.2 %collective-permute-start.7 = (bf16[512,640]{1,0:T(8,128)(2,1)S(1)}, bf16[512,640]{1,0:T(8,128)(2,1)S(1)}, u32[]{:S(2)}, u32[]{:S(2)}) collective-permute-start(bf16[512,640]{1,0:T(8,128)(2,1)S(1)} %shard_map.112.refs_2_), channel_id=1, source_target_pairs={{0,128},{32,160},{64,224},{96,192},{128,32},{160,0},{192,64},{224,... | collective-permute-start | bytes 1966088 | tf_op jit(solution)/shard_map/ppermute | solution.py:29
  51.9 2.2 %collective-permute-start.8 = (bf16[512,512]{1,0:T(8,128)(2,1)S(1)}, bf16[512,512]{1,0:T(8,128)(2,1)S(1)}, u32[]{:S(2)}, u32[]{:S(2)}) collective-permute-start(bf16[512,512]{1,0:T(8,128)(2,1)S(1)} %shard_map.115), channel_id=1, source_target_pairs={{0,64},{64,0},{1,65},{65,1},{2,66},{66,2},{3,67},{67,3},{4,68},{68... | collective-permute-start | bytes 1572872 | tf_op jit(solution)/shard_map/ppermute | solution.py:29
  52.3 13.0 %collective-permute-start.10 = (bf16[512,512]{1,0:T(8,128)(2,1)S(1)}, bf16[512,512]{1,0:T(8,128)(2,1)S(1)}, u32[]{:S(2)}, u32[]{:S(2)}) collective-permute-start(bf16[512,512]{1,0:T(8,128)(2,1)S(1)} %shard_map.117), channel_id=1, source_target_pairs={{0,128},{32,160},{64,224},{96,192},{128,32},{160,0},{192,64},{224,... | collective-permute-start | bytes 1572872 | tf_op jit(solution)/shard_map/ppermute | solution.py:29
  53.6 12.9 %collective-permute-start.5 = (bf16[512,512]{1,0:T(8,128)(2,1)S(1)}, bf16[512,512]{1,0:T(8,128)(2,1)S(1)}, u32[]{:S(2)}, u32[]{:S(2)}) collective-permute-start(bf16[512,512]{1,0:T(8,128)(2,1)S(1)} %shard_map.108), channel_id=1, source_target_pairs={{0,64},{64,0},{1,65},{65,1},{2,66},{66,2},{3,67},{67,3},{4,68},{68... | collective-permute-start | bytes 1572872 | tf_op jit(solution)/shard_map/ppermute | solution.py:29
  66.4 7.7 %collective-permute-start.11 = (bf16[128,512]{1,0:T(8,128)(2,1)S(1)}, bf16[128,512]{1,0:T(8,128)(2,1)S(1)}, u32[]{:S(2)}, u32[]{:S(2)}) collective-permute-start(bf16[128,512]{1,0:T(8,128)(2,1)S(1)} %get-tuple-element.66), channel_id=1, source_target_pairs={{0,1},{1,2},{2,3},{3,0},{4,5},{5,6},{6,7},{7,4},{8,9},{9,10},{10,1... | collective-permute-start | bytes 393224 | tf_op jit(solution)/shard_map/ppermute | solution.py:29
  67.6 17.0 %collective-permute-start.14 = (bf16[128,640]{1,0:T(8,128)(2,1)S(1)}, bf16[128,640]{1,0:T(8,128)(2,1)S(1)}, u32[]{:S(2)}, u32[]{:S(2)}) collective-permute-start(bf16[128,640]{1,0:T(8,128)(2,1)S(1)} %get-tuple-element.69), channel_id=1, source_target_pairs={{0,1},{1,2},{2,3},{3,0},{4,5},{5,6},{6,7},{7,4},{8,9},{9,10},{10,1... | collective-permute-start | bytes 491528 | tf_op jit(solution)/shard_map/ppermute | solution.py:29
  67.7 16.9 %collective-permute-start.15 = (bf16[128,640]{1,0:T(8,128)(2,1)S(1)}, bf16[128,640]{1,0:T(8,128)(2,1)S(1)}, u32[]{:S(2)}, u32[]{:S(2)}) collective-permute-start(bf16[128,640]{1,0:T(8,128)(2,1)S(1)} %get-tuple-element.70), channel_id=1, source_target_pairs={{0,2},{1,3},{2,0},{3,1},{4,6},{5,7},{6,4},{7,5},{8,10},{9,11},{10,... | collective-permute-start | bytes 491528 | tf_op jit(solution)/shard_map/ppermute | solution.py:29
  72.3 12.2 %collective-permute-start.16 = (bf16[128,640]{1,0:T(8,128)(2,1)S(1)}, bf16[128,640]{1,0:T(8,128)(2,1)S(1)}, u32[]{:S(2)}, u32[]{:S(2)}) collective-permute-start(bf16[128,640]{1,0:T(8,128)(2,1)S(1)} %get-tuple-element.71), channel_id=1, source_target_pairs={{0,3},{1,0},{2,1},{3,2},{4,7},{5,4},{6,5},{7,6},{8,11},{9,8},{10,9... | collective-permute-start | bytes 491528 | tf_op jit(solution)/shard_map/ppermute | solution.py:29
  72.3 10.0 %collective-permute-start.12 = (bf16[128,512]{1,0:T(8,128)(2,1)S(1)}, bf16[128,512]{1,0:T(8,128)(2,1)S(1)}, u32[]{:S(2)}, u32[]{:S(2)}) collective-permute-start(bf16[128,512]{1,0:T(8,128)(2,1)S(1)} %get-tuple-element.67), channel_id=1, source_target_pairs={{0,2},{1,3},{2,0},{3,1},{4,6},{5,7},{6,4},{7,5},{8,10},{9,11},{10,... | collective-permute-start | bytes 393224 | tf_op jit(solution)/shard_map/ppermute | solution.py:29
  74.1 10.5 %collective-permute-start.13 = (bf16[128,512]{1,0:T(8,128)(2,1)S(1)}, bf16[128,512]{1,0:T(8,128)(2,1)S(1)}, u32[]{:S(2)}, u32[]{:S(2)}) collective-permute-start(bf16[128,512]{1,0:T(8,128)(2,1)S(1)} %get-tuple-element.68), channel_id=1, source_target_pairs={{0,3},{1,0},{2,1},{3,2},{4,7},{5,4},{6,5},{7,6},{8,11},{9,8},{10,9... | collective-permute-start | bytes 393224 | tf_op jit(solution)/shard_map/ppermute | solution.py:29
  119.7 14.7 %collective-permute-start.19 = (bf16[128,1152]{1,0:T(8,128)(2,1)S(1)}, bf16[128,1152]{1,0:T(8,128)(2,1)S(1)}, u32[]{:S(2)}, u32[]{:S(2)}) collective-permute-start(bf16[128,1152]{1,0:T(8,128)(2,1)S(1)} %bitcast.8), channel_id=1, source_target_pairs={{0,3},{1,0},{2,1},{3,2},{4,7},{5,4},{6,5},{7,6},{8,11},{9,8},{10,9... | collective-permute-start | bytes 884744 | tf_op jit(solution)/shard_map/ppermute | solution.py:29
  123.8 11.2 %collective-permute-start.18 = (bf16[128,1152]{1,0:T(8,128)(2,1)S(1)}, bf16[128,1152]{1,0:T(8,128)(2,1)S(1)}, u32[]{:S(2)}, u32[]{:S(2)}) collective-permute-start(bf16[128,1152]{1,0:T(8,128)(2,1)S(1)} %bitcast.9), channel_id=1, source_target_pairs={{0,2},{1,3},{2,0},{3,1},{4,6},{5,7},{6,4},{7,5},{8,10},{9,11},{10,... | collective-permute-start | bytes 884744 | tf_op jit(solution)/shard_map/ppermute | solution.py:29
  124.3 13.7 %collective-permute-start.17 = (bf16[128,1152]{1,0:T(8,128)(2,1)S(1)}, bf16[128,1152]{1,0:T(8,128)(2,1)S(1)}, u32[]{:S(2)}, u32[]{:S(2)}) collective-permute-start(bf16[128,1152]{1,0:T(8,128)(2,1)S(1)} %bitcast.10), channel_id=1, source_target_pairs={{0,1},{1,2},{2,3},{3,0},{4,5},{5,6},{6,7},{7,4},{8,9},{9,10},{10,1... | collective-permute-start | bytes 884744 | tf_op jit(solution)/shard_map/ppermute | solution.py:29
